TPU v7x, 32 devices: a whole 2x2x4 slice. The times are simulated.
32 devices in a mesh: row: 4 (over y, x), col: 4 (over z), sea: 2 (over core).
Axes of the slice: x: 2, y: 2, z: 4, core: 2. Of those that a mesh axis runs over, the one named last changes fastest.
Arguments:
- kernel: bfloat16 [16, 4, 192, 768], P(None, None, 'col', 'row'), may hold values from -0.0546875 to 0.0546875
- history: bfloat16 [15, 4, 192, 512], P(None, None, 'col', 'sea'), may hold values from -6 to 6
- displacement: float32 [768, 512], P(('row', 'col'), 'sea'), may hold values from -6 to 6
- velocity: float32 [768, 512], P(('row', 'col'), 'sea'), may hold values from -6 to 6
- acceleration: float32 [768, 512], P(('row', 'col'), 'sea'), may hold values from -6 to 6
- excitation: float32 [3, 768, 512], P(None, ('row', 'col'), 'sea'), may hold values from -6 to 6
- solve_inverse: float32 [128, 6, 6], P(('row', 'col')), may hold values from -2.5 to 2.5
- stiffness: float32 [128, 6, 6], P(('row', 'col')), may hold values from -2.5 to 2.5
- owned: int32 [128], replicated, may hold values from 0 to 127, as said below
- links: int32 [128, 16], P(('row', 'col')), may hold values from 0 to 2047, as said below
- arms: float32 [128, 3, 16], P(('row', 'col')), may hold values from -1 to 1
Outputs:
- final_velocity: float32 [768, 512], P(('row', 'col'), 'sea')
- deck_gaps: float32 [128, 16, 3, 512], P(('row', 'col'), None, None, 'sea')
Inputs may be any that keep to these rules, and one draw needn't show every extreme that they name: `owned`: A permutation of the 128 modules. Module m has its modes on the grid device m // 8 (row-major over row, col); its owner has the same col. The modules that one device sends to one owner number at most 4, exactly 4 wherever any are sent, and their list positions differ modulo 4. `links`: the partner point lies on another module listed to the same owner.
All inputs are finite; a program needn't handle non-finite values.
Results may differ from a plain program's by a relative error of at most 0.00037.
Values may be sent and summed in bfloat16 or wider, within the bound.
No kernel may reach another device: no remote copies, remote signals or barrier semaphores. Data moves between devices by JAX's collectives and lax.ppermute only.
A program may use at most 128 MiB of HBM per device.

v0:
```python
import functools

import jax
import jax.numpy as jnp
from jax import lax
from jax.experimental import pallas as pl
from jax.experimental.pallas import tpu as pltpu
from jax.sharding import PartitionSpec as P


DT = 0.5
QUARTER = DT * DT / 4.0
F32 = jnp.float32
BF16 = jnp.bfloat16
HIGHEST = lax.Precision.HIGHEST
VMEM = pl.BlockSpec(memory_space=pltpu.VMEM)
SMEM = pl.BlockSpec(memory_space=pltpu.SMEM)


def sends_to(i, d, n):
    return i ^ d if n & (n - 1) == 0 else (i + d) % n


def comes_from(i, d, n):
    return i ^ d if n & (n - 1) == 0 else (i + n - d) % n


def exchange(pieces, axis):
    n = lax.axis_size(axis)
    out = [pieces[0]] + [None] * (n - 1)
    for d in range(n - 1, 0, -1):
        out[d] = lax.ppermute(pieces[d], axis, [(i, sends_to(i, d, n)) for i in range(n)])
    return out


def dot_rows(a, b):
    return lax.dot_general(a, b, (((0,), (0,)), ((), ())), preferred_element_type=F32)


def dot_exact(a, b):
    return jnp.dot(a, b, precision=HIGHEST, preferred_element_type=F32)


def padded_bytes(shape, dtype):
    size = jnp.dtype(dtype).itemsize
    dims = (1, 1, *shape)
    up = lambda n, m: -(-n // m) * m
    major = 1
    for n in dims[:-2]:
        major *= n
    return major * up(dims[-2], 32 // size) * up(dims[-1], 128) * size


def call(body, shapes, in_specs, args, flops, nbytes, scratch=()):
    arrays = list(args) + jax.tree.leaves(shapes)
    held = sum(padded_bytes(t.shape, t.dtype) for t in arrays)
    held += sum(padded_bytes(t.shape, t.dtype) for t in scratch if t.shape[1:])
    return pl.pallas_call(
        body,
        out_shape=shapes,
        in_specs=in_specs,
        out_specs=jax.tree.map(lambda _: VMEM, shapes),
        scratch_shapes=scratch,
        compiler_params=pltpu.CompilerParams(vmem_limit_bytes=min(2 * held + (2 << 20), 60 << 20)),
        cost_estimate=pl.CostEstimate(flops=flops, bytes_accessed=nbytes, transcendentals=0),
    )(*args)


def known_kernel(lag_rows, steps, per, k_hbm, h_hbm, lags_ref, *refs):
    outs, (k_ref, h_ref, k_sem, h_sem) = refs[:steps], refs[steps:]
    total, known = k_ref.shape[0], h_ref.shape[0]
    size = per * lag_rows
    count = -(-total // size)
    copies = []
    for i in range(count):
        k_rows = pl.ds(i * size, min(size, total - i * size))
        h_rows = pl.ds(i * size, min(size, known - i * size))
        pair = (
            pltpu.make_async_copy(k_hbm.at[k_rows], k_ref.at[k_rows], k_sem.at[i]),
            pltpu.make_async_copy(h_hbm.at[h_rows], h_ref.at[h_rows], h_sem.at[i]),
        )
        pair[0].start()
        pair[1].start()
        copies.append(pair)
    for i in range(count):
        copies[i][0].wait()
        copies[i][1].wait()
        for s in range(steps):
            first = max(i * size, (s + 1) * lag_rows)
            last = min((i + 1) * size, total)
            if first >= last:
                continue
            shift = (s + 1) * lag_rows
            term = dot_rows(k_ref[first:last, :], h_ref[first - shift : last - shift, :])
            outs[s][...] = term if i == 0 else outs[s][...] + term
    lags_ref[...] = k_ref[: steps * lag_rows, :]


def known_forces(kernel_flat, history_flat, lag_rows, steps):
    block = kernel_flat.shape[1]
    shape = jax.ShapeDtypeStruct((block, history_flat.shape[1]), F32)
    per = steps + 1
    count = -(-kernel_flat.shape[0] // (per * lag_rows))
    out = call(
        functools.partial(known_kernel, lag_rows, steps, per),
        (jax.ShapeDtypeStruct((steps * lag_rows, block), BF16),) + (shape,) * steps,
        [pl.BlockSpec(memory_space=pltpu.MemorySpace.HBM)] * 2,
        (kernel_flat, history_flat),
        2 * steps * kernel_flat.size * history_flat.shape[1],
        2 * (kernel_flat.size + history_flat.size),
        [
            pltpu.VMEM(kernel_flat.shape, BF16),
            pltpu.VMEM(history_flat.shape, BF16),
            pltpu.SemaphoreType.DMA((count,)),
            pltpu.SemaphoreType.DMA((count,)),
        ],
    )
    return out[0], out[1:]


def force_kernel(rows, cols, ahead, *refs):
    k_ref = refs[0]
    arrived = refs[1 : 1 + rows]
    bases = refs[1 + rows : 1 + rows + ahead]
    outs = refs[1 + rows + ahead : -2]
    chunks, later = outs[:cols], outs[cols:]
    whole, total = refs[-2:]
    slab = arrived[0].shape[0]
    row, col = lax.axis_index("row"), lax.axis_index("col")
    for d in range(rows):
        start = pl.multiple_of(comes_from(row, d, rows) * slab, 16)
        whole[pl.ds(start, slab), :] = arrived[d][...]
    lag_rows = rows * slab
    total[...] = bases[0][...] + dot_rows(k_ref[:lag_rows, :], whole[...])
    for d in range(cols):
        start = pl.multiple_of(sends_to(col, d, cols) * slab, 8)
        chunks[d][...] = total[pl.ds(start, slab), :]
    for n in range(1, ahead):
        later[n - 1][...] = bases[n][...] + dot_rows(
            k_ref[n * lag_rows : (n + 1) * lag_rows, :], whole[...]
        )


def force_pieces(kernel_lags, arrived, bases, cols):
    rows, ahead = len(arrived), len(bases)
    slab, reals = arrived[0].shape
    block = kernel_lags.shape[1]
    shapes = (jax.ShapeDtypeStruct((slab, reals), F32),) * cols + (
        jax.ShapeDtypeStruct((block, reals), F32),
    ) * (ahead - 1)
    out = call(
        functools.partial(force_kernel, rows, cols, ahead),
        shapes,
        [VMEM] * (1 + rows + ahead),
        (kernel_lags, *arrived, *bases),
        2 * ahead * rows * slab * block * reals,
        4 * 2 * ahead * block * reals,
        [pltpu.VMEM((rows * slab, reals), BF16), pltpu.VMEM((block, reals), F32)],
    )
    return out[:cols], out[cols:]


def prepare_kernel(x, v, a, e, stiff, predicted, load):
    p = x[...] + DT * v[...] + QUARTER * a[...]
    predicted[...] = p
    load[...] = e[...] - dot_exact(stiff[...], p)


def prepare(x, v, a, e, stiff):
    shape = jax.ShapeDtypeStruct(x.shape, F32)
    return call(
        prepare_kernel, (shape, shape), [VMEM] * 5, (x, v, a, e, stiff),
        12 * x.size * x.shape[0], 24 * x.size,
    )


def advance_kernel(cols, *refs):
    parts = refs[:cols]
    predicted, v, a, load, inverse = refs[cols : cols + 5]
    x_out, v_out, a_out, v_half = refs[cols + 5 :]
    force = parts[0][...]
    for part in parts[1:]:
        force = force + part[...]
    a_next = dot_exact(inverse[...], load[...] - force)
    v_next = v[...] + 0.5 * DT * (a[...] + a_next)
    v_half[...] = v_next.astype(BF16)
    v_out[...] = v_next
    a_out[...] = a_next
    x_out[...] = predicted[...] + QUARTER * a_next


def advance(parts, predicted, v, a, load, inverse):
    shape = jax.ShapeDtypeStruct(v.shape, F32)
    return call(
        functools.partial(advance_kernel, len(parts)),
        (shape, shape, shape, jax.ShapeDtypeStruct(v.shape, BF16)),
        [VMEM] * (len(parts) + 5),
        (*parts, predicted, v, a, load, inverse),
        12 * v.size * v.shape[0], 40 * v.size,
    )


def finish_kernel(cols, rows, *refs):
    parts = refs[:cols]
    predicted, v, a, load, inverse, route = refs[cols : cols + 6]
    v_out, *sends = refs[cols + 6 :]
    force = parts[0][...]
    for part in parts[1:]:
        force = force + part[...]
    a_next = dot_exact(inverse[...], load[...] - force)
    v_out[...] = v[...] + 0.5 * DT * (a[...] + a_next)
    x_next = predicted[...] + QUARTER * a_next
    moved = dot_exact(route[...], x_next)
    size = route.shape[0] // rows
    for d in range(rows):
        sends[d][...] = moved[d * size : (d + 1) * size, :]


def finish(parts, predicted, v, a, load, inverse, route, rows):
    shapes = (jax.ShapeDtypeStruct(v.shape, F32),) + (
        jax.ShapeDtypeStruct((route.shape[0] // rows, v.shape[1]), F32),
    ) * rows
    out = call(
        functools.partial(finish_kernel, len(parts), rows),
        shapes,
        [VMEM] * (len(parts) + 6),
        (*parts, predicted, v, a, load, inverse, route),
        12 * v.size * v.shape[0], 40 * v.size,
    )
    return out[0], out[1:]


def gaps_kernel(rows, *refs):
    weights, arrived, out, held = refs[0], refs[1 : 1 + rows], refs[-2], refs[-1]
    size = arrived[0].shape[0]
    for d in range(rows):
        held[d * size : (d + 1) * size, :] = arrived[d][...]
    out[...] = dot_exact(weights[...], held[...])


def gaps(weights, arrived):
    points, reals = weights.shape[0], arrived[0].shape[1]
    return call(
        functools.partial(gaps_kernel, len(arrived)),
        jax.ShapeDtypeStruct((points, reals), F32),
        [VMEM] * (1 + len(arrived)),
        (weights, *arrived),
        12 * weights.size * reals, 4 * points * reals,
        [pltpu.VMEM((weights.shape[1], reals), F32)],
    )


def diagonals_kernel(*refs):
    half = len(refs) // 2
    for blocks, out in zip(refs[:half], refs[half:]):
        modules = blocks.shape[1]
        width = 6 * modules
        lane = lax.broadcasted_iota(jnp.int32, (modules, width), 1) // 6
        module = lax.broadcasted_iota(jnp.int32, (modules, width), 0)
        for i in range(6):
            spread = jnp.concatenate([blocks[i]] * modules, axis=1)
            out[pl.ds(i, modules, stride=6), :] = jnp.where(lane == module, spread, 0.0)


def diagonals(*matrices):
    width = 6 * matrices[0].shape[0]
    shape = jax.ShapeDtypeStruct((width, width), F32)
    return call(
        diagonals_kernel, (shape,) * len(matrices), [VMEM] * len(matrices),
        tuple(m.transpose(1, 0, 2) for m in matrices), 100 * width * width, 16 * width * width,
    )


def plan_kernel(rows, cols, capacity, slot_rows, owned, links, arms, send, weights, table):
    modules = send.shape[1] // 6
    points = links.shape[0] // modules
    row, col = lax.axis_index("row"), lax.axis_index("col")
    grid_index = row * cols + col
    first_module = grid_index * modules
    shape = (slot_rows, modules * 6)
    i = lax.broadcasted_iota(jnp.int32, shape, 0)
    j = lax.broadcasted_iota(jnp.int32, shape, 1)
    for d in range(rows):
        listed = (sends_to(row, d, rows) * cols + col) * modules
        wanted = jnp.full(shape, -1, jnp.int32)
        for k in range(modules):
            local = owned[listed + k] - first_module
            here = (local >= 0) & (local < modules)
            wanted = jnp.where((i // 6 == k % capacity) & here, local, wanted)
        hit = (wanted == j // 6) & (i % 6 == j % 6)
        send[d * slot_rows : (d + 1) * slot_rows, :] = jnp.where(hit, 1.0, 0.0)
    count = modules * points
    table[:, 0:3] = arms[...]
    for q in range(modules):
        home = owned[first_module + q] // (cols * modules)
        home_d = home ^ row if rows & (rows - 1) == 0 else (row + rows - home) % rows
        place = home_d * slot_rows + (q % capacity) * 6
        table[q * points : (q + 1) * points, 3:4] = jnp.full((points, 1), place, jnp.int32).astype(F32)
    own = table[...]
    point = lax.broadcasted_iota(jnp.int32, (count, count), 1)
    meets = jnp.where(links[...] - first_module * points == point, 1.0, 0.0)
    partner = dot_exact(meets, own)
    wide = (count, rows * slot_rows)
    column = lax.broadcasted_iota(jnp.int32, wide, 1)
    total = [None] * 3
    for sign, side in ((1.0, own), (-1.0, partner)):
        mode = column - (side[:, 3:4] + 0.5).astype(jnp.int32)
        e = [jnp.broadcast_to(sign * side[:, c : c + 1], wide) for c in range(3)]
        for c in range(3):
            up, down = (c + 1) % 3, (c + 2) % 3
            value = jnp.where(mode == c, sign, 0.0)
            value = jnp.where(mode == 3 + up, e[down], value)
            value = jnp.where(mode == 3 + down, -e[up], value)
            total[c] = value if total[c] is None else total[c] + value
    for q in range(modules):
        for c in range(3):
            start = (q * 3 + c) * points
            weights[start : start + points, :] = total[c][q * points : (q + 1) * points, :]


def plan(owned, links, arms, rows, cols):
    modules, points = links.shape
    capacity = 2 * modules // rows
    slot_rows = -(-capacity * 6 // 8) * 8
    return call(
        functools.partial(plan_kernel, rows, cols, capacity, slot_rows),
        (
            jax.ShapeDtypeStruct((rows * slot_rows, modules * 6), F32),
            jax.ShapeDtypeStruct((modules * 3 * points, rows * slot_rows), F32),
        ),
        [SMEM, VMEM, VMEM],
        (owned, links.reshape(-1, 1), arms.transpose(0, 2, 1).reshape(-1, 3)),
        12 * (modules * points) ** 2 * 4, 4 * modules * 3 * points * rows * slot_rows,
        [pltpu.VMEM((modules * points, 4), F32)],
    )


def after(value, *others):
    return lax.optimization_barrier((value, *others))[0]


def body(
    kernel,
    history,
    displacement,
    velocity,
    acceleration,
    excitation,
    solve_inverse,
    stiffness,
    owned,
    links,
    arms,
):
    rows, cols = lax.axis_size("row"), lax.axis_size("col")
    steps = excitation.shape[0]
    slab, reals = velocity.shape
    modules, points = links.shape
    x, v, a = displacement, velocity, acceleration
    arrived = exchange([v.astype(BF16)] * rows, "row")
    lags, bases = known_forces(
        kernel.reshape(-1, kernel.shape[3]), history.reshape(-1, reals), rows * slab, steps
    )
    inverse, stiff = diagonals(solve_inverse, stiffness)
    for n in range(steps):
        predicted, load = prepare(x, v, a, excitation[n], stiff)
        pieces, bases = force_pieces(lags, arrived, bases, cols)
        if n == 0:
            send, weights = plan(after(owned, pieces[0]), links, arms, rows, cols)
        parts = exchange(pieces, "col")
        if n < steps - 1:
            x, v, a, v_half = advance(parts, predicted, v, a, load, inverse)
            arrived = exchange([v_half] * rows, "row")
        else:
            v, sends = finish(parts, predicted, v, a, load, inverse, send, rows)
    moved = exchange(sends, "row")
    out = gaps(weights, moved).reshape(modules, 3, points, reals)
    return v, out.transpose(0, 2, 1, 3)


def solution(mesh):
    placed = (
        P(None, None, "col", "row"),
        P(None, None, "col", "sea"),
        P(("row", "col"), "sea"),
        P(("row", "col"), "sea"),
        P(("row", "col"), "sea"),
        P(None, ("row", "col"), "sea"),
        P(("row", "col"), None, None),
        P(("row", "col"), None, None),
        P(),
        P(("row", "col"), None),
        P(("row", "col"), None, None),
    )
    return jax.shard_map(
        body,
        mesh=mesh,
        in_specs=placed,
        out_specs=(P(("row", "col"), "sea"), P(("row", "col"), None, None, "sea")),
        check_vma=False,
    )
```

profile of v0, /device:TPU:0, one launch (start us, length us, event | category | flops | bytes accessed | tf_op | source)
XLA Modules:
  0.0 61.8 jit_solution(715165958980047938)
XLA Ops:
  1.4 3.0 %collective-permute-start = (bf16[48,256]{1,0:T(8,128)(2,1)S(1)}, bf16[48,256]{1,0:T(8,128)(2,1)S(1)}, u32[]{:S(2)}, u32[]{:S(2)}) collective-permute-start(bf16[48,256]{1,0:T(8,128)(2,1)S(1)} %convert_element_type.3.refs_1_), channel_id=1, source_target_pairs={{0,8},{8,0},{16,24},{24,16},{1,9},{9,1},{17,25},{25,17},{2,10},{10... | collective-permute-start | bytes 73736 | tf_op jit(solution)/shard_map/ppermute | solution.py:32
  4.4 1.5 %collective-permute-start.1 = (bf16[48,256]{1,0:T(8,128)(2,1)S(1)}, bf16[48,256]{1,0:T(8,128)(2,1)S(1)}, u32[]{:S(2)}, u32[]{:S(2)}) collective-permute-start(bf16[48,256]{1,0:T(8,128)(2,1)S(1)} %convert_element_type.3.refs_1_), channel_id=1, source_target_pairs={{0,16},{8,24},{16,0},{24,8},{1,17},{9,25},{17,1},{25,9},{2,18},{10... | collective-permute-start | bytes 73736 | tf_op jit(solution)/shard_map/ppermute | solution.py:32
  5.9 1.4 %copy-done.6 = bf16[16,4,48,192]{3,2,1,0:T(8,128)(2,1)S(1)} copy-done((bf16[16,4,48,192]{3,2,1,0:T(8,128)(2,1)S(1)}, bf16[16,4,48,192]{3,2,1,0:T(8,128)(2,1)}, u32[]{:S(2)}) %copy-start.6) | copy-done | bytes 1179672
  7.3 1.4 %copy-done.7 = bf16[15,4,48,256]{3,2,1,0:T(8,128)(2,1)S(1)} copy-done((bf16[15,4,48,256]{3,2,1,0:T(8,128)(2,1)S(1)}, bf16[15,4,48,256]{3,2,1,0:T(8,128)(2,1)}, u32[]{:S(2)}) %copy-start.7) | copy-done | bytes 1474584
  8.7 3.2 %shard_map.122 = (bf16[576,192]{1,0:T(8,128)(2,1)S(1)}, f32[192,256]{1,0:T(8,128)S(1)}, f32[192,256]{1,0:T(8,128)S(1)}, f32[192,256]{1,0:T(8,128)S(1)}) custom-call(bf16[3072,192]{1,0:T(8,128)(2,1)S(1)} %bitcast.18, bf16[2880,256]{1,0:T(8,128)(2,1)S(1)} %bitcast.19), custom_call_target="tpu_custom_call" | custom-call | flops 905969664 | bytes 2654208 | tf_op jit(solution)/shard_map/pallas_call | solution.py:58
  12.3 2.1 %collective-permute-start.3 = (f32[48,256]{1,0:T(8,128)S(1)}, f32[48,256]{1,0:T(8,128)S(1)}, u32[]{:S(2)}, u32[]{:S(2)}) collective-permute-start(f32[48,256]{1,0:T(8,128)S(1)} %get-tuple-element.50), channel_id=1, source_target_pairs={{0,2},{2,0},{4,6},{6,4},{1,3},{3,1},{5,7},{7,5},{8,10},{10,8},{12,... | collective-permute-start | bytes 147464 | tf_op jit(solution)/shard_map/ppermute | solution.py:32
  14.4 2.6 %collective-permute-start.4 = (f32[48,256]{1,0:T(8,128)S(1)}, f32[48,256]{1,0:T(8,128)S(1)}, u32[]{:S(2)}, u32[]{:S(2)}) collective-permute-start(f32[48,256]{1,0:T(8,128)S(1)} %get-tuple-element.51), channel_id=1, source_target_pairs={{0,4},{2,6},{4,0},{6,2},{1,5},{3,7},{5,1},{7,3},{8,12},{10,14},{12... | collective-permute-start | bytes 147464 | tf_op jit(solution)/shard_map/ppermute | solution.py:32
  17.4 3.0 %collective-permute-done.4.refs_2_ = f32[48,256]{1,0:T(8,128)S(1)} collective-permute-done((f32[48,256]{1,0:T(8,128)S(1)}, f32[48,256]{1,0:T(8,128)S(1)}, u32[]{:S(2)}, u32[]{:S(2)}) %collective-permute-start.4) | collective-permute-done | bytes 49184 | tf_op jit(solution)/shard_map/ppermute | solution.py:32
  20.5 2.4 %collective-permute-done.5.refs_3_ = f32[48,256]{1,0:T(8,128)S(1)} collective-permute-done((f32[48,256]{1,0:T(8,128)S(1)}, f32[48,256]{1,0:T(8,128)S(1)}, u32[]{:S(2)}, u32[]{:S(2)}) %collective-permute-start.5) | collective-permute-done | bytes 49184 | tf_op jit(solution)/shard_map/ppermute | solution.py:32
  23.1 1.6 %collective-permute-start.6 = (bf16[48,256]{1,0:T(8,128)(2,1)S(1)}, bf16[48,256]{1,0:T(8,128)(2,1)S(1)}, u32[]{:S(2)}, u32[]{:S(2)}) collective-permute-start(bf16[48,256]{1,0:T(8,128)(2,1)S(1)} %get-tuple-element.57.refs_1_), channel_id=1, source_target_pairs={{0,8},{8,0},{16,24},{24,16},{1,9},{9,1},{17,25},{25,17},{2,10},{10... | collective-permute-start | bytes 73736 | tf_op jit(solution)/shard_map/ppermute | solution.py:32
  24.7 1.5 %collective-permute-start.7 = (bf16[48,256]{1,0:T(8,128)(2,1)S(1)}, bf16[48,256]{1,0:T(8,128)(2,1)S(1)}, u32[]{:S(2)}, u32[]{:S(2)}) collective-permute-start(bf16[48,256]{1,0:T(8,128)(2,1)S(1)} %get-tuple-element.57.refs_1_), channel_id=1, source_target_pairs={{0,16},{8,24},{16,0},{24,8},{1,17},{9,25},{17,1},{25,9},{2,18},{10... | collective-permute-start | bytes 73736 | tf_op jit(solution)/shard_map/ppermute | solution.py:32
  27.0 1.5 %collective-permute-done.7.refs_3_ = bf16[48,256]{1,0:T(8,128)(2,1)S(1)} collective-permute-done((bf16[48,256]{1,0:T(8,128)(2,1)S(1)}, bf16[48,256]{1,0:T(8,128)(2,1)S(1)}, u32[]{:S(2)}, u32[]{:S(2)}) %collective-permute-start.7) | collective-permute-done | bytes 24608 | tf_op jit(solution)/shard_map/ppermute | solution.py:32
  28.5 2.4 %collective-permute-done.8.refs_4_ = bf16[48,256]{1,0:T(8,128)(2,1)S(1)} collective-permute-done((bf16[48,256]{1,0:T(8,128)(2,1)S(1)}, bf16[48,256]{1,0:T(8,128)(2,1)S(1)}, u32[]{:S(2)}, u32[]{:S(2)}) %collective-permute-start.8) | collective-permute-done | bytes 24608 | tf_op jit(solution)/shard_map/ppermute | solution.py:32
  32.2 2.5 %collective-permute-start.9 = (f32[48,256]{1,0:T(8,128)S(1)}, f32[48,256]{1,0:T(8,128)S(1)}, u32[]{:S(2)}, u32[]{:S(2)}) collective-permute-start(f32[48,256]{1,0:T(8,128)S(1)} %get-tuple-element.61), channel_id=1, source_target_pairs={{0,2},{2,0},{4,6},{6,4},{1,3},{3,1},{5,7},{7,5},{8,10},{10,8},{12,... | collective-permute-start | bytes 147464 | tf_op jit(solution)/shard_map/ppermute | solution.py:32
  34.9 1.3 %collective-permute-done.10.refs_2_ = f32[48,256]{1,0:T(8,128)S(1)} collective-permute-done((f32[48,256]{1,0:T(8,128)S(1)}, f32[48,256]{1,0:T(8,128)S(1)}, u32[]{:S(2)}, u32[]{:S(2)}) %collective-permute-start.10) | collective-permute-done | bytes 49184 | tf_op jit(solution)/shard_map/ppermute | solution.py:32
  38.6 2.4 %collective-permute-start.14 = (bf16[48,256]{1,0:T(8,128)(2,1)S(1)}, bf16[48,256]{1,0:T(8,128)(2,1)S(1)}, u32[]{:S(2)}, u32[]{:S(2)}) collective-permute-start(bf16[48,256]{1,0:T(8,128)(2,1)S(1)} %get-tuple-element.69.refs_1_), channel_id=1, source_target_pairs={{0,24},{8,16},{16,8},{24,0},{1,25},{9,17},{17,9},{25,1},{2,26},{10... | collective-permute-start | bytes 73736 | tf_op jit(solution)/shard_map/ppermute | solution.py:32
  41.9 1.4 %collective-permute-done.14.refs_4_ = bf16[48,256]{1,0:T(8,128)(2,1)S(1)} collective-permute-done((bf16[48,256]{1,0:T(8,128)(2,1)S(1)}, bf16[48,256]{1,0:T(8,128)(2,1)S(1)}, u32[]{:S(2)}, u32[]{:S(2)}) %collective-permute-start.14) | collective-permute-done | bytes 24608 | tf_op jit(solution)/shard_map/ppermute | solution.py:32
  43.6 1.6 %collective-permute-start.15 = (f32[48,256]{1,0:T(8,128)S(1)}, f32[48,256]{1,0:T(8,128)S(1)}, u32[]{:S(2)}, u32[]{:S(2)}) collective-permute-start(f32[48,256]{1,0:T(8,128)S(1)} %get-tuple-element.72), channel_id=1, source_target_pairs={{0,2},{2,0},{4,6},{6,4},{1,3},{3,1},{5,7},{7,5},{8,10},{10,8},{12,... | collective-permute-start | bytes 147464 | tf_op jit(solution)/shard_map/ppermute | solution.py:32
  46.1 1.9 %collective-permute-start.17 = (f32[48,256]{1,0:T(8,128)S(1)}, f32[48,256]{1,0:T(8,128)S(1)}, u32[]{:S(2)}, u32[]{:S(2)}) collective-permute-start(f32[48,256]{1,0:T(8,128)S(1)} %get-tuple-element.74), channel_id=1, source_target_pairs={{0,6},{2,4},{4,2},{6,0},{1,7},{3,5},{5,3},{7,1},{8,14},{10,12},{12... | collective-permute-start | bytes 147464 | tf_op jit(solution)/shard_map/ppermute | solution.py:32
  50.6 1.4 %collective-permute-done.17.refs_3_ = f32[48,256]{1,0:T(8,128)S(1)} collective-permute-done((f32[48,256]{1,0:T(8,128)S(1)}, f32[48,256]{1,0:T(8,128)S(1)}, u32[]{:S(2)}, u32[]{:S(2)}) %collective-permute-start.17) | collective-permute-done | bytes 49184 | tf_op jit(solution)/shard_map/ppermute | solution.py:32
  52.9 1.5 %collective-permute-start.18 = (f32[24,256]{1,0:T(8,128)S(1)}, f32[24,256]{1,0:T(8,128)S(1)}, u32[]{:S(2)}, u32[]{:S(2)}) collective-permute-start(f32[24,256]{1,0:T(8,128)S(1)} %get-tuple-element.85), channel_id=1, source_target_pairs={{0,8},{8,0},{16,24},{24,16},{1,9},{9,1},{17,25},{25,17},{2,10},{10... | collective-permute-start | bytes 73736 | tf_op jit(solution)/shard_map/ppermute | solution.py:32
  54.3 1.5 %collective-permute-start.19 = (f32[24,256]{1,0:T(8,128)S(1)}, f32[24,256]{1,0:T(8,128)S(1)}, u32[]{:S(2)}, u32[]{:S(2)}) collective-permute-start(f32[24,256]{1,0:T(8,128)S(1)} %get-tuple-element.86), channel_id=1, source_target_pairs={{0,16},{8,24},{16,0},{24,8},{1,17},{9,25},{17,1},{25,9},{2,18},{10... | collective-permute-start | bytes 73736 | tf_op jit(solution)/shard_map/ppermute | solution.py:32
  56.7 1.5 %collective-permute-done.19.refs_3_ = f32[24,256]{1,0:T(8,128)S(1)} collective-permute-done((f32[24,256]{1,0:T(8,128)S(1)}, f32[24,256]{1,0:T(8,128)S(1)}, u32[]{:S(2)}, u32[]{:S(2)}) %collective-permute-start.19) | collective-permute-done | bytes 24608 | tf_op jit(solution)/shard_map/ppermute | solution.py:32
  58.2 2.4 %collective-permute-done.20.refs_4_ = f32[24,256]{1,0:T(8,128)S(1)} collective-permute-done((f32[24,256]{1,0:T(8,128)S(1)}, f32[24,256]{1,0:T(8,128)S(1)}, u32[]{:S(2)}, u32[]{:S(2)}) %collective-permute-start.20) | collective-permute-done | bytes 24608 | tf_op jit(solution)/shard_map/ppermute | solution.py:32
  (57 shorter events, 13.9 us)
Async XLA Ops:
  1.4 10.5 %collective-permute-start = (bf16[48,256]{1,0:T(8,128)(2,1)S(1)}, bf16[48,256]{1,0:T(8,128)(2,1)S(1)}, u32[]{:S(2)}, u32[]{:S(2)}) collective-permute-start(bf16[48,256]{1,0:T(8,128)(2,1)S(1)} %convert_element_type.3.refs_1_), channel_id=1, source_target_pairs={{0,8},{8,0},{16,24},{24,16},{1,9},{9,1},{17,25},{25,17},{2,10},{10... | collective-permute-start | bytes 73736 | tf_op jit(solution)/shard_map/ppermute | solution.py:32
  4.4 7.6 %collective-permute-start.1 = (bf16[48,256]{1,0:T(8,128)(2,1)S(1)}, bf16[48,256]{1,0:T(8,128)(2,1)S(1)}, u32[]{:S(2)}, u32[]{:S(2)}) collective-permute-start(bf16[48,256]{1,0:T(8,128)(2,1)S(1)} %convert_element_type.3.refs_1_), channel_id=1, source_target_pairs={{0,16},{8,24},{16,0},{24,8},{1,17},{9,25},{17,1},{25,9},{2,18},{10... | collective-permute-start | bytes 73736 | tf_op jit(solution)/shard_map/ppermute | solution.py:32
  5.9 6.0 %collective-permute-start.2 = (bf16[48,256]{1,0:T(8,128)(2,1)S(1)}, bf16[48,256]{1,0:T(8,128)(2,1)S(1)}, u32[]{:S(2)}, u32[]{:S(2)}) collective-permute-start(bf16[48,256]{1,0:T(8,128)(2,1)S(1)} %convert_element_type.3.refs_1_), channel_id=1, source_target_pairs={{0,24},{8,16},{16,8},{24,0},{1,25},{9,17},{17,9},{25,1},{2,26},{10... | collective-permute-start | bytes 73736 | tf_op jit(solution)/shard_map/ppermute | solution.py:32
  12.3 35.8 %copy-start.9 = (f32[8,3,16]{2,0,1:T(8,128)S(1)}, f32[8,3,16]{2,0,1:T(8,128)}, u32[]{:S(2)}) copy-start(f32[8,3,16]{2,0,1:T(8,128)} %param.21) | copy-start | bytes 4612
  12.3 35.9 %copy-start.10 = (s32[8,16]{1,0:T(8,128)S(1)}, s32[8,16]{1,0:T(8,128)}, u32[]{:S(2)}) copy-start(s32[8,16]{1,0:T(8,128)} %param.20) | copy-start | bytes 1540
  12.3 5.1 %collective-permute-start.3 = (f32[48,256]{1,0:T(8,128)S(1)}, f32[48,256]{1,0:T(8,128)S(1)}, u32[]{:S(2)}, u32[]{:S(2)}) collective-permute-start(f32[48,256]{1,0:T(8,128)S(1)} %get-tuple-element.50), channel_id=1, source_target_pairs={{0,2},{2,0},{4,6},{6,4},{1,3},{3,1},{5,7},{7,5},{8,10},{10,8},{12,... | collective-permute-start | bytes 147464 | tf_op jit(solution)/shard_map/ppermute | solution.py:32
  14.4 6.0 %collective-permute-start.4 = (f32[48,256]{1,0:T(8,128)S(1)}, f32[48,256]{1,0:T(8,128)S(1)}, u32[]{:S(2)}, u32[]{:S(2)}) collective-permute-start(f32[48,256]{1,0:T(8,128)S(1)} %get-tuple-element.51), channel_id=1, source_target_pairs={{0,4},{2,6},{4,0},{6,2},{1,5},{3,7},{5,1},{7,3},{8,12},{10,14},{12... | collective-permute-start | bytes 147464 | tf_op jit(solution)/shard_map/ppermute | solution.py:32
  17.0 31.2 %copy-start.5 = (s32[128]{0:T(128)S(1)}, s32[128]{0:T(128)}, u32[]{:S(2)}) copy-start(s32[128]{0:T(128)} %owned) | copy-start | bytes 1540
  17.0 5.9 %collective-permute-start.5 = (f32[48,256]{1,0:T(8,128)S(1)}, f32[48,256]{1,0:T(8,128)S(1)}, u32[]{:S(2)}, u32[]{:S(2)}) collective-permute-start(f32[48,256]{1,0:T(8,128)S(1)} %get-tuple-element.52), channel_id=1, source_target_pairs={{0,6},{2,4},{4,2},{6,0},{1,7},{3,5},{5,3},{7,1},{8,14},{10,12},{12... | collective-permute-start | bytes 147464 | tf_op jit(solution)/shard_map/ppermute | solution.py:32
  23.1 3.9 %collective-permute-start.6 = (bf16[48,256]{1,0:T(8,128)(2,1)S(1)}, bf16[48,256]{1,0:T(8,128)(2,1)S(1)}, u32[]{:S(2)}, u32[]{:S(2)}) collective-permute-start(bf16[48,256]{1,0:T(8,128)(2,1)S(1)} %get-tuple-element.57.refs_1_), channel_id=1, source_target_pairs={{0,8},{8,0},{16,24},{24,16},{1,9},{9,1},{17,25},{25,17},{2,10},{10... | collective-permute-start | bytes 73736 | tf_op jit(solution)/shard_map/ppermute | solution.py:32
  24.7 3.8 %collective-permute-start.7 = (bf16[48,256]{1,0:T(8,128)(2,1)S(1)}, bf16[48,256]{1,0:T(8,128)(2,1)S(1)}, u32[]{:S(2)}, u32[]{:S(2)}) collective-permute-start(bf16[48,256]{1,0:T(8,128)(2,1)S(1)} %get-tuple-element.57.refs_1_), channel_id=1, source_target_pairs={{0,16},{8,24},{16,0},{24,8},{1,17},{9,25},{17,1},{25,9},{2,18},{10... | collective-permute-start | bytes 73736 | tf_op jit(solution)/shard_map/ppermute | solution.py:32
  26.2 4.7 %collective-permute-start.8 = (bf16[48,256]{1,0:T(8,128)(2,1)S(1)}, bf16[48,256]{1,0:T(8,128)(2,1)S(1)}, u32[]{:S(2)}, u32[]{:S(2)}) collective-permute-start(bf16[48,256]{1,0:T(8,128)(2,1)S(1)} %get-tuple-element.57.refs_1_), channel_id=1, source_target_pairs={{0,24},{8,16},{16,8},{24,0},{1,25},{9,17},{17,9},{25,1},{2,26},{10... | collective-permute-start | bytes 73736 | tf_op jit(solution)/shard_map/ppermute | solution.py:32
  31.2 5.1 %collective-permute-start.10 = (f32[48,256]{1,0:T(8,128)S(1)}, f32[48,256]{1,0:T(8,128)S(1)}, u32[]{:S(2)}, u32[]{:S(2)}) collective-permute-start(f32[48,256]{1,0:T(8,128)S(1)} %get-tuple-element.62), channel_id=1, source_target_pairs={{0,4},{2,6},{4,0},{6,2},{1,5},{3,7},{5,1},{7,3},{8,12},{10,14},{12... | collective-permute-start | bytes 147464 | tf_op jit(solution)/shard_map/ppermute | solution.py:32
  31.2 6.1 %collective-permute-start.11 = (f32[48,256]{1,0:T(8,128)S(1)}, f32[48,256]{1,0:T(8,128)S(1)}, u32[]{:S(2)}, u32[]{:S(2)}) collective-permute-start(f32[48,256]{1,0:T(8,128)S(1)} %get-tuple-element.63), channel_id=1, source_target_pairs={{0,6},{2,4},{4,2},{6,0},{1,7},{3,5},{5,3},{7,1},{8,14},{10,12},{12... | collective-permute-start | bytes 147464 | tf_op jit(solution)/shard_map/ppermute | solution.py:32
  32.2 5.1 %collective-permute-start.9 = (f32[48,256]{1,0:T(8,128)S(1)}, f32[48,256]{1,0:T(8,128)S(1)}, u32[]{:S(2)}, u32[]{:S(2)}) collective-permute-start(f32[48,256]{1,0:T(8,128)S(1)} %get-tuple-element.61), channel_id=1, source_target_pairs={{0,2},{2,0},{4,6},{6,4},{1,3},{3,1},{5,7},{7,5},{8,10},{10,8},{12,... | collective-permute-start | bytes 147464 | tf_op jit(solution)/shard_map/ppermute | solution.py:32
  37.5 3.9 %collective-permute-start.12 = (bf16[48,256]{1,0:T(8,128)(2,1)S(1)}, bf16[48,256]{1,0:T(8,128)(2,1)S(1)}, u32[]{:S(2)}, u32[]{:S(2)}) collective-permute-start(bf16[48,256]{1,0:T(8,128)(2,1)S(1)} %get-tuple-element.69.refs_1_), channel_id=1, source_target_pairs={{0,8},{8,0},{16,24},{24,16},{1,9},{9,1},{17,25},{25,17},{2,10},{10... | collective-permute-start | bytes 73736 | tf_op jit(solution)/shard_map/ppermute | solution.py:32
  38.1 3.8 %collective-permute-start.13 = (bf16[48,256]{1,0:T(8,128)(2,1)S(1)}, bf16[48,256]{1,0:T(8,128)(2,1)S(1)}, u32[]{:S(2)}, u32[]{:S(2)}) collective-permute-start(bf16[48,256]{1,0:T(8,128)(2,1)S(1)} %get-tuple-element.69.refs_1_), channel_id=1, source_target_pairs={{0,16},{8,24},{16,0},{24,8},{1,17},{9,25},{17,1},{25,9},{2,18},{10... | collective-permute-start | bytes 73736 | tf_op jit(solution)/shard_map/ppermute | solution.py:32
  38.6 4.7 %collective-permute-start.14 = (bf16[48,256]{1,0:T(8,128)(2,1)S(1)}, bf16[48,256]{1,0:T(8,128)(2,1)S(1)}, u32[]{:S(2)}, u32[]{:S(2)}) collective-permute-start(bf16[48,256]{1,0:T(8,128)(2,1)S(1)} %get-tuple-element.69.refs_1_), channel_id=1, source_target_pairs={{0,24},{8,16},{16,8},{24,0},{1,25},{9,17},{17,9},{25,1},{2,26},{10... | collective-permute-start | bytes 73736 | tf_op jit(solution)/shard_map/ppermute | solution.py:32
  43.6 5.9 %collective-permute-start.15 = (f32[48,256]{1,0:T(8,128)S(1)}, f32[48,256]{1,0:T(8,128)S(1)}, u32[]{:S(2)}, u32[]{:S(2)}) collective-permute-start(f32[48,256]{1,0:T(8,128)S(1)} %get-tuple-element.72), channel_id=1, source_target_pairs={{0,2},{2,0},{4,6},{6,4},{1,3},{3,1},{5,7},{7,5},{8,10},{10,8},{12,... | collective-permute-start | bytes 147464 | tf_op jit(solution)/shard_map/ppermute | solution.py:32
  45.1 5.5 %collective-permute-start.16 = (f32[48,256]{1,0:T(8,128)S(1)}, f32[48,256]{1,0:T(8,128)S(1)}, u32[]{:S(2)}, u32[]{:S(2)}) collective-permute-start(f32[48,256]{1,0:T(8,128)S(1)} %get-tuple-element.73), channel_id=1, source_target_pairs={{0,4},{2,6},{4,0},{6,2},{1,5},{3,7},{5,1},{7,3},{8,12},{10,14},{12... | collective-permute-start | bytes 147464 | tf_op jit(solution)/shard_map/ppermute | solution.py:32
  46.1 5.9 %collective-permute-start.17 = (f32[48,256]{1,0:T(8,128)S(1)}, f32[48,256]{1,0:T(8,128)S(1)}, u32[]{:S(2)}, u32[]{:S(2)}) collective-permute-start(f32[48,256]{1,0:T(8,128)S(1)} %get-tuple-element.74), channel_id=1, source_target_pairs={{0,6},{2,4},{4,2},{6,0},{1,7},{3,5},{5,3},{7,1},{8,14},{10,12},{12... | collective-permute-start | bytes 147464 | tf_op jit(solution)/shard_map/ppermute | solution.py:32
  52.9 3.8 %collective-permute-start.18 = (f32[24,256]{1,0:T(8,128)S(1)}, f32[24,256]{1,0:T(8,128)S(1)}, u32[]{:S(2)}, u32[]{:S(2)}) collective-permute-start(f32[24,256]{1,0:T(8,128)S(1)} %get-tuple-element.85), channel_id=1, source_target_pairs={{0,8},{8,0},{16,24},{24,16},{1,9},{9,1},{17,25},{25,17},{2,10},{10... | collective-permute-start | bytes 73736 | tf_op jit(solution)/shard_map/ppermute | solution.py:32
  54.3 3.8 %collective-permute-start.19 = (f32[24,256]{1,0:T(8,128)S(1)}, f32[24,256]{1,0:T(8,128)S(1)}, u32[]{:S(2)}, u32[]{:S(2)}) collective-permute-start(f32[24,256]{1,0:T(8,128)S(1)} %get-tuple-element.86), channel_id=1, source_target_pairs={{0,16},{8,24},{16,0},{24,8},{1,17},{9,25},{17,1},{25,9},{2,18},{10... | collective-permute-start | bytes 73736 | tf_op jit(solution)/shard_map/ppermute | solution.py:32
  55.9 4.7 %collective-permute-start.20 = (f32[24,256]{1,0:T(8,128)S(1)}, f32[24,256]{1,0:T(8,128)S(1)}, u32[]{:S(2)}, u32[]{:S(2)}) collective-permute-start(f32[24,256]{1,0:T(8,128)S(1)} %get-tuple-element.87), channel_id=1, source_target_pairs={{0,24},{8,16},{16,8},{24,0},{1,25},{9,17},{17,9},{25,1},{2,26},{10... | collective-permute-start | bytes 73736 | tf_op jit(solution)/shard_map/ppermute | solution.py:32
  (8 other events, 53.2 us)
where the time goes:
time: 62 us; the launch traced here: 61.8 us
  starting transfers between devices  27.8 us (45%)
  waiting for transfers between devices  21.2 us (34%)
  Pallas kernels  8.12 us (13%)
  local copies, waits for them, and re-layouts  3.04 us (5%)
  between operations  0.86 us (1%)
  other arithmetic  0.81 us (1%)
    ppermute x21, starting transfers between devices, exchange(): lax.ppermute(pieces[d], axis, [(i, sends_to(i, d, n)) for i in range(n)])  27.8 us
    ppermute x21, waiting for transfers between devices, exchange(): lax.ppermute(pieces[d], axis, [(i, sends_to(i, d, n)) for i in range(n)])  21.2 us
    pallas_call x13, Pallas kernels, call(): pl.pallas_call(body, out_shape=shapes, in_specs=in_specs, out_specs=jax.t...  8.12 us
    unnamed x22, local copies, waits for them, and re-layouts  2.82 us
  transfers between devices with their start and end apart: 21, of which 15 were waited for; matrix products, arithmetic and copies ran while one was open for 0% of the time, Pallas kernels for 8%

commit v1 on v0

--- a/solution.py
+++ b/solution.py
@@ -61,7 +61,9 @@
         in_specs=in_specs,
         out_specs=jax.tree.map(lambda _: VMEM, shapes),
         scratch_shapes=scratch,
-        compiler_params=pltpu.CompilerParams(vmem_limit_bytes=min(2 * held + (2 << 20), 60 << 20)),
+        compiler_params=pltpu.CompilerParams(
+            vmem_limit_bytes=min(2 * held + (2 << 20), 60 << 20)
+        ),
         cost_estimate=pl.CostEstimate(flops=flops, bytes_accessed=nbytes, transcendentals=0),
     )(*args)
 
@@ -105,7 +107,10 @@
         functools.partial(known_kernel, lag_rows, steps, per),
         (jax.ShapeDtypeStruct((steps * lag_rows, block), BF16),) + (shape,) * steps,
         [pl.BlockSpec(memory_space=pltpu.MemorySpace.HBM)] * 2,
-        (kernel_flat, history_flat),
+        tuple(
+            pltpu.with_memory_space_constraint(t, pltpu.MemorySpace.HBM)
+            for t in (kernel_flat, history_flat)
+        ),
         2 * steps * kernel_flat.size * history_flat.shape[1],
         2 * (kernel_flat.size + history_flat.size),
         [

time: 62 us -> 59 us (0.952)
  local copies, waits for them, and re-layouts: 3.04 us -> 0.26 us
    unnamed x22 -> x18, local copies, waits for them, and re-layouts: 2.82 us -> 0.05 us
  transfers between devices with their start and end apart: 21 -> 21, of which waited for: 15 -> 16; matrix products, arithmetic and copies ran while one was open for 0% -> 0% of each run, Pallas kernels for 8% -> 8%
where the time goes in v1:
time: 59 us; the launch traced here: 58.8 us
  starting transfers between devices  27.5 us (47%)
  waiting for transfers between devices  21.4 us (36%)
  Pallas kernels  7.94 us (13%)
  between operations  0.86 us (1%)
  other arithmetic  0.81 us (1%)
    ppermute x21, starting transfers between devices, exchange(): lax.ppermute(pieces[d], axis, [(i, sends_to(i, d, n)) for i in range(n)])  27.5 us
    ppermute x21, waiting for transfers between devices, exchange(): lax.ppermute(pieces[d], axis, [(i, sends_to(i, d, n)) for i in range(n)])  21.4 us
    pallas_call x13, Pallas kernels, call(): pl.pallas_call(body, out_shape=shapes, in_specs=in_specs, out_specs=jax.t...  7.94 us
  transfers between devices with their start and end apart: 21, of which 16 were waited for; matrix products, arithmetic and copies ran while one was open for 0% of the time, Pallas kernels for 8%

profile of v1, /device:TPU:0, one launch (start us, length us, event | category | flops | bytes accessed | tf_op | source)
XLA Modules:
  0.0 58.8 jit_solution(1870097788975146902)
XLA Ops:
  1.4 3.0 %collective-permute-start = (bf16[48,256]{1,0:T(8,128)(2,1)S(1)}, bf16[48,256]{1,0:T(8,128)(2,1)S(1)}, u32[]{:S(2)}, u32[]{:S(2)}) collective-permute-start(bf16[48,256]{1,0:T(8,128)(2,1)S(1)} %convert_element_type.3.refs_1_), channel_id=1, source_target_pairs={{0,8},{8,0},{16,24},{24,16},{1,9},{9,1},{17,25},{25,17},{2,10},{10... | collective-permute-start | bytes 73736 | tf_op jit(solution)/shard_map/ppermute | solution.py:32
  4.4 1.5 %collective-permute-start.1 = (bf16[48,256]{1,0:T(8,128)(2,1)S(1)}, bf16[48,256]{1,0:T(8,128)(2,1)S(1)}, u32[]{:S(2)}, u32[]{:S(2)}) collective-permute-start(bf16[48,256]{1,0:T(8,128)(2,1)S(1)} %convert_element_type.3.refs_1_), channel_id=1, source_target_pairs={{0,16},{8,24},{16,0},{24,8},{1,17},{9,25},{17,1},{25,9},{2,18},{10... | collective-permute-start | bytes 73736 | tf_op jit(solution)/shard_map/ppermute | solution.py:32
  6.0 3.0 %shard_map.122 = (bf16[576,192]{1,0:T(8,128)(2,1)S(1)}, f32[192,256]{1,0:T(8,128)S(1)}, f32[192,256]{1,0:T(8,128)S(1)}, f32[192,256]{1,0:T(8,128)S(1)}) custom-call(bf16[3072,192]{1,0:T(8,128)(2,1)} %bitcast.20, bf16[2880,256]{1,0:T(8,128)(2,1)} %bitcast.21), custom_call_target="tpu_custom_call" | custom-call | flops 905969664 | bytes 2654208 | tf_op jit(solution)/shard_map/pallas_call | solution.py:58
  9.0 1.6 %collective-permute-done.2.refs_4_ = bf16[48,256]{1,0:T(8,128)(2,1)S(1)} collective-permute-done((bf16[48,256]{1,0:T(8,128)(2,1)S(1)}, bf16[48,256]{1,0:T(8,128)(2,1)S(1)}, u32[]{:S(2)}, u32[]{:S(2)}) %collective-permute-start.2) | collective-permute-done | bytes 24608 | tf_op jit(solution)/shard_map/ppermute | solution.py:32
  11.0 1.6 %collective-permute-start.3 = (f32[48,256]{1,0:T(8,128)S(1)}, f32[48,256]{1,0:T(8,128)S(1)}, u32[]{:S(2)}, u32[]{:S(2)}) collective-permute-start(f32[48,256]{1,0:T(8,128)S(1)} %get-tuple-element.50), channel_id=1, source_target_pairs={{0,2},{2,0},{4,6},{6,4},{1,3},{3,1},{5,7},{7,5},{8,10},{10,8},{12,... | collective-permute-start | bytes 147464 | tf_op jit(solution)/shard_map/ppermute | solution.py:32
  12.6 2.6 %collective-permute-start.4 = (f32[48,256]{1,0:T(8,128)S(1)}, f32[48,256]{1,0:T(8,128)S(1)}, u32[]{:S(2)}, u32[]{:S(2)}) collective-permute-start(f32[48,256]{1,0:T(8,128)S(1)} %get-tuple-element.51), channel_id=1, source_target_pairs={{0,4},{2,6},{4,0},{6,2},{1,5},{3,7},{5,1},{7,3},{8,12},{10,14},{12... | collective-permute-start | bytes 147464 | tf_op jit(solution)/shard_map/ppermute | solution.py:32
  15.8 2.8 %collective-permute-done.4.refs_2_ = f32[48,256]{1,0:T(8,128)S(1)} collective-permute-done((f32[48,256]{1,0:T(8,128)S(1)}, f32[48,256]{1,0:T(8,128)S(1)}, u32[]{:S(2)}, u32[]{:S(2)}) %collective-permute-start.4) | collective-permute-done | bytes 49184 | tf_op jit(solution)/shard_map/ppermute | solution.py:32
  18.7 2.4 %collective-permute-done.5.refs_3_ = f32[48,256]{1,0:T(8,128)S(1)} collective-permute-done((f32[48,256]{1,0:T(8,128)S(1)}, f32[48,256]{1,0:T(8,128)S(1)}, u32[]{:S(2)}, u32[]{:S(2)}) %collective-permute-start.5) | collective-permute-done | bytes 49184 | tf_op jit(solution)/shard_map/ppermute | solution.py:32
  21.9 1.3 %collective-permute-start.7 = (bf16[48,256]{1,0:T(8,128)(2,1)S(1)}, bf16[48,256]{1,0:T(8,128)(2,1)S(1)}, u32[]{:S(2)}, u32[]{:S(2)}) collective-permute-start(bf16[48,256]{1,0:T(8,128)(2,1)S(1)} %get-tuple-element.57.refs_1_), channel_id=1, source_target_pairs={{0,16},{8,24},{16,0},{24,8},{1,17},{9,25},{17,1},{25,9},{2,18},{10... | collective-permute-start | bytes 73736 | tf_op jit(solution)/shard_map/ppermute | solution.py:32
  23.2 1.6 %collective-permute-start.8 = (bf16[48,256]{1,0:T(8,128)(2,1)S(1)}, bf16[48,256]{1,0:T(8,128)(2,1)S(1)}, u32[]{:S(2)}, u32[]{:S(2)}) collective-permute-start(bf16[48,256]{1,0:T(8,128)(2,1)S(1)} %get-tuple-element.57.refs_1_), channel_id=1, source_target_pairs={{0,24},{8,16},{16,8},{24,0},{1,25},{9,17},{17,9},{25,1},{2,26},{10... | collective-permute-start | bytes 73736 | tf_op jit(solution)/shard_map/ppermute | solution.py:32
  25.7 2.2 %collective-permute-done.8.refs_4_ = bf16[48,256]{1,0:T(8,128)(2,1)S(1)} collective-permute-done((bf16[48,256]{1,0:T(8,128)(2,1)S(1)}, bf16[48,256]{1,0:T(8,128)(2,1)S(1)}, u32[]{:S(2)}, u32[]{:S(2)}) %collective-permute-start.8) | collective-permute-done | bytes 24608 | tf_op jit(solution)/shard_map/ppermute | solution.py:32
  29.3 2.5 %collective-permute-start.9 = (f32[48,256]{1,0:T(8,128)S(1)}, f32[48,256]{1,0:T(8,128)S(1)}, u32[]{:S(2)}, u32[]{:S(2)}) collective-permute-start(f32[48,256]{1,0:T(8,128)S(1)} %get-tuple-element.61), channel_id=1, source_target_pairs={{0,2},{2,0},{4,6},{6,4},{1,3},{3,1},{5,7},{7,5},{8,10},{10,8},{12,... | collective-permute-start | bytes 147464 | tf_op jit(solution)/shard_map/ppermute | solution.py:32
  31.9 1.3 %collective-permute-done.10.refs_2_ = f32[48,256]{1,0:T(8,128)S(1)} collective-permute-done((f32[48,256]{1,0:T(8,128)S(1)}, f32[48,256]{1,0:T(8,128)S(1)}, u32[]{:S(2)}, u32[]{:S(2)}) %collective-permute-start.10) | collective-permute-done | bytes 49184 | tf_op jit(solution)/shard_map/ppermute | solution.py:32
  35.3 1.5 %collective-permute-start.13 = (bf16[48,256]{1,0:T(8,128)(2,1)S(1)}, bf16[48,256]{1,0:T(8,128)(2,1)S(1)}, u32[]{:S(2)}, u32[]{:S(2)}) collective-permute-start(bf16[48,256]{1,0:T(8,128)(2,1)S(1)} %get-tuple-element.69.refs_1_), channel_id=1, source_target_pairs={{0,16},{8,24},{16,0},{24,8},{1,17},{9,25},{17,1},{25,9},{2,18},{10... | collective-permute-start | bytes 73736 | tf_op jit(solution)/shard_map/ppermute | solution.py:32
  36.8 1.3 %collective-permute-start.14 = (bf16[48,256]{1,0:T(8,128)(2,1)S(1)}, bf16[48,256]{1,0:T(8,128)(2,1)S(1)}, u32[]{:S(2)}, u32[]{:S(2)}) collective-permute-start(bf16[48,256]{1,0:T(8,128)(2,1)S(1)} %get-tuple-element.69.refs_1_), channel_id=1, source_target_pairs={{0,24},{8,16},{16,8},{24,0},{1,25},{9,17},{17,9},{25,1},{2,26},{10... | collective-permute-start | bytes 73736 | tf_op jit(solution)/shard_map/ppermute | solution.py:32
  39.1 2.4 %collective-permute-done.14.refs_4_ = bf16[48,256]{1,0:T(8,128)(2,1)S(1)} collective-permute-done((bf16[48,256]{1,0:T(8,128)(2,1)S(1)}, bf16[48,256]{1,0:T(8,128)(2,1)S(1)}, u32[]{:S(2)}, u32[]{:S(2)}) %collective-permute-start.14) | collective-permute-done | bytes 24608 | tf_op jit(solution)/shard_map/ppermute | solution.py:32
  41.8 1.6 %collective-permute-start.15 = (f32[48,256]{1,0:T(8,128)S(1)}, f32[48,256]{1,0:T(8,128)S(1)}, u32[]{:S(2)}, u32[]{:S(2)}) collective-permute-start(f32[48,256]{1,0:T(8,128)S(1)} %get-tuple-element.72), channel_id=1, source_target_pairs={{0,2},{2,0},{4,6},{6,4},{1,3},{3,1},{5,7},{7,5},{8,10},{10,8},{12,... | collective-permute-start | bytes 147464 | tf_op jit(solution)/shard_map/ppermute | solution.py:32
  44.3 1.9 %collective-permute-start.17 = (f32[48,256]{1,0:T(8,128)S(1)}, f32[48,256]{1,0:T(8,128)S(1)}, u32[]{:S(2)}, u32[]{:S(2)}) collective-permute-start(f32[48,256]{1,0:T(8,128)S(1)} %get-tuple-element.74), channel_id=1, source_target_pairs={{0,6},{2,4},{4,2},{6,0},{1,7},{3,5},{5,3},{7,1},{8,14},{10,12},{12... | collective-permute-start | bytes 147464 | tf_op jit(solution)/shard_map/ppermute | solution.py:32
  47.7 1.1 %collective-permute-done.16.refs_2_ = f32[48,256]{1,0:T(8,128)S(1)} collective-permute-done((f32[48,256]{1,0:T(8,128)S(1)}, f32[48,256]{1,0:T(8,128)S(1)}, u32[]{:S(2)}, u32[]{:S(2)}) %collective-permute-start.16) | collective-permute-done | bytes 49184 | tf_op jit(solution)/shard_map/ppermute | solution.py:32
  48.8 1.4 %collective-permute-done.17.refs_3_ = f32[48,256]{1,0:T(8,128)S(1)} collective-permute-done((f32[48,256]{1,0:T(8,128)S(1)}, f32[48,256]{1,0:T(8,128)S(1)}, u32[]{:S(2)}, u32[]{:S(2)}) %collective-permute-start.17) | collective-permute-done | bytes 49184 | tf_op jit(solution)/shard_map/ppermute | solution.py:32
  51.6 1.3 %collective-permute-start.19 = (f32[24,256]{1,0:T(8,128)S(1)}, f32[24,256]{1,0:T(8,128)S(1)}, u32[]{:S(2)}, u32[]{:S(2)}) collective-permute-start(f32[24,256]{1,0:T(8,128)S(1)} %get-tuple-element.86), channel_id=1, source_target_pairs={{0,16},{8,24},{16,0},{24,8},{1,17},{9,25},{17,1},{25,9},{2,18},{10... | collective-permute-start | bytes 73736 | tf_op jit(solution)/shard_map/ppermute | solution.py:32
  52.9 1.6 %collective-permute-start.20 = (f32[24,256]{1,0:T(8,128)S(1)}, f32[24,256]{1,0:T(8,128)S(1)}, u32[]{:S(2)}, u32[]{:S(2)}) collective-permute-start(f32[24,256]{1,0:T(8,128)S(1)} %get-tuple-element.87), channel_id=1, source_target_pairs={{0,24},{8,16},{16,8},{24,0},{1,25},{9,17},{17,9},{25,1},{2,26},{10... | collective-permute-start | bytes 73736 | tf_op jit(solution)/shard_map/ppermute | solution.py:32
  55.4 2.2 %collective-permute-done.20.refs_4_ = f32[24,256]{1,0:T(8,128)S(1)} collective-permute-done((f32[24,256]{1,0:T(8,128)S(1)}, f32[24,256]{1,0:T(8,128)S(1)}, u32[]{:S(2)}, u32[]{:S(2)}) %collective-permute-start.20) | collective-permute-done | bytes 24608 | tf_op jit(solution)/shard_map/ppermute | solution.py:32
  57.6 1.2 %shard_map.134 = f32[384,256]{1,0:T(8,128)} custom-call(f32[384,96]{1,0:T(8,128)S(1)} %get-tuple-element.83.refs_0_, f32[24,256]{1,0:T(8,128)S(1)} %get-tuple-element.84.refs_1_, f32[24,256]{1,0:T(8,128)S(1)} %collective-permute-done.18.refs_2_, f32[24,256]{1,0:T(8,128)S(1)} %collective-permute-done.19.refs_3_, f32[24,256]{1,0:T(8,128)S(1)} %collective-permute-done.20.refs_4_), custom_call_target="tpu_custom_call" | custom-call | flops 113246208 | bytes 393216 | tf_op jit(solution)/shard_map/pallas_call | solution.py:58
  (53 shorter events, 12.8 us)
Async XLA Ops:
  1.4 7.6 %collective-permute-start = (bf16[48,256]{1,0:T(8,128)(2,1)S(1)}, bf16[48,256]{1,0:T(8,128)(2,1)S(1)}, u32[]{:S(2)}, u32[]{:S(2)}) collective-permute-start(bf16[48,256]{1,0:T(8,128)(2,1)S(1)} %convert_element_type.3.refs_1_), channel_id=1, source_target_pairs={{0,8},{8,0},{16,24},{24,16},{1,9},{9,1},{17,25},{25,17},{2,10},{10... | collective-permute-start | bytes 73736 | tf_op jit(solution)/shard_map/ppermute | solution.py:32
  4.4 4.6 %collective-permute-start.1 = (bf16[48,256]{1,0:T(8,128)(2,1)S(1)}, bf16[48,256]{1,0:T(8,128)(2,1)S(1)}, u32[]{:S(2)}, u32[]{:S(2)}) collective-permute-start(bf16[48,256]{1,0:T(8,128)(2,1)S(1)} %convert_element_type.3.refs_1_), channel_id=1, source_target_pairs={{0,16},{8,24},{16,0},{24,8},{1,17},{9,25},{17,1},{25,9},{2,18},{10... | collective-permute-start | bytes 73736 | tf_op jit(solution)/shard_map/ppermute | solution.py:32
  5.9 4.7 %collective-permute-start.2 = (bf16[48,256]{1,0:T(8,128)(2,1)S(1)}, bf16[48,256]{1,0:T(8,128)(2,1)S(1)}, u32[]{:S(2)}, u32[]{:S(2)}) collective-permute-start(bf16[48,256]{1,0:T(8,128)(2,1)S(1)} %convert_element_type.3.refs_1_), channel_id=1, source_target_pairs={{0,24},{8,16},{16,8},{24,0},{1,25},{9,17},{17,9},{25,1},{2,26},{10... | collective-permute-start | bytes 73736 | tf_op jit(solution)/shard_map/ppermute | solution.py:32
  10.9 35.3 %copy-start.7 = (f32[8,3,16]{2,0,1:T(8,128)S(1)}, f32[8,3,16]{2,0,1:T(8,128)}, u32[]{:S(2)}) copy-start(f32[8,3,16]{2,0,1:T(8,128)} %param.21) | copy-start | bytes 4612
  11.0 35.4 %copy-start.8 = (s32[8,16]{1,0:T(8,128)S(1)}, s32[8,16]{1,0:T(8,128)}, u32[]{:S(2)}) copy-start(s32[8,16]{1,0:T(8,128)} %param.20) | copy-start | bytes 1540
  11.0 4.9 %collective-permute-start.3 = (f32[48,256]{1,0:T(8,128)S(1)}, f32[48,256]{1,0:T(8,128)S(1)}, u32[]{:S(2)}, u32[]{:S(2)}) collective-permute-start(f32[48,256]{1,0:T(8,128)S(1)} %get-tuple-element.50), channel_id=1, source_target_pairs={{0,2},{2,0},{4,6},{6,4},{1,3},{3,1},{5,7},{7,5},{8,10},{10,8},{12,... | collective-permute-start | bytes 147464 | tf_op jit(solution)/shard_map/ppermute | solution.py:32
  12.6 6.0 %collective-permute-start.4 = (f32[48,256]{1,0:T(8,128)S(1)}, f32[48,256]{1,0:T(8,128)S(1)}, u32[]{:S(2)}, u32[]{:S(2)}) collective-permute-start(f32[48,256]{1,0:T(8,128)S(1)} %get-tuple-element.51), channel_id=1, source_target_pairs={{0,4},{2,6},{4,0},{6,2},{1,5},{3,7},{5,1},{7,3},{8,12},{10,14},{12... | collective-permute-start | bytes 147464 | tf_op jit(solution)/shard_map/ppermute | solution.py:32
  15.2 31.2 %copy-start.5 = (s32[128]{0:T(128)S(1)}, s32[128]{0:T(128)}, u32[]{:S(2)}) copy-start(s32[128]{0:T(128)} %owned) | copy-start | bytes 1540
  15.2 5.9 %collective-permute-start.5 = (f32[48,256]{1,0:T(8,128)S(1)}, f32[48,256]{1,0:T(8,128)S(1)}, u32[]{:S(2)}, u32[]{:S(2)}) collective-permute-start(f32[48,256]{1,0:T(8,128)S(1)} %get-tuple-element.52), channel_id=1, source_target_pairs={{0,6},{2,4},{4,2},{6,0},{1,7},{3,5},{5,3},{7,1},{8,14},{10,12},{12... | collective-permute-start | bytes 147464 | tf_op jit(solution)/shard_map/ppermute | solution.py:32
  21.3 3.9 %collective-permute-start.6 = (bf16[48,256]{1,0:T(8,128)(2,1)S(1)}, bf16[48,256]{1,0:T(8,128)(2,1)S(1)}, u32[]{:S(2)}, u32[]{:S(2)}) collective-permute-start(bf16[48,256]{1,0:T(8,128)(2,1)S(1)} %get-tuple-element.57.refs_1_), channel_id=1, source_target_pairs={{0,8},{8,0},{16,24},{24,16},{1,9},{9,1},{17,25},{25,17},{2,10},{10... | collective-permute-start | bytes 73736 | tf_op jit(solution)/shard_map/ppermute | solution.py:32
  21.9 3.8 %collective-permute-start.7 = (bf16[48,256]{1,0:T(8,128)(2,1)S(1)}, bf16[48,256]{1,0:T(8,128)(2,1)S(1)}, u32[]{:S(2)}, u32[]{:S(2)}) collective-permute-start(bf16[48,256]{1,0:T(8,128)(2,1)S(1)} %get-tuple-element.57.refs_1_), channel_id=1, source_target_pairs={{0,16},{8,24},{16,0},{24,8},{1,17},{9,25},{17,1},{25,9},{2,18},{10... | collective-permute-start | bytes 73736 | tf_op jit(solution)/shard_map/ppermute | solution.py:32
  23.2 4.7 %collective-permute-start.8 = (bf16[48,256]{1,0:T(8,128)(2,1)S(1)}, bf16[48,256]{1,0:T(8,128)(2,1)S(1)}, u32[]{:S(2)}, u32[]{:S(2)}) collective-permute-start(bf16[48,256]{1,0:T(8,128)(2,1)S(1)} %get-tuple-element.57.refs_1_), channel_id=1, source_target_pairs={{0,24},{8,16},{16,8},{24,0},{1,25},{9,17},{17,9},{25,1},{2,26},{10... | collective-permute-start | bytes 73736 | tf_op jit(solution)/shard_map/ppermute | solution.py:32
  28.2 5.1 %collective-permute-start.10 = (f32[48,256]{1,0:T(8,128)S(1)}, f32[48,256]{1,0:T(8,128)S(1)}, u32[]{:S(2)}, u32[]{:S(2)}) collective-permute-start(f32[48,256]{1,0:T(8,128)S(1)} %get-tuple-element.62), channel_id=1, source_target_pairs={{0,4},{2,6},{4,0},{6,2},{1,5},{3,7},{5,1},{7,3},{8,12},{10,14},{12... | collective-permute-start | bytes 147464 | tf_op jit(solution)/shard_map/ppermute | solution.py:32
  28.3 6.1 %collective-permute-start.11 = (f32[48,256]{1,0:T(8,128)S(1)}, f32[48,256]{1,0:T(8,128)S(1)}, u32[]{:S(2)}, u32[]{:S(2)}) collective-permute-start(f32[48,256]{1,0:T(8,128)S(1)} %get-tuple-element.63), channel_id=1, source_target_pairs={{0,6},{2,4},{4,2},{6,0},{1,7},{3,5},{5,3},{7,1},{8,14},{10,12},{12... | collective-permute-start | bytes 147464 | tf_op jit(solution)/shard_map/ppermute | solution.py:32
  29.3 5.1 %collective-permute-start.9 = (f32[48,256]{1,0:T(8,128)S(1)}, f32[48,256]{1,0:T(8,128)S(1)}, u32[]{:S(2)}, u32[]{:S(2)}) collective-permute-start(f32[48,256]{1,0:T(8,128)S(1)} %get-tuple-element.61), channel_id=1, source_target_pairs={{0,2},{2,0},{4,6},{6,4},{1,3},{3,1},{5,7},{7,5},{8,10},{10,8},{12,... | collective-permute-start | bytes 147464 | tf_op jit(solution)/shard_map/ppermute | solution.py:32
  34.5 3.9 %collective-permute-start.12 = (bf16[48,256]{1,0:T(8,128)(2,1)S(1)}, bf16[48,256]{1,0:T(8,128)(2,1)S(1)}, u32[]{:S(2)}, u32[]{:S(2)}) collective-permute-start(bf16[48,256]{1,0:T(8,128)(2,1)S(1)} %get-tuple-element.69.refs_1_), channel_id=1, source_target_pairs={{0,8},{8,0},{16,24},{24,16},{1,9},{9,1},{17,25},{25,17},{2,10},{10... | collective-permute-start | bytes 73736 | tf_op jit(solution)/shard_map/ppermute | solution.py:32
  35.3 3.8 %collective-permute-start.13 = (bf16[48,256]{1,0:T(8,128)(2,1)S(1)}, bf16[48,256]{1,0:T(8,128)(2,1)S(1)}, u32[]{:S(2)}, u32[]{:S(2)}) collective-permute-start(bf16[48,256]{1,0:T(8,128)(2,1)S(1)} %get-tuple-element.69.refs_1_), channel_id=1, source_target_pairs={{0,16},{8,24},{16,0},{24,8},{1,17},{9,25},{17,1},{25,9},{2,18},{10... | collective-permute-start | bytes 73736 | tf_op jit(solution)/shard_map/ppermute | solution.py:32
  36.8 4.7 %collective-permute-start.14 = (bf16[48,256]{1,0:T(8,128)(2,1)S(1)}, bf16[48,256]{1,0:T(8,128)(2,1)S(1)}, u32[]{:S(2)}, u32[]{:S(2)}) collective-permute-start(bf16[48,256]{1,0:T(8,128)(2,1)S(1)} %get-tuple-element.69.refs_1_), channel_id=1, source_target_pairs={{0,24},{8,16},{16,8},{24,0},{1,25},{9,17},{17,9},{25,1},{2,26},{10... | collective-permute-start | bytes 73736 | tf_op jit(solution)/shard_map/ppermute | solution.py:32
  41.8 5.9 %collective-permute-start.15 = (f32[48,256]{1,0:T(8,128)S(1)}, f32[48,256]{1,0:T(8,128)S(1)}, u32[]{:S(2)}, u32[]{:S(2)}) collective-permute-start(f32[48,256]{1,0:T(8,128)S(1)} %get-tuple-element.72), channel_id=1, source_target_pairs={{0,2},{2,0},{4,6},{6,4},{1,3},{3,1},{5,7},{7,5},{8,10},{10,8},{12,... | collective-permute-start | bytes 147464 | tf_op jit(solution)/shard_map/ppermute | solution.py:32
  43.3 5.5 %collective-permute-start.16 = (f32[48,256]{1,0:T(8,128)S(1)}, f32[48,256]{1,0:T(8,128)S(1)}, u32[]{:S(2)}, u32[]{:S(2)}) collective-permute-start(f32[48,256]{1,0:T(8,128)S(1)} %get-tuple-element.73), channel_id=1, source_target_pairs={{0,4},{2,6},{4,0},{6,2},{1,5},{3,7},{5,1},{7,3},{8,12},{10,14},{12... | collective-permute-start | bytes 147464 | tf_op jit(solution)/shard_map/ppermute | solution.py:32
  44.3 5.9 %collective-permute-start.17 = (f32[48,256]{1,0:T(8,128)S(1)}, f32[48,256]{1,0:T(8,128)S(1)}, u32[]{:S(2)}, u32[]{:S(2)}) collective-permute-start(f32[48,256]{1,0:T(8,128)S(1)} %get-tuple-element.74), channel_id=1, source_target_pairs={{0,6},{2,4},{4,2},{6,0},{1,7},{3,5},{5,3},{7,1},{8,14},{10,12},{12... | collective-permute-start | bytes 147464 | tf_op jit(solution)/shard_map/ppermute | solution.py:32
  51.0 3.8 %collective-permute-start.18 = (f32[24,256]{1,0:T(8,128)S(1)}, f32[24,256]{1,0:T(8,128)S(1)}, u32[]{:S(2)}, u32[]{:S(2)}) collective-permute-start(f32[24,256]{1,0:T(8,128)S(1)} %get-tuple-element.85), channel_id=1, source_target_pairs={{0,8},{8,0},{16,24},{24,16},{1,9},{9,1},{17,25},{25,17},{2,10},{10... | collective-permute-start | bytes 73736 | tf_op jit(solution)/shard_map/ppermute | solution.py:32
  51.6 3.8 %collective-permute-start.19 = (f32[24,256]{1,0:T(8,128)S(1)}, f32[24,256]{1,0:T(8,128)S(1)}, u32[]{:S(2)}, u32[]{:S(2)}) collective-permute-start(f32[24,256]{1,0:T(8,128)S(1)} %get-tuple-element.86), channel_id=1, source_target_pairs={{0,16},{8,24},{16,0},{24,8},{1,17},{9,25},{17,1},{25,9},{2,18},{10... | collective-permute-start | bytes 73736 | tf_op jit(solution)/shard_map/ppermute | solution.py:32
  52.9 4.7 %collective-permute-start.20 = (f32[24,256]{1,0:T(8,128)S(1)}, f32[24,256]{1,0:T(8,128)S(1)}, u32[]{:S(2)}, u32[]{:S(2)}) collective-permute-start(f32[24,256]{1,0:T(8,128)S(1)} %get-tuple-element.87), channel_id=1, source_target_pairs={{0,24},{8,16},{16,8},{24,0},{1,25},{9,17},{17,9},{25,1},{2,26},{10... | collective-permute-start | bytes 73736 | tf_op jit(solution)/shard_map/ppermute | solution.py:32
  (6 other events, 57.6 us)

commit v2 on v1

--- a/solution.py
+++ b/solution.py
@@ -134,7 +134,7 @@
     row, col = lax.axis_index("row"), lax.axis_index("col")
     for d in range(rows):
         start = pl.multiple_of(comes_from(row, d, rows) * slab, 16)
-        whole[pl.ds(start, slab), :] = arrived[d][...]
+        whole[pl.ds(start, slab), :] = arrived[d][...].astype(BF16)
     lag_rows = rows * slab
     total[...] = bases[0][...] + dot_rows(k_ref[:lag_rows, :], whole[...])
     for d in range(cols):
@@ -235,24 +235,49 @@
     return out[0], out[1:]
 
 
-def gaps_kernel(rows, *refs):
-    weights, arrived, out, held = refs[0], refs[1 : 1 + rows], refs[-2], refs[-1]
+def settle_kernel(v, out):
+    out[...] = v[...]
+
+
+def settle(v):
+    return call(settle_kernel, jax.ShapeDtypeStruct(v.shape, F32), [VMEM], (v,), v.size, 8 * v.size)
+
+
+def gaps_kernel(rows, modules, *refs):
+    weights, arrived, out, held, done, sems = refs[0], refs[1 : 1 + rows], *refs[1 + rows :]
     size = arrived[0].shape[0]
     for d in range(rows):
         held[d * size : (d + 1) * size, :] = arrived[d][...]
-    out[...] = dot_exact(weights[...], held[...])
-
-
-def gaps(weights, arrived):
+    pieces = 4 if modules % 4 == 0 else 1
+    lines = weights.shape[0] // pieces
+    copies = []
+    for i in range(pieces):
+        at = pl.ds(i * lines, lines)
+        done[at, :] = dot_exact(weights[at, :], held[...])
+        copies.append(pltpu.make_async_copy(done.at[at], out.at[at], sems.at[i]))
+        copies[-1].start()
+    for copy in copies:
+        copy.wait()
+
+
+def gaps(weights, arrived, modules):
     points, reals = weights.shape[0], arrived[0].shape[1]
-    return call(
-        functools.partial(gaps_kernel, len(arrived)),
-        jax.ShapeDtypeStruct((points, reals), F32),
-        [VMEM] * (1 + len(arrived)),
-        (weights, *arrived),
-        12 * weights.size * reals, 4 * points * reals,
-        [pltpu.VMEM((weights.shape[1], reals), F32)],
-    )
+    shape = jax.ShapeDtypeStruct((points, reals), F32)
+    return pl.pallas_call(
+        functools.partial(gaps_kernel, len(arrived), modules),
+        out_shape=shape,
+        in_specs=[VMEM] * (1 + len(arrived)),
+        out_specs=pl.BlockSpec(memory_space=pltpu.MemorySpace.HBM),
+        scratch_shapes=[
+            pltpu.VMEM((weights.shape[1], reals), F32),
+            pltpu.VMEM((points, reals), F32),
+            pltpu.SemaphoreType.DMA((4,)),
+        ],
+        compiler_params=pltpu.CompilerParams(vmem_limit_bytes=16 << 20),
+        cost_estimate=pl.CostEstimate(
+            flops=12 * weights.size * reals, bytes_accessed=4 * points * reals, transcendentals=0
+        ),
+    )(weights, *arrived)
 
 
 def diagonals_kernel(*refs):
@@ -362,7 +387,7 @@
     slab, reals = velocity.shape
     modules, points = links.shape
     x, v, a = displacement, velocity, acceleration
-    arrived = exchange([v.astype(BF16)] * rows, "row")
+    arrived = exchange([v] * rows, "row")
     lags, bases = known_forces(
         kernel.reshape(-1, kernel.shape[3]), history.reshape(-1, reals), rows * slab, steps
     )
@@ -379,7 +404,8 @@
         else:
             v, sends = finish(parts, predicted, v, a, load, inverse, send, rows)
     moved = exchange(sends, "row")
-    out = gaps(weights, moved).reshape(modules, 3, points, reals)
+    v = settle(v)
+    out = gaps(weights, moved, modules).reshape(modules, 3, points, reals)
     return v, out.transpose(0, 2, 1, 3)
 
 

time: 59 us -> 57.9 us (0.981)
  other arithmetic: 0.81 us -> 0 us
  waiting for transfers between devices: 21.4 us -> 20.8 us
    pallas_call x0 -> x1, Pallas kernels: none -> 1.16 us  [gaps(): pl.pallas_call(functools.partial(gaps_kernel, len(arrived), modules), out...]
    pallas_call x13, Pallas kernels: 7.94 us -> 6.94 us  [call(): pl.pallas_call(body, out_shape=shapes, in_specs=in_specs, out_specs=jax.t...]
    convert_element_type x1 -> x0, other arithmetic: 0.81 us -> none  [body(): arrived = exchange([v.astype(BF16)] * rows, 'row')]
  transfers between devices with their start and end apart: 21 -> 21, of which waited for: 16 -> 15; matrix products, arithmetic and copies ran while one was open for 0% -> 0% of each run, Pallas kernels for 8% -> 9%
where the time goes in v2:
time: 57.9 us; the launch traced here: 57.7 us
  starting transfers between devices  27.7 us (48%)
  waiting for transfers between devices  20.8 us (36%)
  Pallas kernels  8.09 us (14%)
  between operations  0.85 us (1%)
    ppermute x21, starting transfers between devices, exchange(): lax.ppermute(pieces[d], axis, [(i, sends_to(i, d, n)) for i in range(n)])  27.7 us
    ppermute x21, waiting for transfers between devices, exchange(): lax.ppermute(pieces[d], axis, [(i, sends_to(i, d, n)) for i in range(n)])  20.8 us
    pallas_call x13, Pallas kernels, call(): pl.pallas_call(body, out_shape=shapes, in_specs=in_specs, out_specs=jax.t...  6.94 us
    pallas_call x1, Pallas kernels, gaps(): pl.pallas_call(functools.partial(gaps_kernel, len(arrived), modules), out...  1.16 us
  transfers between devices with their start and end apart: 21, of which 15 were waited for; matrix products, arithmetic and copies ran while one was open for 0% of the time, Pallas kernels for 9%

profile of v2, /device:TPU:0, one launch (start us, length us, event | category | flops | bytes accessed | tf_op | source)
XLA Modules:
  0.0 57.7 jit_solution(7195339313243208401)
XLA Ops:
  0.6 3.0 %collective-permute-start = (f32[48,256]{1,0:T(8,128)}, f32[48,256]{1,0:T(8,128)S(1)}, u32[]{:S(2)}, u32[]{:S(2)}) collective-permute-start(f32[48,256]{1,0:T(8,128)} %refs_5_.1), channel_id=1, source_target_pairs={{0,8},{8,0},{16,24},{24,16},{1,9},{9,1},{17,25},{25,17},{2,10},{10... | collective-permute-start | bytes 147464 | tf_op jit(solution)/shard_map/ppermute | solution.py:32
  3.7 1.5 %collective-permute-start.1 = (f32[48,256]{1,0:T(8,128)}, f32[48,256]{1,0:T(8,128)S(1)}, u32[]{:S(2)}, u32[]{:S(2)}) collective-permute-start(f32[48,256]{1,0:T(8,128)} %refs_5_.1), channel_id=1, source_target_pairs={{0,16},{8,24},{16,0},{24,8},{1,17},{9,25},{17,1},{25,9},{2,18},{10... | collective-permute-start | bytes 147464 | tf_op jit(solution)/shard_map/ppermute | solution.py:32
  5.2 3.0 %shard_map.122 = (bf16[576,192]{1,0:T(8,128)(2,1)S(1)}, f32[192,256]{1,0:T(8,128)S(1)}, f32[192,256]{1,0:T(8,128)S(1)}, f32[192,256]{1,0:T(8,128)S(1)}) custom-call(bf16[3072,192]{1,0:T(8,128)(2,1)} %bitcast.20, bf16[2880,256]{1,0:T(8,128)(2,1)} %bitcast.21), custom_call_target="tpu_custom_call" | custom-call | flops 905969664 | bytes 2654208 | tf_op jit(solution)/shard_map/pallas_call | solution.py:58
  8.2 2.1 %collective-permute-done.2.refs_4_ = f32[48,256]{1,0:T(8,128)S(1)} collective-permute-done((f32[48,256]{1,0:T(8,128)}, f32[48,256]{1,0:T(8,128)S(1)}, u32[]{:S(2)}, u32[]{:S(2)}) %collective-permute-start.2) | collective-permute-done | bytes 49184 | tf_op jit(solution)/shard_map/ppermute | solution.py:32
  10.7 1.6 %collective-permute-start.3 = (f32[48,256]{1,0:T(8,128)S(1)}, f32[48,256]{1,0:T(8,128)S(1)}, u32[]{:S(2)}, u32[]{:S(2)}) collective-permute-start(f32[48,256]{1,0:T(8,128)S(1)} %get-tuple-element.50), channel_id=1, source_target_pairs={{0,2},{2,0},{4,6},{6,4},{1,3},{3,1},{5,7},{7,5},{8,10},{10,8},{12,... | collective-permute-start | bytes 147464 | tf_op jit(solution)/shard_map/ppermute | solution.py:32
  12.3 2.6 %collective-permute-start.4 = (f32[48,256]{1,0:T(8,128)S(1)}, f32[48,256]{1,0:T(8,128)S(1)}, u32[]{:S(2)}, u32[]{:S(2)}) collective-permute-start(f32[48,256]{1,0:T(8,128)S(1)} %get-tuple-element.51), channel_id=1, source_target_pairs={{0,4},{2,6},{4,0},{6,2},{1,5},{3,7},{5,1},{7,3},{8,12},{10,14},{12... | collective-permute-start | bytes 147464 | tf_op jit(solution)/shard_map/ppermute | solution.py:32
  15.6 2.8 %collective-permute-done.4.refs_2_ = f32[48,256]{1,0:T(8,128)S(1)} collective-permute-done((f32[48,256]{1,0:T(8,128)S(1)}, f32[48,256]{1,0:T(8,128)S(1)}, u32[]{:S(2)}, u32[]{:S(2)}) %collective-permute-start.4) | collective-permute-done | bytes 49184 | tf_op jit(solution)/shard_map/ppermute | solution.py:32
  18.4 2.4 %collective-permute-done.5.refs_3_ = f32[48,256]{1,0:T(8,128)S(1)} collective-permute-done((f32[48,256]{1,0:T(8,128)S(1)}, f32[48,256]{1,0:T(8,128)S(1)}, u32[]{:S(2)}, u32[]{:S(2)}) %collective-permute-start.5) | collective-permute-done | bytes 49184 | tf_op jit(solution)/shard_map/ppermute | solution.py:32
  22.4 2.1 %collective-permute-start.8 = (bf16[48,256]{1,0:T(8,128)(2,1)S(1)}, bf16[48,256]{1,0:T(8,128)(2,1)S(1)}, u32[]{:S(2)}, u32[]{:S(2)}) collective-permute-start(bf16[48,256]{1,0:T(8,128)(2,1)S(1)} %get-tuple-element.57.refs_1_), channel_id=1, source_target_pairs={{0,24},{8,16},{16,8},{24,0},{1,25},{9,17},{17,9},{25,1},{2,26},{10... | collective-permute-start | bytes 73736 | tf_op jit(solution)/shard_map/ppermute | solution.py:32
  25.5 1.7 %collective-permute-done.8.refs_4_ = bf16[48,256]{1,0:T(8,128)(2,1)S(1)} collective-permute-done((bf16[48,256]{1,0:T(8,128)(2,1)S(1)}, bf16[48,256]{1,0:T(8,128)(2,1)S(1)}, u32[]{:S(2)}, u32[]{:S(2)}) %collective-permute-start.8) | collective-permute-done | bytes 24608 | tf_op jit(solution)/shard_map/ppermute | solution.py:32
  28.5 2.5 %collective-permute-start.9 = (f32[48,256]{1,0:T(8,128)S(1)}, f32[48,256]{1,0:T(8,128)S(1)}, u32[]{:S(2)}, u32[]{:S(2)}) collective-permute-start(f32[48,256]{1,0:T(8,128)S(1)} %get-tuple-element.61), channel_id=1, source_target_pairs={{0,2},{2,0},{4,6},{6,4},{1,3},{3,1},{5,7},{7,5},{8,10},{10,8},{12,... | collective-permute-start | bytes 147464 | tf_op jit(solution)/shard_map/ppermute | solution.py:32
  31.2 1.3 %collective-permute-done.10.refs_2_ = f32[48,256]{1,0:T(8,128)S(1)} collective-permute-done((f32[48,256]{1,0:T(8,128)S(1)}, f32[48,256]{1,0:T(8,128)S(1)}, u32[]{:S(2)}, u32[]{:S(2)}) %collective-permute-start.10) | collective-permute-done | bytes 49184 | tf_op jit(solution)/shard_map/ppermute | solution.py:32
  32.5 1.1 %collective-permute-done.11.refs_3_ = f32[48,256]{1,0:T(8,128)S(1)} collective-permute-done((f32[48,256]{1,0:T(8,128)S(1)}, f32[48,256]{1,0:T(8,128)S(1)}, u32[]{:S(2)}, u32[]{:S(2)}) %collective-permute-start.11) | collective-permute-done | bytes 49184 | tf_op jit(solution)/shard_map/ppermute | solution.py:32
  33.8 1.2 %collective-permute-start.12 = (bf16[48,256]{1,0:T(8,128)(2,1)S(1)}, bf16[48,256]{1,0:T(8,128)(2,1)S(1)}, u32[]{:S(2)}, u32[]{:S(2)}) collective-permute-start(bf16[48,256]{1,0:T(8,128)(2,1)S(1)} %get-tuple-element.69.refs_1_), channel_id=1, source_target_pairs={{0,8},{8,0},{16,24},{24,16},{1,9},{9,1},{17,25},{25,17},{2,10},{10... | collective-permute-start | bytes 73736 | tf_op jit(solution)/shard_map/ppermute | solution.py:32
  35.0 1.5 %collective-permute-start.13 = (bf16[48,256]{1,0:T(8,128)(2,1)S(1)}, bf16[48,256]{1,0:T(8,128)(2,1)S(1)}, u32[]{:S(2)}, u32[]{:S(2)}) collective-permute-start(bf16[48,256]{1,0:T(8,128)(2,1)S(1)} %get-tuple-element.69.refs_1_), channel_id=1, source_target_pairs={{0,16},{8,24},{16,0},{24,8},{1,17},{9,25},{17,1},{25,9},{2,18},{10... | collective-permute-start | bytes 73736 | tf_op jit(solution)/shard_map/ppermute | solution.py:32
  37.7 1.2 %collective-permute-done.13.refs_3_ = bf16[48,256]{1,0:T(8,128)(2,1)S(1)} collective-permute-done((bf16[48,256]{1,0:T(8,128)(2,1)S(1)}, bf16[48,256]{1,0:T(8,128)(2,1)S(1)}, u32[]{:S(2)}, u32[]{:S(2)}) %collective-permute-start.13) | collective-permute-done | bytes 24608 | tf_op jit(solution)/shard_map/ppermute | solution.py:32
  38.9 2.4 %collective-permute-done.14.refs_4_ = bf16[48,256]{1,0:T(8,128)(2,1)S(1)} collective-permute-done((bf16[48,256]{1,0:T(8,128)(2,1)S(1)}, bf16[48,256]{1,0:T(8,128)(2,1)S(1)}, u32[]{:S(2)}, u32[]{:S(2)}) %collective-permute-start.14) | collective-permute-done | bytes 24608 | tf_op jit(solution)/shard_map/ppermute | solution.py:32
  41.5 1.6 %collective-permute-start.15 = (f32[48,256]{1,0:T(8,128)S(1)}, f32[48,256]{1,0:T(8,128)S(1)}, u32[]{:S(2)}, u32[]{:S(2)}) collective-permute-start(f32[48,256]{1,0:T(8,128)S(1)} %get-tuple-element.72), channel_id=1, source_target_pairs={{0,2},{2,0},{4,6},{6,4},{1,3},{3,1},{5,7},{7,5},{8,10},{10,8},{12,... | collective-permute-start | bytes 147464 | tf_op jit(solution)/shard_map/ppermute | solution.py:32
  44.1 1.9 %collective-permute-start.17 = (f32[48,256]{1,0:T(8,128)S(1)}, f32[48,256]{1,0:T(8,128)S(1)}, u32[]{:S(2)}, u32[]{:S(2)}) collective-permute-start(f32[48,256]{1,0:T(8,128)S(1)} %get-tuple-element.74), channel_id=1, source_target_pairs={{0,6},{2,4},{4,2},{6,0},{1,7},{3,5},{5,3},{7,1},{8,14},{10,12},{12... | collective-permute-start | bytes 147464 | tf_op jit(solution)/shard_map/ppermute | solution.py:32
  47.4 1.1 %collective-permute-done.16.refs_2_ = f32[48,256]{1,0:T(8,128)S(1)} collective-permute-done((f32[48,256]{1,0:T(8,128)S(1)}, f32[48,256]{1,0:T(8,128)S(1)}, u32[]{:S(2)}, u32[]{:S(2)}) %collective-permute-start.16) | collective-permute-done | bytes 49184 | tf_op jit(solution)/shard_map/ppermute | solution.py:32
  48.6 1.4 %collective-permute-done.17.refs_3_ = f32[48,256]{1,0:T(8,128)S(1)} collective-permute-done((f32[48,256]{1,0:T(8,128)S(1)}, f32[48,256]{1,0:T(8,128)S(1)}, u32[]{:S(2)}, u32[]{:S(2)}) %collective-permute-start.17) | collective-permute-done | bytes 49184 | tf_op jit(solution)/shard_map/ppermute | solution.py:32
  51.8 2.1 %collective-permute-start.20 = (f32[24,256]{1,0:T(8,128)S(1)}, f32[24,256]{1,0:T(8,128)S(1)}, u32[]{:S(2)}, u32[]{:S(2)}) collective-permute-start(f32[24,256]{1,0:T(8,128)S(1)} %get-tuple-element.87), channel_id=1, source_target_pairs={{0,24},{8,16},{16,8},{24,0},{1,25},{9,17},{17,9},{25,1},{2,26},{10... | collective-permute-start | bytes 73736 | tf_op jit(solution)/shard_map/ppermute | solution.py:32
  54.8 1.7 %collective-permute-done.20.refs_4_ = f32[24,256]{1,0:T(8,128)S(1)} collective-permute-done((f32[24,256]{1,0:T(8,128)S(1)}, f32[24,256]{1,0:T(8,128)S(1)}, u32[]{:S(2)}, u32[]{:S(2)}) %collective-permute-start.20) | collective-permute-done | bytes 24608 | tf_op jit(solution)/shard_map/ppermute | solution.py:32
  56.6 1.2 %shard_map.135 = f32[384,256]{1,0:T(8,128)} custom-call(f32[384,96]{1,0:T(8,128)S(1)} %get-tuple-element.83.refs_0_, f32[24,256]{1,0:T(8,128)S(1)} %get-tuple-element.84.refs_1_, f32[24,256]{1,0:T(8,128)S(1)} %collective-permute-done.18.refs_2_, f32[24,256]{1,0:T(8,128)S(1)} %collective-permute-done.19.refs_3_, f32[24,256]{1,0:T(8,128)S(1)} %collective-permute-done.20.refs_4_), custom_call_target="tpu_custom_call" | custom-call | flops 113246208 | bytes 393216 | tf_op jit(solution)/shard_map/pallas_call | solution.py:266
  (53 shorter events, 11.6 us)
Async XLA Ops:
  0.6 7.6 %collective-permute-start = (f32[48,256]{1,0:T(8,128)}, f32[48,256]{1,0:T(8,128)S(1)}, u32[]{:S(2)}, u32[]{:S(2)}) collective-permute-start(f32[48,256]{1,0:T(8,128)} %refs_5_.1), channel_id=1, source_target_pairs={{0,8},{8,0},{16,24},{24,16},{1,9},{9,1},{17,25},{25,17},{2,10},{10... | collective-permute-start | bytes 147464 | tf_op jit(solution)/shard_map/ppermute | solution.py:32
  3.7 4.6 %collective-permute-start.1 = (f32[48,256]{1,0:T(8,128)}, f32[48,256]{1,0:T(8,128)S(1)}, u32[]{:S(2)}, u32[]{:S(2)}) collective-permute-start(f32[48,256]{1,0:T(8,128)} %refs_5_.1), channel_id=1, source_target_pairs={{0,16},{8,24},{16,0},{24,8},{1,17},{9,25},{17,1},{25,9},{2,18},{10... | collective-permute-start | bytes 147464 | tf_op jit(solution)/shard_map/ppermute | solution.py:32
  5.2 5.2 %collective-permute-start.2 = (f32[48,256]{1,0:T(8,128)}, f32[48,256]{1,0:T(8,128)S(1)}, u32[]{:S(2)}, u32[]{:S(2)}) collective-permute-start(f32[48,256]{1,0:T(8,128)} %refs_5_.1), channel_id=1, source_target_pairs={{0,24},{8,16},{16,8},{24,0},{1,25},{9,17},{17,9},{25,1},{2,26},{10... | collective-permute-start | bytes 147464 | tf_op jit(solution)/shard_map/ppermute | solution.py:32
  10.7 35.3 %copy-start.7 = (f32[8,3,16]{2,0,1:T(8,128)S(1)}, f32[8,3,16]{2,0,1:T(8,128)}, u32[]{:S(2)}) copy-start(f32[8,3,16]{2,0,1:T(8,128)} %param.21) | copy-start | bytes 4612
  10.7 35.4 %copy-start.8 = (s32[8,16]{1,0:T(8,128)S(1)}, s32[8,16]{1,0:T(8,128)}, u32[]{:S(2)}) copy-start(s32[8,16]{1,0:T(8,128)} %param.20) | copy-start | bytes 1540
  10.7 4.9 %collective-permute-start.3 = (f32[48,256]{1,0:T(8,128)S(1)}, f32[48,256]{1,0:T(8,128)S(1)}, u32[]{:S(2)}, u32[]{:S(2)}) collective-permute-start(f32[48,256]{1,0:T(8,128)S(1)} %get-tuple-element.50), channel_id=1, source_target_pairs={{0,2},{2,0},{4,6},{6,4},{1,3},{3,1},{5,7},{7,5},{8,10},{10,8},{12,... | collective-permute-start | bytes 147464 | tf_op jit(solution)/shard_map/ppermute | solution.py:32
  12.3 6.0 %collective-permute-start.4 = (f32[48,256]{1,0:T(8,128)S(1)}, f32[48,256]{1,0:T(8,128)S(1)}, u32[]{:S(2)}, u32[]{:S(2)}) collective-permute-start(f32[48,256]{1,0:T(8,128)S(1)} %get-tuple-element.51), channel_id=1, source_target_pairs={{0,4},{2,6},{4,0},{6,2},{1,5},{3,7},{5,1},{7,3},{8,12},{10,14},{12... | collective-permute-start | bytes 147464 | tf_op jit(solution)/shard_map/ppermute | solution.py:32
  14.9 31.2 %copy-start.5 = (s32[128]{0:T(128)S(1)}, s32[128]{0:T(128)}, u32[]{:S(2)}) copy-start(s32[128]{0:T(128)} %owned) | copy-start | bytes 1540
  14.9 5.9 %collective-permute-start.5 = (f32[48,256]{1,0:T(8,128)S(1)}, f32[48,256]{1,0:T(8,128)S(1)}, u32[]{:S(2)}, u32[]{:S(2)}) collective-permute-start(f32[48,256]{1,0:T(8,128)S(1)} %get-tuple-element.52), channel_id=1, source_target_pairs={{0,6},{2,4},{4,2},{6,0},{1,7},{3,5},{5,3},{7,1},{8,14},{10,12},{12... | collective-permute-start | bytes 147464 | tf_op jit(solution)/shard_map/ppermute | solution.py:32
  21.0 3.9 %collective-permute-start.6 = (bf16[48,256]{1,0:T(8,128)(2,1)S(1)}, bf16[48,256]{1,0:T(8,128)(2,1)S(1)}, u32[]{:S(2)}, u32[]{:S(2)}) collective-permute-start(bf16[48,256]{1,0:T(8,128)(2,1)S(1)} %get-tuple-element.57.refs_1_), channel_id=1, source_target_pairs={{0,8},{8,0},{16,24},{24,16},{1,9},{9,1},{17,25},{25,17},{2,10},{10... | collective-permute-start | bytes 73736 | tf_op jit(solution)/shard_map/ppermute | solution.py:32
  21.6 3.8 %collective-permute-start.7 = (bf16[48,256]{1,0:T(8,128)(2,1)S(1)}, bf16[48,256]{1,0:T(8,128)(2,1)S(1)}, u32[]{:S(2)}, u32[]{:S(2)}) collective-permute-start(bf16[48,256]{1,0:T(8,128)(2,1)S(1)} %get-tuple-element.57.refs_1_), channel_id=1, source_target_pairs={{0,16},{8,24},{16,0},{24,8},{1,17},{9,25},{17,1},{25,9},{2,18},{10... | collective-permute-start | bytes 73736 | tf_op jit(solution)/shard_map/ppermute | solution.py:32
  22.4 4.7 %collective-permute-start.8 = (bf16[48,256]{1,0:T(8,128)(2,1)S(1)}, bf16[48,256]{1,0:T(8,128)(2,1)S(1)}, u32[]{:S(2)}, u32[]{:S(2)}) collective-permute-start(bf16[48,256]{1,0:T(8,128)(2,1)S(1)} %get-tuple-element.57.refs_1_), channel_id=1, source_target_pairs={{0,24},{8,16},{16,8},{24,0},{1,25},{9,17},{17,9},{25,1},{2,26},{10... | collective-permute-start | bytes 73736 | tf_op jit(solution)/shard_map/ppermute | solution.py:32
  27.4 5.1 %collective-permute-start.10 = (f32[48,256]{1,0:T(8,128)S(1)}, f32[48,256]{1,0:T(8,128)S(1)}, u32[]{:S(2)}, u32[]{:S(2)}) collective-permute-start(f32[48,256]{1,0:T(8,128)S(1)} %get-tuple-element.62), channel_id=1, source_target_pairs={{0,4},{2,6},{4,0},{6,2},{1,5},{3,7},{5,1},{7,3},{8,12},{10,14},{12... | collective-permute-start | bytes 147464 | tf_op jit(solution)/shard_map/ppermute | solution.py:32
  27.5 6.1 %collective-permute-start.11 = (f32[48,256]{1,0:T(8,128)S(1)}, f32[48,256]{1,0:T(8,128)S(1)}, u32[]{:S(2)}, u32[]{:S(2)}) collective-permute-start(f32[48,256]{1,0:T(8,128)S(1)} %get-tuple-element.63), channel_id=1, source_target_pairs={{0,6},{2,4},{4,2},{6,0},{1,7},{3,5},{5,3},{7,1},{8,14},{10,12},{12... | collective-permute-start | bytes 147464 | tf_op jit(solution)/shard_map/ppermute | solution.py:32
  28.5 5.1 %collective-permute-start.9 = (f32[48,256]{1,0:T(8,128)S(1)}, f32[48,256]{1,0:T(8,128)S(1)}, u32[]{:S(2)}, u32[]{:S(2)}) collective-permute-start(f32[48,256]{1,0:T(8,128)S(1)} %get-tuple-element.61), channel_id=1, source_target_pairs={{0,2},{2,0},{4,6},{6,4},{1,3},{3,1},{5,7},{7,5},{8,10},{10,8},{12,... | collective-permute-start | bytes 147464 | tf_op jit(solution)/shard_map/ppermute | solution.py:32
  33.8 3.9 %collective-permute-start.12 = (bf16[48,256]{1,0:T(8,128)(2,1)S(1)}, bf16[48,256]{1,0:T(8,128)(2,1)S(1)}, u32[]{:S(2)}, u32[]{:S(2)}) collective-permute-start(bf16[48,256]{1,0:T(8,128)(2,1)S(1)} %get-tuple-element.69.refs_1_), channel_id=1, source_target_pairs={{0,8},{8,0},{16,24},{24,16},{1,9},{9,1},{17,25},{25,17},{2,10},{10... | collective-permute-start | bytes 73736 | tf_op jit(solution)/shard_map/ppermute | solution.py:32
  35.0 3.8 %collective-permute-start.13 = (bf16[48,256]{1,0:T(8,128)(2,1)S(1)}, bf16[48,256]{1,0:T(8,128)(2,1)S(1)}, u32[]{:S(2)}, u32[]{:S(2)}) collective-permute-start(bf16[48,256]{1,0:T(8,128)(2,1)S(1)} %get-tuple-element.69.refs_1_), channel_id=1, source_target_pairs={{0,16},{8,24},{16,0},{24,8},{1,17},{9,25},{17,1},{25,9},{2,18},{10... | collective-permute-start | bytes 73736 | tf_op jit(solution)/shard_map/ppermute | solution.py:32
  36.5 4.7 %collective-permute-start.14 = (bf16[48,256]{1,0:T(8,128)(2,1)S(1)}, bf16[48,256]{1,0:T(8,128)(2,1)S(1)}, u32[]{:S(2)}, u32[]{:S(2)}) collective-permute-start(bf16[48,256]{1,0:T(8,128)(2,1)S(1)} %get-tuple-element.69.refs_1_), channel_id=1, source_target_pairs={{0,24},{8,16},{16,8},{24,0},{1,25},{9,17},{17,9},{25,1},{2,26},{10... | collective-permute-start | bytes 73736 | tf_op jit(solution)/shard_map/ppermute | solution.py:32
  41.5 5.9 %collective-permute-start.15 = (f32[48,256]{1,0:T(8,128)S(1)}, f32[48,256]{1,0:T(8,128)S(1)}, u32[]{:S(2)}, u32[]{:S(2)}) collective-permute-start(f32[48,256]{1,0:T(8,128)S(1)} %get-tuple-element.72), channel_id=1, source_target_pairs={{0,2},{2,0},{4,6},{6,4},{1,3},{3,1},{5,7},{7,5},{8,10},{10,8},{12,... | collective-permute-start | bytes 147464 | tf_op jit(solution)/shard_map/ppermute | solution.py:32
  43.1 5.5 %collective-permute-start.16 = (f32[48,256]{1,0:T(8,128)S(1)}, f32[48,256]{1,0:T(8,128)S(1)}, u32[]{:S(2)}, u32[]{:S(2)}) collective-permute-start(f32[48,256]{1,0:T(8,128)S(1)} %get-tuple-element.73), channel_id=1, source_target_pairs={{0,4},{2,6},{4,0},{6,2},{1,5},{3,7},{5,1},{7,3},{8,12},{10,14},{12... | collective-permute-start | bytes 147464 | tf_op jit(solution)/shard_map/ppermute | solution.py:32
  44.1 5.9 %collective-permute-start.17 = (f32[48,256]{1,0:T(8,128)S(1)}, f32[48,256]{1,0:T(8,128)S(1)}, u32[]{:S(2)}, u32[]{:S(2)}) collective-permute-start(f32[48,256]{1,0:T(8,128)S(1)} %get-tuple-element.74), channel_id=1, source_target_pairs={{0,6},{2,4},{4,2},{6,0},{1,7},{3,5},{5,3},{7,1},{8,14},{10,12},{12... | collective-permute-start | bytes 147464 | tf_op jit(solution)/shard_map/ppermute | solution.py:32
  50.4 4.2 %collective-permute-start.18 = (f32[24,256]{1,0:T(8,128)S(1)}, f32[24,256]{1,0:T(8,128)S(1)}, u32[]{:S(2)}, u32[]{:S(2)}) collective-permute-start(f32[24,256]{1,0:T(8,128)S(1)} %get-tuple-element.85), channel_id=1, source_target_pairs={{0,8},{8,0},{16,24},{24,16},{1,9},{9,1},{17,25},{25,17},{2,10},{10... | collective-permute-start | bytes 73736 | tf_op jit(solution)/shard_map/ppermute | solution.py:32
  51.0 3.8 %collective-permute-start.19 = (f32[24,256]{1,0:T(8,128)S(1)}, f32[24,256]{1,0:T(8,128)S(1)}, u32[]{:S(2)}, u32[]{:S(2)}) collective-permute-start(f32[24,256]{1,0:T(8,128)S(1)} %get-tuple-element.86), channel_id=1, source_target_pairs={{0,16},{8,24},{16,0},{24,8},{1,17},{9,25},{17,1},{25,9},{2,18},{10... | collective-permute-start | bytes 73736 | tf_op jit(solution)/shard_map/ppermute | solution.py:32
  51.8 4.7 %collective-permute-start.20 = (f32[24,256]{1,0:T(8,128)S(1)}, f32[24,256]{1,0:T(8,128)S(1)}, u32[]{:S(2)}, u32[]{:S(2)}) collective-permute-start(f32[24,256]{1,0:T(8,128)S(1)} %get-tuple-element.87), channel_id=1, source_target_pairs={{0,24},{8,16},{16,8},{24,0},{1,25},{9,17},{17,9},{25,1},{2,26},{10... | collective-permute-start | bytes 73736 | tf_op jit(solution)/shard_map/ppermute | solution.py:32
  (6 other events, 55.4 us)

commit v3 on v2

v3 whole, which is shorter than its diff:
```python
import functools

import jax
import jax.numpy as jnp
from jax import lax
from jax.experimental import pallas as pl
from jax.experimental.pallas import tpu as pltpu
from jax.sharding import PartitionSpec as P


DT = 0.5
QUARTER = DT * DT / 4.0
F32 = jnp.float32
BF16 = jnp.bfloat16
HIGHEST = lax.Precision.HIGHEST
VMEM = pl.BlockSpec(memory_space=pltpu.VMEM)
SMEM = pl.BlockSpec(memory_space=pltpu.SMEM)


def sends_to(i, d, n):
    return i ^ d if n & (n - 1) == 0 else (i + d) % n


def comes_from(i, d, n):
    return i ^ d if n & (n - 1) == 0 else (i + n - d) % n


def exchange(pieces, axis):
    n = lax.axis_size(axis)
    out = [pieces[0]] + [None] * (n - 1)
    for d in range(n - 1, 0, -1):
        out[d] = lax.ppermute(pieces[d], axis, [(i, sends_to(i, d, n)) for i in range(n)])
    return out


def dot_rows(a, b):
    return lax.dot_general(a, b, (((0,), (0,)), ((), ())), preferred_element_type=F32)


def dot_exact(a, b):
    return jnp.dot(a, b, precision=HIGHEST, preferred_element_type=F32)


def padded_bytes(shape, dtype):
    size = jnp.dtype(dtype).itemsize
    dims = (1, 1, *shape)
    up = lambda n, m: -(-n // m) * m
    major = 1
    for n in dims[:-2]:
        major *= n
    return major * up(dims[-2], 32 // size) * up(dims[-1], 128) * size


def call(body, shapes, in_specs, args, flops, nbytes, scratch=()):
    arrays = list(args) + jax.tree.leaves(shapes)
    held = sum(padded_bytes(t.shape, t.dtype) for t in arrays)
    held += sum(padded_bytes(t.shape, t.dtype) for t in scratch if t.shape[1:])
    return pl.pallas_call(
        body,
        out_shape=shapes,
        in_specs=in_specs,
        out_specs=jax.tree.map(lambda _: VMEM, shapes),
        scratch_shapes=scratch,
        compiler_params=pltpu.CompilerParams(
            vmem_limit_bytes=min(2 * held + (2 << 20), 60 << 20)
        ),
        cost_estimate=pl.CostEstimate(flops=flops, bytes_accessed=nbytes, transcendentals=0),
    )(*args)


def known_kernel(lag_rows, steps, per, k_hbm, h_hbm, lags_ref, *refs):
    outs, (k_ref, h_ref, k_sem, h_sem) = refs[:steps], refs[steps:]
    total, known = k_ref.shape[0], h_ref.shape[0]
    size = per * lag_rows
    count = -(-total // size)
    copies = []
    for i in range(count):
        k_rows = pl.ds(i * size, min(size, total - i * size))
        h_rows = pl.ds(i * size, min(size, known - i * size))
        pair = (
            pltpu.make_async_copy(k_hbm.at[k_rows], k_ref.at[k_rows], k_sem.at[i]),
            pltpu.make_async_copy(h_hbm.at[h_rows], h_ref.at[h_rows], h_sem.at[i]),
        )
        pair[0].start()
        pair[1].start()
        copies.append(pair)
    for i in range(count):
        copies[i][0].wait()
        copies[i][1].wait()
        last = min((i + 1) * size, total)
        turned = k_ref[i * size : last, :].T if i else None
        for s in range(steps):
            shift = (s + 1) * lag_rows
            if i == 0:
                outs[s][...] = dot_rows(k_ref[shift:last, :], h_ref[: last - shift, :])
            else:
                known = h_ref[i * size - shift : last - shift, :]
                outs[s][...] += jnp.dot(turned, known, preferred_element_type=F32)
    lags_ref[...] = k_ref[: steps * lag_rows, :]


def known_forces(kernel_flat, history_flat, lag_rows, steps):
    block = kernel_flat.shape[1]
    shape = jax.ShapeDtypeStruct((block, history_flat.shape[1]), F32)
    per = steps + 1
    count = -(-kernel_flat.shape[0] // (per * lag_rows))
    out = call(
        functools.partial(known_kernel, lag_rows, steps, per),
        (jax.ShapeDtypeStruct((steps * lag_rows, block), BF16),) + (shape,) * steps,
        [pl.BlockSpec(memory_space=pltpu.MemorySpace.HBM)] * 2,
        tuple(
            pltpu.with_memory_space_constraint(t, pltpu.MemorySpace.HBM)
            for t in (kernel_flat, history_flat)
        ),
        2 * steps * kernel_flat.size * history_flat.shape[1],
        2 * (kernel_flat.size + history_flat.size),
        [
            pltpu.VMEM(kernel_flat.shape, BF16),
            pltpu.VMEM(history_flat.shape, BF16),
            pltpu.SemaphoreType.DMA((count,)),
            pltpu.SemaphoreType.DMA((count,)),
        ],
    )
    return out[0], out[1:]


def force_kernel(cols, ahead, keep, *refs):
    lags = refs[0]
    arrived, refs = refs[1 : 1 + keep], refs[1 + keep :]
    bases, outs = refs[:ahead], refs[ahead:-2]
    chunks, later = outs[:cols], outs[cols:]
    whole, total = refs[-2:]
    rows = keep
    slab, reals = chunks[0].shape[0] // (2 if ahead == 2 else 1), chunks[0].shape[1]
    row, col = lax.axis_index("row"), lax.axis_index("col")
    for d in range(rows):
        start = pl.multiple_of(comes_from(row, d, rows) * slab, 16)
        whole[pl.ds(start, slab), :] = arrived[d][0:slab, 0:reals].astype(BF16)
    lag_rows = rows * slab
    for n in range(ahead):
        value = bases[n][...] + dot_rows(lags[n * lag_rows : (n + 1) * lag_rows, :], whole[...])
        if n == 0 or ahead == 2:
            total[...] = value
            for d in range(cols):
                start = pl.multiple_of(sends_to(col, d, cols) * slab, 8)
                chunks[d][n * slab : (n + 1) * slab, :] = total[pl.ds(start, slab), :]
        else:
            later[n - 1][...] = value


def force_pieces(lags, arrived, bases, slab, cols):
    rows, ahead = len(arrived), len(bases)
    block, reals = bases[0].shape
    both = ahead == 2
    shapes = (jax.ShapeDtypeStruct((slab * (2 if both else 1), reals), F32),) * cols
    if not both:
        shapes += (jax.ShapeDtypeStruct((block, reals), F32),) * (ahead - 1)
    out = call(
        functools.partial(force_kernel, cols, ahead, rows),
        shapes,
        [VMEM] * (1 + rows + ahead),
        (lags, *arrived, *bases),
        2 * ahead * rows * slab * block * reals,
        4 * 2 * ahead * block * reals,
        [pltpu.VMEM((rows * slab, reals), BF16), pltpu.VMEM((block, reals), F32)],
    )
    return out[:cols], out[cols:]


def prepare_kernel(x, v, a, e, stiff, predicted, load):
    p = x[...] + DT * v[...] + QUARTER * a[...]
    predicted[...] = p
    load[...] = e[...] - dot_exact(stiff[...], p)


def prepare(x, v, a, e, stiff):
    shape = jax.ShapeDtypeStruct(x.shape, F32)
    return call(
        prepare_kernel, (shape, shape), [VMEM] * 5, (x, v, a, e, stiff),
        12 * x.size * x.shape[0], 24 * x.size,
    )


def summed(parts, first, count):
    total = parts[0][first : first + count, :]
    for part in parts[1:]:
        total = total + part[first : first + count, :]
    return total


def split(value):
    out = []
    for _ in range(3):
        out.append(value.astype(BF16).astype(F32))
        value = value - out[-1]
    return out


def first_advance_kernel(cols, rows, *refs):
    parts = refs[:cols]
    predicted, v, a, load, inverse = refs[cols : cols + 5]
    riders = refs[cols + 5 : cols + 5 + rows]
    x_out, v_out, a_out, *messages = refs[cols + 5 + rows :]
    slab, reals = v.shape
    a_next = dot_exact(inverse[...], load[...] - summed(parts, 0, slab))
    v_next = v[...] + 0.5 * DT * (a[...] + a_next)
    v_half = v_next.astype(BF16)
    for message, rider in zip(messages, riders):
        message[0:slab, 0:reals] = v_half
        message[slab:, :] = rider[...]
    v_out[...] = v_next
    a_out[...] = a_next
    x_out[...] = predicted[...] + QUARTER * a_next


def first_advance(parts, predicted, v, a, load, inverse, riders):
    shape = jax.ShapeDtypeStruct(v.shape, F32)
    lines, lanes = riders[0].shape
    message = jax.ShapeDtypeStruct((v.shape[0] + lines, lanes), BF16)
    out = call(
        functools.partial(first_advance_kernel, len(parts), len(riders)),
        (shape,) * 3 + (message,) * len(riders),
        [VMEM] * (len(parts) + 5 + len(riders)),
        (*parts, predicted, v, a, load, inverse, *riders),
        12 * v.size * v.shape[0], 40 * v.size,
    )
    return out[0], out[1], out[2], out[3:]


def last_advance_kernel(cols, rows, *refs):
    parts = refs[:cols]
    predicted, v, a, load, e, inverse, stiff, send = refs[cols : cols + 8]
    settled, *messages = refs[cols + 8 : -1]
    held = refs[-1]
    slab, _ = v.shape
    size = send.shape[0] // rows
    a_next = dot_exact(inverse[...], load[...] - summed(parts, 0, slab))
    v_next = v[...] + 0.5 * DT * (a[...] + a_next)
    x_next = predicted[...] + QUARTER * a_next
    ahead = x_next + DT * v_next + QUARTER * a_next
    known = e[...] - summed(parts, slab, slab) - dot_exact(stiff[...], ahead)
    push = dot_exact(inverse[...], known)
    settled[...] = v_next + 0.5 * DT * (a_next + push)
    moved = dot_exact(send[...], ahead + QUARTER * push)
    v_half = v_next.astype(BF16)
    cuts = split(moved)
    for d in range(rows):
        for k in range(3):
            held[k * size : (k + 1) * size, :] = cuts[k][d * size : (d + 1) * size, :]
        messages[d][0:slab, :] = v_half
        messages[d][slab:, :] = held[...].astype(BF16)


def last_advance(parts, predicted, v, a, load, e, inverse, stiff, send, rows):
    slab, reals = v.shape
    size = send.shape[0] // rows
    out = call(
        functools.partial(last_advance_kernel, len(parts), rows),
        (jax.ShapeDtypeStruct(v.shape, F32),)
        + (jax.ShapeDtypeStruct((slab + 3 * size, reals), BF16),) * rows,
        [VMEM] * (len(parts) + 8),
        (*parts, predicted, v, a, load, e, inverse, stiff, send),
        48 * v.size * slab, 40 * v.size,
        [pltpu.VMEM((3 * size, reals), F32)],
    )
    return out[0], out[1:]


def last_force_kernel(cols, rows, *refs):
    lags, listed = refs[0], refs[1]
    arrived = refs[2 : 2 + rows]
    chunks, (whole, total) = refs[2 + rows : -2], refs[-2:]
    slab = chunks[0].shape[0] // 2
    row, col = lax.axis_index("row"), lax.axis_index("col")
    for d in range(rows):
        start = pl.multiple_of(comes_from(row, d, rows) * slab, 16)
        whole[pl.ds(start, slab), :] = arrived[d][0:slab, :]
    newest = whole[...]
    total[0] = dot_rows(lags[0 : rows * slab, :], newest)
    total[1] = jnp.dot(listed[...], newest, preferred_element_type=F32)
    for d in range(cols):
        start = pl.multiple_of(sends_to(col, d, cols) * slab, 8)
        for k in range(2):
            chunks[d][k * slab : (k + 1) * slab, :] = total[k, pl.ds(start, slab), :]


def last_force(lags, listed, arrived, slab, cols):
    rows, block, reals = len(arrived), lags.shape[1], arrived[0].shape[1]
    return call(
        functools.partial(last_force_kernel, cols, rows),
        (jax.ShapeDtypeStruct((2 * slab, reals), F32),) * cols,
        [VMEM] * (2 + rows),
        (lags, listed, *arrived),
        4 * rows * slab * block * reals, 8 * block * reals,
        [pltpu.VMEM((rows * slab, reals), BF16), pltpu.VMEM((2, block, reals), F32)],
    )


def listed_kernel(rows, cols, slab, lag_rows, *refs):
    arrived, (take, own_take, weights) = refs[:rows], refs[rows : rows + 3]
    listed, pull, held, stack, blocks = refs[rows + 3 :]
    size = own_take.shape[1] // rows
    modules = slab // 6
    for d in range(rows):
        held[...] = arrived[d][slab:, :].astype(F32)
        for c in range(cols):
            stack[c, d * size : (d + 1) * size, :] = held[c * size : (c + 1) * size, 0:lag_rows]
        cuts = [held[0:size, lag_rows + 6 * k : lag_rows + 6 * k + 6] for k in range(3)]
        blocks[d * size : (d + 1) * size, :] = (cuts[2] + cuts[1]) + cuts[0]
    for c in range(cols):
        found = jnp.dot(take[c].astype(BF16), stack[c].astype(BF16), preferred_element_type=F32)
        listed[c * slab : (c + 1) * slab, :] = found.astype(BF16)
    block = dot_exact(own_take[...], blocks[...])
    lane = lax.broadcasted_iota(jnp.int32, (slab, slab), 1) // 6
    module = lax.broadcasted_iota(jnp.int32, (slab, slab), 0) // 6
    inverse = jnp.where(lane == module, jnp.concatenate([block] * modules, axis=1), 0.0)
    pull[...] = QUARTER * dot_exact(weights[...], inverse)


def listed_parts(arrived, take, own_take, weights, slab, lag_rows):
    rows, cols = len(arrived), take.shape[0]
    lines, lanes = arrived[0].shape
    return call(
        functools.partial(listed_kernel, rows, cols, slab, lag_rows),
        (
            jax.ShapeDtypeStruct((cols * slab, lag_rows), BF16),
            jax.ShapeDtypeStruct(weights.shape, F32),
        ),
        [VMEM] * (rows + 3),
        (*arrived, take, own_take, weights),
        4 * take.size * lag_rows, 4 * take.size,
        [
            pltpu.VMEM((lines - slab, lanes), F32),
            pltpu.VMEM((cols, own_take.shape[1], lag_rows), F32),
            pltpu.VMEM((own_take.shape[1], 6), F32),
        ],
    )


def settled_gaps_kernel(rows, *refs):
    arrived, (own_take, weights, out, held) = refs[:rows], refs[rows:]
    size = own_take.shape[1] // rows
    slab = own_take.shape[0]
    for d in range(rows):
        cuts = arrived[d][slab:, :].astype(F32)
        held[d * size : (d + 1) * size, :] = (
            cuts[2 * size : 3 * size, :] + cuts[size : 2 * size, :]
        ) + cuts[0:size, :]
    out[...] = dot_exact(weights[...], dot_exact(own_take[...], held[...]))


def settled_gaps(arrived, own_take, weights):
    rows, reals = len(arrived), arrived[0].shape[1]
    return call(
        functools.partial(settled_gaps_kernel, rows),
        jax.ShapeDtypeStruct((weights.shape[0], reals), F32),
        [VMEM] * (rows + 2),
        (*arrived, own_take, weights),
        12 * weights.size * reals, 4 * weights.shape[0] * reals,
        [pltpu.VMEM((own_take.shape[1], reals), F32)],
    )


def end_kernel(cols, pieces, *refs):
    parts = refs[:cols]
    settled, inverse, known, pull, v_out, out, v_done, done, sems = refs[cols:]
    slab = settled.shape[0]
    lines = known.shape[0] // pieces
    force = summed(parts, slab, slab)
    copies = []
    for i in range(pieces):
        at = pl.ds(i * lines, lines)
        done[at, :] = known[at, :] - dot_exact(pull[at, :], force)
        copies.append(pltpu.make_async_copy(done.at[at], out.at[at], sems.at[i]))
        copies[-1].start()
        if i == 0:
            push = dot_exact(inverse[...], summed(parts, 0, slab))
            v_done[...] = settled[...] - 0.5 * DT * push
            copies.append(pltpu.make_async_copy(v_done, v_out, sems.at[pieces]))
            copies[-1].start()
    for copy in copies:
        copy.wait()


def end(parts, settled, inverse, known, pull, pieces):
    hbm = pl.BlockSpec(memory_space=pltpu.MemorySpace.HBM)
    v_shape = jax.ShapeDtypeStruct(settled.shape, F32)
    shape = jax.ShapeDtypeStruct(known.shape, F32)
    return pl.pallas_call(
        functools.partial(end_kernel, len(parts), pieces),
        out_shape=(v_shape, shape),
        in_specs=[VMEM] * (len(parts) + 4),
        out_specs=(hbm, hbm),
        scratch_shapes=[
            pltpu.VMEM(settled.shape, F32),
            pltpu.VMEM(known.shape, F32),
            pltpu.SemaphoreType.DMA((pieces + 1,)),
        ],
        compiler_params=pltpu.CompilerParams(vmem_limit_bytes=16 << 20),
        cost_estimate=pl.CostEstimate(
            flops=12 * pull.size * settled.shape[1], bytes_accessed=8 * known.size, transcendentals=0
        ),
    )(*parts, settled, inverse, known, pull)


def diagonals_kernel(*refs):
    half = len(refs) // 2
    for blocks, out in zip(refs[:half], refs[half:]):
        modules = blocks.shape[1]
        width = 6 * modules
        lane = lax.broadcasted_iota(jnp.int32, (modules, width), 1) // 6
        module = lax.broadcasted_iota(jnp.int32, (modules, width), 0)
        for i in range(6):
            spread = jnp.concatenate([blocks[i]] * modules, axis=1)
            out[pl.ds(i, modules, stride=6), :] = jnp.where(lane == module, spread, 0.0)


def diagonals(*matrices):
    width = 6 * matrices[0].shape[0]
    shape = jax.ShapeDtypeStruct((width, width), F32)
    return call(
        diagonals_kernel, (shape,) * len(matrices), [VMEM] * len(matrices),
        tuple(m.transpose(1, 0, 2) for m in matrices), 100 * width * width, 16 * width * width,
    )


def plan_kernel(rows, cols, capacity, size, *refs):
    owned, links, arms, lags, blocks = refs[:5]
    riders = refs[5 : 5 + rows]
    send, take, own_take, weights, table, sends, coef, turned, held = refs[5 + rows :]
    modules = weights.shape[1] // 6
    points = links.shape[0] // modules
    row, col = lax.axis_index("row"), lax.axis_index("col")
    slab, lag_rows = modules * 6, turned.shape[1]
    turned[...] = lags[0:lag_rows, :].T
    shape = (size, slab)
    i = lax.broadcasted_iota(jnp.int32, shape, 0)
    j = lax.broadcasted_iota(jnp.int32, shape, 1)
    wide = (slab, rows * size)
    p = lax.broadcasted_iota(jnp.int32, wide, 0)
    q = lax.broadcasted_iota(jnp.int32, wide, 1)
    for c in range(cols):
        home = (row * cols + c) * modules
        for d in range(rows):
            first = (sends_to(row, d, rows) * cols + c) * modules
            wanted = jnp.full(shape, -1, jnp.int32)
            for k in range(modules):
                local = owned[first + k] - home
                here = (local >= 0) & (local < modules)
                wanted = jnp.where((i // 6 == k % capacity) & here, local, wanted)
            hit = (wanted == j // 6) & (i % 6 == j % 6)
            sends[c, d * size : (d + 1) * size, :] = jnp.where(hit, 1.0, 0.0)
        place = p % 6
        for k in range(modules):
            source = owned[home + k] // (cols * modules)
            d = source ^ row if rows & (rows - 1) == 0 else (row + rows - source) % rows
            place = place + jnp.where(p // 6 == k, d * size + k % capacity * 6, 0)
        take[c] = jnp.where(place == q, 1.0, 0.0)
        picked = jnp.dot(
            sends[c].astype(BF16), turned[c * slab : (c + 1) * slab, :], preferred_element_type=F32
        )
        for d in range(rows):
            held[d, c * size : (c + 1) * size, 0:lag_rows] = picked[d * size : (d + 1) * size, :]
    send[...] = sends[col]
    own_take[...] = take[col]
    for k in range(6):
        coef[pl.ds(k, modules, stride=6), :] = blocks[k]
    cuts = jnp.concatenate(split(dot_exact(send[...], coef[...])), axis=1)
    for d in range(rows):
        held[d, 0:size, lag_rows : lag_rows + 18] = cuts[d * size : (d + 1) * size, :]
        riders[d][...] = held[d].astype(BF16)
    count = modules * points
    table[:, 0:3] = arms[...]
    position = lax.broadcasted_iota(jnp.int32, (count, 1), 0)
    table[:, 3:4] = (position // points * 6).astype(F32)
    own = table[...]
    first_point = (row * cols + col) * count
    point = lax.broadcasted_iota(jnp.int32, (count, count), 1)
    meets = jnp.where(links[...] - first_point == point, 1.0, 0.0)
    partner = dot_exact(meets, own)
    deep = (count, slab)
    column = lax.broadcasted_iota(jnp.int32, deep, 1)
    total = [None] * 3
    for sign, side in ((1.0, own), (-1.0, partner)):
        mode = column - (side[:, 3:4] + 0.5).astype(jnp.int32)
        e = [jnp.broadcast_to(sign * side[:, c : c + 1], deep) for c in range(3)]
        for c in range(3):
            up, down = (c + 1) % 3, (c + 2) % 3
            value = jnp.where(mode == c, sign, 0.0)
            value = jnp.where(mode == 3 + up, e[down], value)
            value = jnp.where(mode == 3 + down, -e[up], value)
            total[c] = value if total[c] is None else total[c] + value
    for m in range(modules):
        for c in range(3):
            start = (m * 3 + c) * points
            weights[start : start + points, :] = total[c][m * points : (m + 1) * points, :]


def plan(owned, links, arms, lags, solve_inverse, rows, cols, lag_rows, reals):
    modules, points = links.shape
    slab, block = modules * 6, lags.shape[1]
    capacity = 2 * modules // rows
    size = -(-capacity * 6 // 8) * 8
    lines, lanes = cols * size, max(reals, lag_rows + 18)
    out = call(
        functools.partial(plan_kernel, rows, cols, capacity, size),
        (jax.ShapeDtypeStruct((lines, lanes), BF16),) * rows
        + (
            jax.ShapeDtypeStruct((rows * size, slab), F32),
            jax.ShapeDtypeStruct((cols, slab, rows * size), F32),
            jax.ShapeDtypeStruct((slab, rows * size), F32),
            jax.ShapeDtypeStruct((modules * 3 * points, slab), F32),
        ),
        [SMEM] + [VMEM] * 4,
        (
            owned,
            links.reshape(-1, 1),
            arms.transpose(0, 2, 1).reshape(-1, 3),
            lags,
            solve_inverse.transpose(1, 0, 2),
        ),
        12 * (modules * points) ** 2 * 4, 4 * modules * 3 * points * rows * modules * 6,
        [
            pltpu.VMEM((modules * points, 4), F32),
            pltpu.VMEM((cols, rows * size, slab), F32),
            pltpu.VMEM((slab, 6), F32),
            pltpu.VMEM((block, lag_rows), BF16),
            pltpu.VMEM((rows, lines, lanes), F32),
        ],
    )
    return out[:rows], *out[rows:]


def after(value, *others):
    return lax.optimization_barrier((value, *others))[0]


def body(
    kernel,
    history,
    displacement,
    velocity,
    acceleration,
    excitation,
    solve_inverse,
    stiffness,
    owned,
    links,
    arms,
):
    rows, cols = lax.axis_size("row"), lax.axis_size("col")
    steps = excitation.shape[0]
    slab, reals = velocity.shape
    modules, points = links.shape
    x, v, a = displacement, velocity, acceleration
    arrived = exchange([v] * rows, "row")
    lags, bases = known_forces(
        kernel.reshape(-1, kernel.shape[3]), history.reshape(-1, reals), rows * slab, steps
    )
    inverse, stiff = diagonals(solve_inverse, stiffness)
    predicted, load = prepare(x, v, a, excitation[0], stiff)
    pieces, bases = force_pieces(lags, arrived, bases, slab, cols)
    riders, send, take, own_take, weights = plan(
        after(owned, pieces[0]), links, arms, lags, solve_inverse, rows, cols, rows * slab, reals
    )
    parts = exchange(pieces, "col")
    x, v, a, messages = first_advance(parts, predicted, v, a, load, inverse, riders)
    arrived = exchange(messages, "row")
    predicted, load = prepare(x, v, a, excitation[1], stiff)
    pieces, _ = force_pieces(lags, arrived, bases, slab, cols)
    parts = exchange(pieces, "col")
    listed, pull = listed_parts(arrived, take, own_take, weights, slab, rows * slab)
    settled, messages = last_advance(
        parts, predicted, v, a, load, excitation[2], inverse, stiff, send, rows
    )
    arrived = exchange(messages, "row")
    pieces = last_force(lags, listed, arrived, slab, cols)
    parts = exchange(pieces, "col")
    known = settled_gaps(arrived, own_take, weights)
    v, out = end(parts, settled, inverse, known, pull, 4 if modules % 4 == 0 else 1)
    return v, out.reshape(modules, 3, points, reals).transpose(0, 2, 1, 3)


def solution(mesh):
    placed = (
        P(None, None, "col", "row"),
        P(None, None, "col", "sea"),
        P(("row", "col"), "sea"),
        P(("row", "col"), "sea"),
        P(("row", "col"), "sea"),
        P(None, ("row", "col"), "sea"),
        P(("row", "col"), None, None),
        P(("row", "col"), None, None),
        P(),
        P(("row", "col"), None),
        P(("row", "col"), None, None),
    )
    return jax.shard_map(
        body,
        mesh=mesh,
        in_specs=placed,
        out_specs=(P(("row", "col"), "sea"), P(("row", "col"), None, None, "sea")),
        check_vma=False,
    )
```

time: 57.9 us -> 55.4 us (0.957)
  starting transfers between devices: 27.7 us -> 25.1 us
  Pallas kernels: 8.09 us -> 9.61 us
  waiting for transfers between devices: 20.8 us -> 19.5 us
    ppermute x21 -> x18, starting transfers between devices: 27.7 us -> 25.1 us  [exchange(): lax.ppermute(pieces[d], axis, [(i, sends_to(i, d, n)) for i in range(n)])]
    pallas_call x13 -> x12, Pallas kernels: 6.94 us -> 8.38 us  [call(): pl.pallas_call(body, out_shape=shapes, in_specs=in_specs, out_specs=jax.t...]
    ppermute x21 -> x18, waiting for transfers between devices: 20.8 us -> 19.5 us  [exchange(): lax.ppermute(pieces[d], axis, [(i, sends_to(i, d, n)) for i in range(n)])]
  transfers between devices with their start and end apart: 21 -> 18, of which waited for: 15 -> 14; matrix products, arithmetic and copies ran while one was open for 0% -> 0% of each run, Pallas kernels for 9% -> 12%
where the time goes in v3:
time: 55.4 us; the launch traced here: 55.3 us
  starting transfers between devices  25.1 us (45%)
  waiting for transfers between devices  19.5 us (35%)
  Pallas kernels  9.61 us (17%)
  between operations  0.86 us (2%)
    ppermute x18, starting transfers between devices, exchange(): lax.ppermute(pieces[d], axis, [(i, sends_to(i, d, n)) for i in range(n)])  25.1 us
    ppermute x18, waiting for transfers between devices, exchange(): lax.ppermute(pieces[d], axis, [(i, sends_to(i, d, n)) for i in range(n)])  19.5 us
    pallas_call x12, Pallas kernels, call(): pl.pallas_call(body, out_shape=shapes, in_specs=in_specs, out_specs=jax.t...  8.38 us
    pallas_call x1, Pallas kernels, end(): pl.pallas_call(functools.partial(end_kernel, len(parts), pieces), out_sha...  1.22 us
  transfers between devices with their start and end apart: 18, of which 14 were waited for; matrix products, arithmetic and copies ran while one was open for 0% of the time, Pallas kernels for 12%

profile of v3, /device:TPU:0, one launch (start us, length us, event | category | flops | bytes accessed | tf_op | source)
XLA Modules:
  0.0 55.3 jit_solution(6292907198271003847)
XLA Ops:
  0.6 4.0 %collective-permute-start.2 = (f32[48,256]{1,0:T(8,128)}, f32[48,256]{1,0:T(8,128)S(1)}, u32[]{:S(2)}, u32[]{:S(2)}) collective-permute-start(f32[48,256]{1,0:T(8,128)} %refs_5_.1), channel_id=1, source_target_pairs={{0,24},{8,16},{16,8},{24,0},{1,25},{9,17},{17,9},{25,1},{2,26},{10... | collective-permute-start | bytes 147464 | tf_op jit(solution)/shard_map/ppermute | solution.py:32
  5.3 3.0 %shard_map.122 = (bf16[576,192]{1,0:T(8,128)(2,1)S(1)}, f32[192,256]{1,0:T(8,128)S(1)}, f32[192,256]{1,0:T(8,128)S(1)}, f32[192,256]{1,0:T(8,128)S(1)}) custom-call(bf16[3072,192]{1,0:T(8,128)(2,1)} %bitcast.20, bf16[2880,256]{1,0:T(8,128)(2,1)} %bitcast.21), custom_call_target="tpu_custom_call" | custom-call | flops 905969664 | bytes 2654208 | tf_op jit(solution)/shard_map/pallas_call | solution.py:58
  9.7 1.6 %collective-permute-start.3 = (f32[48,256]{1,0:T(8,128)S(1)}, f32[48,256]{1,0:T(8,128)S(1)}, u32[]{:S(2)}, u32[]{:S(2)}) collective-permute-start(f32[48,256]{1,0:T(8,128)S(1)} %get-tuple-element.56), channel_id=1, source_target_pairs={{0,2},{2,0},{4,6},{6,4},{1,3},{3,1},{5,7},{7,5},{8,10},{10,8},{12,... | collective-permute-start | bytes 147464 | tf_op jit(solution)/shard_map/ppermute | solution.py:32
  11.4 2.6 %collective-permute-start.4 = (f32[48,256]{1,0:T(8,128)S(1)}, f32[48,256]{1,0:T(8,128)S(1)}, u32[]{:S(2)}, u32[]{:S(2)}) collective-permute-start(f32[48,256]{1,0:T(8,128)S(1)} %get-tuple-element.57), channel_id=1, source_target_pairs={{0,4},{2,6},{4,0},{6,2},{1,5},{3,7},{5,1},{7,3},{8,12},{10,14},{12... | collective-permute-start | bytes 147464 | tf_op jit(solution)/shard_map/ppermute | solution.py:32
  14.8 1.5 %shard_map.126 = (bf16[96,256]{1,0:T(8,128)(2,1)S(1)}, bf16[96,256]{1,0:T(8,128)(2,1)S(1)}, bf16[96,256]{1,0:T(8,128)(2,1)S(1)}, bf16[96,256]{1,0:T(8,128)(2,1)S...) custom-call(s32[128]{0:T(128)S(1)} %copy-done.5, ...), custom_call_target="tpu_custom_call" | custom-call | flops 786432 | bytes 294912 | tf_op jit(solution)/shard_map/pallas_call | solution.py:58
  16.3 1.1 %collective-permute-done.4.refs_2_ = f32[48,256]{1,0:T(8,128)S(1)} collective-permute-done((f32[48,256]{1,0:T(8,128)S(1)}, f32[48,256]{1,0:T(8,128)S(1)}, u32[]{:S(2)}, u32[]{:S(2)}) %collective-permute-start.4) | collective-permute-done | bytes 49184 | tf_op jit(solution)/shard_map/ppermute | solution.py:32
  17.4 2.4 %collective-permute-done.5.refs_3_ = f32[48,256]{1,0:T(8,128)S(1)} collective-permute-done((f32[48,256]{1,0:T(8,128)S(1)}, f32[48,256]{1,0:T(8,128)S(1)}, u32[]{:S(2)}, u32[]{:S(2)}) %collective-permute-start.5) | collective-permute-done | bytes 49184 | tf_op jit(solution)/shard_map/ppermute | solution.py:32
  20.9 1.5 %collective-permute-start.7 = (bf16[144,256]{1,0:T(8,128)(2,1)S(1)}, bf16[144,256]{1,0:T(8,128)(2,1)S(1)}, u32[]{:S(2)}, u32[]{:S(2)}) collective-permute-start(bf16[144,256]{1,0:T(8,128)(2,1)S(1)} %get-tuple-element.70), channel_id=1, source_target_pairs={{0,16},{8,24},{16,0},{24,8},{1,17},{9,25},{17,1},{25,9},{2,18},{10... | collective-permute-start | bytes 221192 | tf_op jit(solution)/shard_map/ppermute | solution.py:32
  22.5 1.1 %collective-permute-start.8 = (bf16[144,256]{1,0:T(8,128)(2,1)S(1)}, bf16[144,256]{1,0:T(8,128)(2,1)S(1)}, u32[]{:S(2)}, u32[]{:S(2)}) collective-permute-start(bf16[144,256]{1,0:T(8,128)(2,1)S(1)} %get-tuple-element.71), channel_id=1, source_target_pairs={{0,24},{8,16},{16,8},{24,0},{1,25},{9,17},{17,9},{25,1},{2,26},{10... | collective-permute-start | bytes 221192 | tf_op jit(solution)/shard_map/ppermute | solution.py:32
  25.3 2.4 %collective-permute-done.8.refs_3_.refs_4_ = bf16[144,256]{1,0:T(8,128)(2,1)S(1)} collective-permute-done((bf16[144,256]{1,0:T(8,128)(2,1)S(1)}, bf16[144,256]{1,0:T(8,128)(2,1)S(1)}, u32[]{:S(2)}, u32[]{:S(2)}) %collective-permute-start.8) | collective-permute-done | bytes 73760 | tf_op jit(solution)/shard_map/ppermute | solution.py:32
  28.1 1.1 %collective-permute-start.10 = (f32[96,256]{1,0:T(8,128)S(1)}, f32[96,256]{1,0:T(8,128)S(1)}, u32[]{:S(2)}, u32[]{:S(2)}) collective-permute-start(f32[96,256]{1,0:T(8,128)S(1)} %get-tuple-element.80), channel_id=1, source_target_pairs={{0,4},{2,6},{4,0},{6,2},{1,5},{3,7},{5,1},{7,3},{8,12},{10,14},{12... | collective-permute-start | bytes 294920 | tf_op jit(solution)/shard_map/ppermute | solution.py:32
  29.2 3.2 %collective-permute-start.11 = (f32[96,256]{1,0:T(8,128)S(1)}, f32[96,256]{1,0:T(8,128)S(1)}, u32[]{:S(2)}, u32[]{:S(2)}) collective-permute-start(f32[96,256]{1,0:T(8,128)S(1)} %get-tuple-element.81), channel_id=1, source_target_pairs={{0,6},{2,4},{4,2},{6,0},{1,7},{3,5},{5,3},{7,1},{8,14},{10,12},{12... | collective-permute-start | bytes 294920 | tf_op jit(solution)/shard_map/ppermute | solution.py:32
  32.7 1.0 %collective-permute-done.10.refs_2_ = f32[96,256]{1,0:T(8,128)S(1)} collective-permute-done((f32[96,256]{1,0:T(8,128)S(1)}, f32[96,256]{1,0:T(8,128)S(1)}, u32[]{:S(2)}, u32[]{:S(2)}) %collective-permute-start.10) | collective-permute-done | bytes 98336 | tf_op jit(solution)/shard_map/ppermute | solution.py:32
  33.8 2.5 %collective-permute-done.11.refs_3_ = f32[96,256]{1,0:T(8,128)S(1)} collective-permute-done((f32[96,256]{1,0:T(8,128)S(1)}, f32[96,256]{1,0:T(8,128)S(1)}, u32[]{:S(2)}, u32[]{:S(2)}) %collective-permute-start.11) | collective-permute-done | bytes 98336 | tf_op jit(solution)/shard_map/ppermute | solution.py:32
  37.1 1.2 %collective-permute-start.12 = (bf16[120,256]{1,0:T(8,128)(2,1)S(1)}, bf16[120,256]{1,0:T(8,128)(2,1)S(1)}, u32[]{:S(2)}, u32[]{:S(2)}) collective-permute-start(bf16[120,256]{1,0:T(8,128)(2,1)S(1)} %get-tuple-element.89), channel_id=1, source_target_pairs={{0,8},{8,0},{16,24},{24,16},{1,9},{9,1},{17,25},{25,17},{2,10},{10... | collective-permute-start | bytes 184328 | tf_op jit(solution)/shard_map/ppermute | solution.py:32
  38.9 1.8 %collective-permute-start.14 = (bf16[120,256]{1,0:T(8,128)(2,1)S(1)}, bf16[120,256]{1,0:T(8,128)(2,1)S(1)}, u32[]{:S(2)}, u32[]{:S(2)}) collective-permute-start(bf16[120,256]{1,0:T(8,128)(2,1)S(1)} %get-tuple-element.91), channel_id=1, source_target_pairs={{0,24},{8,16},{16,8},{24,0},{1,25},{9,17},{17,9},{25,1},{2,26},{10... | collective-permute-start | bytes 184328 | tf_op jit(solution)/shard_map/ppermute | solution.py:32
  41.5 1.1 %collective-permute-done.13.refs_4_.refs_2_ = bf16[120,256]{1,0:T(8,128)(2,1)S(1)} collective-permute-done((bf16[120,256]{1,0:T(8,128)(2,1)S(1)}, bf16[120,256]{1,0:T(8,128)(2,1)S(1)}, u32[]{:S(2)}, u32[]{:S(2)}) %collective-permute-start.13) | collective-permute-done | bytes 61472 | tf_op jit(solution)/shard_map/ppermute | solution.py:32
  42.6 1.4 %collective-permute-done.14.refs_5_.refs_3_ = bf16[120,256]{1,0:T(8,128)(2,1)S(1)} collective-permute-done((bf16[120,256]{1,0:T(8,128)(2,1)S(1)}, bf16[120,256]{1,0:T(8,128)(2,1)S(1)}, u32[]{:S(2)}, u32[]{:S(2)}) %collective-permute-start.14) | collective-permute-done | bytes 61472 | tf_op jit(solution)/shard_map/ppermute | solution.py:32
  44.2 1.3 %collective-permute-start.15 = (f32[96,256]{1,0:T(8,128)S(1)}, f32[96,256]{1,0:T(8,128)S(1)}, u32[]{:S(2)}, u32[]{:S(2)}) collective-permute-start(f32[96,256]{1,0:T(8,128)S(1)} %get-tuple-element.93), channel_id=1, source_target_pairs={{0,2},{2,0},{4,6},{6,4},{1,3},{3,1},{5,7},{7,5},{8,10},{10,8},{12,... | collective-permute-start | bytes 294920 | tf_op jit(solution)/shard_map/ppermute | solution.py:32
  45.5 2.0 %collective-permute-start.16 = (f32[96,256]{1,0:T(8,128)S(1)}, f32[96,256]{1,0:T(8,128)S(1)}, u32[]{:S(2)}, u32[]{:S(2)}) collective-permute-start(f32[96,256]{1,0:T(8,128)S(1)} %get-tuple-element.94), channel_id=1, source_target_pairs={{0,4},{2,6},{4,0},{6,2},{1,5},{3,7},{5,1},{7,3},{8,12},{10,14},{12... | collective-permute-start | bytes 294920 | tf_op jit(solution)/shard_map/ppermute | solution.py:32
  47.5 1.1 %collective-permute-start.17 = (f32[96,256]{1,0:T(8,128)S(1)}, f32[96,256]{1,0:T(8,128)S(1)}, u32[]{:S(2)}, u32[]{:S(2)}) collective-permute-start(f32[96,256]{1,0:T(8,128)S(1)} %get-tuple-element.95), channel_id=1, source_target_pairs={{0,6},{2,4},{4,2},{6,0},{1,7},{3,5},{5,3},{7,1},{8,14},{10,12},{12... | collective-permute-start | bytes 294920 | tf_op jit(solution)/shard_map/ppermute | solution.py:32
  49.4 2.7 %collective-permute-done.16.refs_2_ = f32[96,256]{1,0:T(8,128)S(1)} collective-permute-done((f32[96,256]{1,0:T(8,128)S(1)}, f32[96,256]{1,0:T(8,128)S(1)}, u32[]{:S(2)}, u32[]{:S(2)}) %collective-permute-start.16) | collective-permute-done | bytes 98336 | tf_op jit(solution)/shard_map/ppermute | solution.py:32
  52.1 2.0 %collective-permute-done.17.refs_3_ = f32[96,256]{1,0:T(8,128)S(1)} collective-permute-done((f32[96,256]{1,0:T(8,128)S(1)}, f32[96,256]{1,0:T(8,128)S(1)}, u32[]{:S(2)}, u32[]{:S(2)}) %collective-permute-start.17) | collective-permute-done | bytes 98336 | tf_op jit(solution)/shard_map/ppermute | solution.py:32
  54.1 1.2 %shard_map.134 = (f32[48,256]{1,0:T(8,128)}, f32[384,256]{1,0:T(8,128)}) custom-call(f32[96,256]{1,0:T(8,128)S(1)} %get-tuple-element.92.refs_0_, f32[96,256]{1,0:T(8,128)S(1)} %collective-permute-done.15.refs_1_, f32[96,256]{1,0:T(8,128)S(1)} %collective-permute-done.16.refs_2_, f32[96,256]{1,0:T(8,128)S(1)} %collective-permute-done.17.refs_3_, ...), custom_call_target="tpu_custom_call" | custom-call | flops 56623104 | bytes 786432 | tf_op jit(solution)/shard_map/pallas_call | solution.py:389
  (46 shorter events, 9.4 us)
Async XLA Ops:
  0.6 7.7 %collective-permute-start.2 = (f32[48,256]{1,0:T(8,128)}, f32[48,256]{1,0:T(8,128)S(1)}, u32[]{:S(2)}, u32[]{:S(2)}) collective-permute-start(f32[48,256]{1,0:T(8,128)} %refs_5_.1), channel_id=1, source_target_pairs={{0,24},{8,16},{16,8},{24,0},{1,25},{9,17},{17,9},{25,1},{2,26},{10... | collective-permute-start | bytes 147464 | tf_op jit(solution)/shard_map/ppermute | solution.py:32
  4.6 4.3 %collective-permute-start.1 = (f32[48,256]{1,0:T(8,128)}, f32[48,256]{1,0:T(8,128)S(1)}, u32[]{:S(2)}, u32[]{:S(2)}) collective-permute-start(f32[48,256]{1,0:T(8,128)} %refs_5_.1), channel_id=1, source_target_pairs={{0,16},{8,24},{16,0},{24,8},{1,17},{9,25},{17,1},{25,9},{2,18},{10... | collective-permute-start | bytes 147464 | tf_op jit(solution)/shard_map/ppermute | solution.py:32
  5.1 4.3 %collective-permute-start = (f32[48,256]{1,0:T(8,128)}, f32[48,256]{1,0:T(8,128)S(1)}, u32[]{:S(2)}, u32[]{:S(2)}) collective-permute-start(f32[48,256]{1,0:T(8,128)} %refs_5_.1), channel_id=1, source_target_pairs={{0,8},{8,0},{16,24},{24,16},{1,9},{9,1},{17,25},{25,17},{2,10},{10... | collective-permute-start | bytes 147464 | tf_op jit(solution)/shard_map/ppermute | solution.py:32
  5.3 8.9 %copy-start.6 = (f32[3,48,256]{2,1,0:T(8,128)S(1)}, f32[3,48,256]{2,1,0:T(8,128)}, u32[]{:S(2)}) copy-start(f32[3,48,256]{2,1,0:T(8,128)} %param.16) | copy-start | bytes 442372
  5.3 8.9 %copy-start.2 = (f32[8,6,6]{2,0,1:T(8,128)S(1)}, f32[8,6,6]{2,0,1:T(8,128)}, u32[]{:S(2)}) copy-start(f32[8,6,6]{2,0,1:T(8,128)} %param.17) | copy-start | bytes 3460
  5.3 8.9 %copy-start.4 = (f32[8,6,6]{2,0,1:T(8,128)S(1)}, f32[8,6,6]{2,0,1:T(8,128)}, u32[]{:S(2)}) copy-start(f32[8,6,6]{2,0,1:T(8,128)} %param.18) | copy-start | bytes 3460
  5.3 9.1 %copy-start.8 = (s32[8,16]{1,0:T(8,128)S(1)}, s32[8,16]{1,0:T(8,128)}, u32[]{:S(2)}) copy-start(s32[8,16]{1,0:T(8,128)} %param.20) | copy-start | bytes 1540
  5.3 9.2 %copy-start.7 = (f32[8,3,16]{2,0,1:T(8,128)S(1)}, f32[8,3,16]{2,0,1:T(8,128)}, u32[]{:S(2)}) copy-start(f32[8,3,16]{2,0,1:T(8,128)} %param.21) | copy-start | bytes 4612
  8.3 6.5 %copy-start.5 = (s32[128]{0:T(128)S(1)}, s32[128]{0:T(128)}, u32[]{:S(2)}) copy-start(s32[128]{0:T(128)} %refs_0_) | copy-start | bytes 1540
  9.7 6.6 %collective-permute-start.3 = (f32[48,256]{1,0:T(8,128)S(1)}, f32[48,256]{1,0:T(8,128)S(1)}, u32[]{:S(2)}, u32[]{:S(2)}) collective-permute-start(f32[48,256]{1,0:T(8,128)S(1)} %get-tuple-element.56), channel_id=1, source_target_pairs={{0,2},{2,0},{4,6},{6,4},{1,3},{3,1},{5,7},{7,5},{8,10},{10,8},{12,... | collective-permute-start | bytes 147464 | tf_op jit(solution)/shard_map/ppermute | solution.py:32
  11.4 6.0 %collective-permute-start.4 = (f32[48,256]{1,0:T(8,128)S(1)}, f32[48,256]{1,0:T(8,128)S(1)}, u32[]{:S(2)}, u32[]{:S(2)}) collective-permute-start(f32[48,256]{1,0:T(8,128)S(1)} %get-tuple-element.57), channel_id=1, source_target_pairs={{0,4},{2,6},{4,0},{6,2},{1,5},{3,7},{5,1},{7,3},{8,12},{10,14},{12... | collective-permute-start | bytes 147464 | tf_op jit(solution)/shard_map/ppermute | solution.py:32
  14.0 5.9 %collective-permute-start.5 = (f32[48,256]{1,0:T(8,128)S(1)}, f32[48,256]{1,0:T(8,128)S(1)}, u32[]{:S(2)}, u32[]{:S(2)}) collective-permute-start(f32[48,256]{1,0:T(8,128)S(1)} %get-tuple-element.58), channel_id=1, source_target_pairs={{0,6},{2,4},{4,2},{6,0},{1,7},{3,5},{5,3},{7,1},{8,14},{10,12},{12... | collective-permute-start | bytes 147464 | tf_op jit(solution)/shard_map/ppermute | solution.py:32
  20.0 4.4 %collective-permute-start.6 = (bf16[144,256]{1,0:T(8,128)(2,1)S(1)}, bf16[144,256]{1,0:T(8,128)(2,1)S(1)}, u32[]{:S(2)}, u32[]{:S(2)}) collective-permute-start(bf16[144,256]{1,0:T(8,128)(2,1)S(1)} %get-tuple-element.69), channel_id=1, source_target_pairs={{0,8},{8,0},{16,24},{24,16},{1,9},{9,1},{17,25},{25,17},{2,10},{10... | collective-permute-start | bytes 221192 | tf_op jit(solution)/shard_map/ppermute | solution.py:32
  20.9 4.4 %collective-permute-start.7 = (bf16[144,256]{1,0:T(8,128)(2,1)S(1)}, bf16[144,256]{1,0:T(8,128)(2,1)S(1)}, u32[]{:S(2)}, u32[]{:S(2)}) collective-permute-start(bf16[144,256]{1,0:T(8,128)(2,1)S(1)} %get-tuple-element.70), channel_id=1, source_target_pairs={{0,16},{8,24},{16,0},{24,8},{1,17},{9,25},{17,1},{25,9},{2,18},{10... | collective-permute-start | bytes 221192 | tf_op jit(solution)/shard_map/ppermute | solution.py:32
  22.5 5.3 %collective-permute-start.8 = (bf16[144,256]{1,0:T(8,128)(2,1)S(1)}, bf16[144,256]{1,0:T(8,128)(2,1)S(1)}, u32[]{:S(2)}, u32[]{:S(2)}) collective-permute-start(bf16[144,256]{1,0:T(8,128)(2,1)S(1)} %get-tuple-element.71), channel_id=1, source_target_pairs={{0,24},{8,16},{16,8},{24,0},{1,25},{9,17},{17,9},{25,1},{2,26},{10... | collective-permute-start | bytes 221192 | tf_op jit(solution)/shard_map/ppermute | solution.py:32
  28.0 4.7 %collective-permute-start.9 = (f32[96,256]{1,0:T(8,128)S(1)}, f32[96,256]{1,0:T(8,128)S(1)}, u32[]{:S(2)}, u32[]{:S(2)}) collective-permute-start(f32[96,256]{1,0:T(8,128)S(1)} %get-tuple-element.79), channel_id=1, source_target_pairs={{0,2},{2,0},{4,6},{6,4},{1,3},{3,1},{5,7},{7,5},{8,10},{10,8},{12,... | collective-permute-start | bytes 294920 | tf_op jit(solution)/shard_map/ppermute | solution.py:32
  28.1 5.7 %collective-permute-start.10 = (f32[96,256]{1,0:T(8,128)S(1)}, f32[96,256]{1,0:T(8,128)S(1)}, u32[]{:S(2)}, u32[]{:S(2)}) collective-permute-start(f32[96,256]{1,0:T(8,128)S(1)} %get-tuple-element.80), channel_id=1, source_target_pairs={{0,4},{2,6},{4,0},{6,2},{1,5},{3,7},{5,1},{7,3},{8,12},{10,14},{12... | collective-permute-start | bytes 294920 | tf_op jit(solution)/shard_map/ppermute | solution.py:32
  29.2 7.0 %collective-permute-start.11 = (f32[96,256]{1,0:T(8,128)S(1)}, f32[96,256]{1,0:T(8,128)S(1)}, u32[]{:S(2)}, u32[]{:S(2)}) collective-permute-start(f32[96,256]{1,0:T(8,128)S(1)} %get-tuple-element.81), channel_id=1, source_target_pairs={{0,6},{2,4},{4,2},{6,0},{1,7},{3,5},{5,3},{7,1},{8,14},{10,12},{12... | collective-permute-start | bytes 294920 | tf_op jit(solution)/shard_map/ppermute | solution.py:32
  37.1 4.4 %collective-permute-start.12 = (bf16[120,256]{1,0:T(8,128)(2,1)S(1)}, bf16[120,256]{1,0:T(8,128)(2,1)S(1)}, u32[]{:S(2)}, u32[]{:S(2)}) collective-permute-start(bf16[120,256]{1,0:T(8,128)(2,1)S(1)} %get-tuple-element.89), channel_id=1, source_target_pairs={{0,8},{8,0},{16,24},{24,16},{1,9},{9,1},{17,25},{25,17},{2,10},{10... | collective-permute-start | bytes 184328 | tf_op jit(solution)/shard_map/ppermute | solution.py:32
  38.3 4.2 %collective-permute-start.13 = (bf16[120,256]{1,0:T(8,128)(2,1)S(1)}, bf16[120,256]{1,0:T(8,128)(2,1)S(1)}, u32[]{:S(2)}, u32[]{:S(2)}) collective-permute-start(bf16[120,256]{1,0:T(8,128)(2,1)S(1)} %get-tuple-element.90), channel_id=1, source_target_pairs={{0,16},{8,24},{16,0},{24,8},{1,17},{9,25},{17,1},{25,9},{2,18},{10... | collective-permute-start | bytes 184328 | tf_op jit(solution)/shard_map/ppermute | solution.py:32
  38.9 5.1 %collective-permute-start.14 = (bf16[120,256]{1,0:T(8,128)(2,1)S(1)}, bf16[120,256]{1,0:T(8,128)(2,1)S(1)}, u32[]{:S(2)}, u32[]{:S(2)}) collective-permute-start(bf16[120,256]{1,0:T(8,128)(2,1)S(1)} %get-tuple-element.91), channel_id=1, source_target_pairs={{0,24},{8,16},{16,8},{24,0},{1,25},{9,17},{17,9},{25,1},{2,26},{10... | collective-permute-start | bytes 184328 | tf_op jit(solution)/shard_map/ppermute | solution.py:32
  44.2 5.2 %collective-permute-start.15 = (f32[96,256]{1,0:T(8,128)S(1)}, f32[96,256]{1,0:T(8,128)S(1)}, u32[]{:S(2)}, u32[]{:S(2)}) collective-permute-start(f32[96,256]{1,0:T(8,128)S(1)} %get-tuple-element.93), channel_id=1, source_target_pairs={{0,2},{2,0},{4,6},{6,4},{1,3},{3,1},{5,7},{7,5},{8,10},{10,8},{12,... | collective-permute-start | bytes 294920 | tf_op jit(solution)/shard_map/ppermute | solution.py:32
  45.5 6.6 %collective-permute-start.16 = (f32[96,256]{1,0:T(8,128)S(1)}, f32[96,256]{1,0:T(8,128)S(1)}, u32[]{:S(2)}, u32[]{:S(2)}) collective-permute-start(f32[96,256]{1,0:T(8,128)S(1)} %get-tuple-element.94), channel_id=1, source_target_pairs={{0,4},{2,6},{4,0},{6,2},{1,5},{3,7},{5,1},{7,3},{8,12},{10,14},{12... | collective-permute-start | bytes 294920 | tf_op jit(solution)/shard_map/ppermute | solution.py:32
  47.5 6.5 %collective-permute-start.17 = (f32[96,256]{1,0:T(8,128)S(1)}, f32[96,256]{1,0:T(8,128)S(1)}, u32[]{:S(2)}, u32[]{:S(2)}) collective-permute-start(f32[96,256]{1,0:T(8,128)S(1)} %get-tuple-element.95), channel_id=1, source_target_pairs={{0,6},{2,4},{4,2},{6,0},{1,7},{3,5},{5,3},{7,1},{8,14},{10,12},{12... | collective-permute-start | bytes 294920 | tf_op jit(solution)/shard_map/ppermute | solution.py:32
  (3 other events, 16.8 us)

commit v4 on v3

--- a/solution.py
+++ b/solution.py
@@ -76,33 +76,41 @@
     copies = []
     for i in range(count):
         k_rows = pl.ds(i * size, min(size, total - i * size))
-        h_rows = pl.ds(i * size, min(size, known - i * size))
-        pair = (
-            pltpu.make_async_copy(k_hbm.at[k_rows], k_ref.at[k_rows], k_sem.at[i]),
-            pltpu.make_async_copy(h_hbm.at[h_rows], h_ref.at[h_rows], h_sem.at[i]),
-        )
-        pair[0].start()
-        pair[1].start()
+        pair = [pltpu.make_async_copy(k_hbm.at[k_rows], k_ref.at[k_rows], k_sem.at[i])]
+        if i * size < known:
+            h_rows = pl.ds(i * size, min(size, known - i * size))
+            pair.append(pltpu.make_async_copy(h_hbm.at[h_rows], h_ref.at[h_rows], h_sem.at[i]))
         copies.append(pair)
+    for i in range(min(2, count)):
+        for copy in copies[i]:
+            copy.start()
     for i in range(count):
-        copies[i][0].wait()
-        copies[i][1].wait()
+        for copy in copies[i]:
+            copy.wait()
+        if i + 2 < count:
+            for copy in copies[i + 2]:
+                copy.start()
         last = min((i + 1) * size, total)
-        turned = k_ref[i * size : last, :].T if i else None
+        turned = k_ref[i * size : last, :].T if i * size >= steps * lag_rows else None
         for s in range(steps):
             shift = (s + 1) * lag_rows
-            if i == 0:
-                outs[s][...] = dot_rows(k_ref[shift:last, :], h_ref[: last - shift, :])
+            first = max(i * size, shift)
+            if first >= last:
+                outs[s][...] = jnp.zeros_like(outs[s])
+                continue
+            rows = h_ref[first - shift : last - shift, :]
+            if turned is None:
+                term = dot_rows(k_ref[first:last, :], rows)
             else:
-                known = h_ref[i * size - shift : last - shift, :]
-                outs[s][...] += jnp.dot(turned, known, preferred_element_type=F32)
+                term = jnp.dot(turned, rows, preferred_element_type=F32)
+            outs[s][...] = term if i == 0 else outs[s][...] + term
     lags_ref[...] = k_ref[: steps * lag_rows, :]
 
 
 def known_forces(kernel_flat, history_flat, lag_rows, steps):
     block = kernel_flat.shape[1]
     shape = jax.ShapeDtypeStruct((block, history_flat.shape[1]), F32)
-    per = steps + 1
+    per = 2
     count = -(-kernel_flat.shape[0] // (per * lag_rows))
     out = call(
         functools.partial(known_kernel, lag_rows, steps, per),
@@ -227,21 +235,39 @@
     return out[0], out[1], out[2], out[3:]
 
 
+def drift_kernel(predicted, v, a, e, early, moved, both):
+    slab = v.shape[0]
+    both[0:slab, :] = predicted[...] + DT * v[...] + 0.5 * DT * DT * a[...]
+    both[slab:, :] = e[...]
+    moved[...] = dot_exact(early[...], both[...])
+
+
+def drift(predicted, v, a, e, early):
+    lines, reals = early.shape[0], v.shape[1]
+    return call(
+        drift_kernel,
+        jax.ShapeDtypeStruct((lines, reals), F32),
+        [VMEM] * 5,
+        (predicted, v, a, e, early),
+        12 * early.size * reals, 24 * v.size,
+        [pltpu.VMEM((2 * v.shape[0], reals), F32)],
+    )
+
+
 def last_advance_kernel(cols, rows, *refs):
     parts = refs[:cols]
-    predicted, v, a, load, e, inverse, stiff, send = refs[cols : cols + 8]
-    settled, *messages = refs[cols + 8 : -1]
-    held = refs[-1]
+    v, a, load, inverse, drifted, late = refs[cols : cols + 6]
+    v_out, a_out, rest, *messages = refs[cols + 6 : -2]
+    held, both = refs[-2:]
     slab, _ = v.shape
-    size = send.shape[0] // rows
-    a_next = dot_exact(inverse[...], load[...] - summed(parts, 0, slab))
+    size = late.shape[0] // rows
+    turning = load[...] - summed(parts, 0, slab)
+    known = summed(parts, slab, slab)
+    both[0:slab, :] = turning
+    both[slab:, :] = known
+    moved = drifted[...] + dot_exact(late[...], both[...])
+    a_next = dot_exact(inverse[...], turning)
     v_next = v[...] + 0.5 * DT * (a[...] + a_next)
-    x_next = predicted[...] + QUARTER * a_next
-    ahead = x_next + DT * v_next + QUARTER * a_next
-    known = e[...] - summed(parts, slab, slab) - dot_exact(stiff[...], ahead)
-    push = dot_exact(inverse[...], known)
-    settled[...] = v_next + 0.5 * DT * (a_next + push)
-    moved = dot_exact(send[...], ahead + QUARTER * push)
     v_half = v_next.astype(BF16)
     cuts = split(moved)
     for d in range(rows):
@@ -249,21 +275,40 @@
             held[k * size : (k + 1) * size, :] = cuts[k][d * size : (d + 1) * size, :]
         messages[d][0:slab, :] = v_half
         messages[d][slab:, :] = held[...].astype(BF16)
-
-
-def last_advance(parts, predicted, v, a, load, e, inverse, stiff, send, rows):
+    v_out[...] = v_next
+    a_out[...] = a_next
+    rest[...] = known
+
+
+def last_advance(parts, v, a, load, inverse, drifted, late, rows):
     slab, reals = v.shape
-    size = send.shape[0] // rows
+    size = late.shape[0] // rows
+    shape = jax.ShapeDtypeStruct(v.shape, F32)
     out = call(
         functools.partial(last_advance_kernel, len(parts), rows),
-        (jax.ShapeDtypeStruct(v.shape, F32),)
-        + (jax.ShapeDtypeStruct((slab + 3 * size, reals), BF16),) * rows,
-        [VMEM] * (len(parts) + 8),
-        (*parts, predicted, v, a, load, e, inverse, stiff, send),
+        (shape,) * 3 + (jax.ShapeDtypeStruct((slab + 3 * size, reals), BF16),) * rows,
+        [VMEM] * (len(parts) + 6),
+        (*parts, v, a, load, inverse, drifted, late),
         48 * v.size * slab, 40 * v.size,
-        [pltpu.VMEM((3 * size, reals), F32)],
-    )
-    return out[0], out[1:]
+        [pltpu.VMEM((3 * size, reals), F32), pltpu.VMEM((2 * slab, reals), F32)],
+    )
+    return out[0], out[1], out[2], out[3:]
+
+
+def settled_kernel(predicted, v, a, e, rest, inverse, stiff, out):
+    ahead = predicted[...] + DT * v[...] + 2 * QUARTER * a[...]
+    push = dot_exact(inverse[...], e[...] - rest[...] - dot_exact(stiff[...], ahead))
+    out[...] = v[...] + 0.5 * DT * (a[...] + push)
+
+
+def settled_velocity(predicted, v, a, e, rest, inverse, stiff):
+    return call(
+        settled_kernel,
+        jax.ShapeDtypeStruct(v.shape, F32),
+        [VMEM] * 7,
+        (predicted, v, a, e, rest, inverse, stiff),
+        24 * v.size * v.shape[0], 32 * v.size,
+    )
 
 
 def last_force_kernel(cols, rows, *refs):
@@ -425,11 +470,10 @@
 
 
 def plan_kernel(rows, cols, capacity, size, *refs):
-    owned, links, arms, lags, blocks = refs[:5]
-    riders = refs[5 : 5 + rows]
-    send, take, own_take, weights, table, sends, coef, turned, held = refs[5 + rows :]
-    modules = weights.shape[1] // 6
-    points = links.shape[0] // modules
+    owned, lags, blocks = refs[:3]
+    riders = refs[3 : 3 + rows]
+    send, take, own_take, sends, coef, turned, held = refs[3 + rows :]
+    modules = send.shape[1] // 6
     row, col = lax.axis_index("row"), lax.axis_index("col")
     slab, lag_rows = modules * 6, turned.shape[1]
     turned[...] = lags[0:lag_rows, :].T
@@ -469,6 +513,14 @@
     for d in range(rows):
         held[d, 0:size, lag_rows : lag_rows + 18] = cuts[d * size : (d + 1) * size, :]
         riders[d][...] = held[d].astype(BF16)
+
+
+def gap_map_kernel(links, arms, inverse, stiff, send, weights, early, late, table):
+    modules = weights.shape[1] // 6
+    points = links.shape[0] // modules
+    row, col = lax.axis_index("row"), lax.axis_index("col")
+    cols = lax.axis_size("col")
+    slab = modules * 6
     count = modules * points
     table[:, 0:3] = arms[...]
     position = lax.broadcasted_iota(jnp.int32, (count, 1), 0)
@@ -494,10 +546,30 @@
         for c in range(3):
             start = (m * 3 + c) * points
             weights[start : start + points, :] = total[c][m * points : (m + 1) * points, :]
-
-
-def plan(owned, links, arms, lags, solve_inverse, rows, cols, lag_rows, reals):
+    press = dot_exact(send[...], QUARTER * inverse[...])
+    drift = send[...] - dot_exact(press, stiff[...])
+    early[:, 0:slab] = drift
+    early[:, slab:] = press
+    late[:, 0:slab] = dot_exact((2 * QUARTER + 0.25 * DT) * drift, inverse[...])
+    late[:, slab:] = -press
+
+
+def gap_map(links, arms, inverse, stiff, send):
     modules, points = links.shape
+    slab = 6 * modules
+    wide = jax.ShapeDtypeStruct((send.shape[0], 2 * slab), F32)
+    return call(
+        gap_map_kernel,
+        (jax.ShapeDtypeStruct((modules * 3 * points, slab), F32), wide, wide),
+        [VMEM] * 5,
+        (links.reshape(-1, 1), arms.transpose(0, 2, 1).reshape(-1, 3), inverse, stiff, send),
+        12 * (modules * points) ** 2 * 4, 16 * modules * 3 * points * slab,
+        [pltpu.VMEM((modules * points, 4), F32)],
+    )
+
+
+def plan(owned, lags, solve_inverse, rows, cols, lag_rows, reals):
+    modules = solve_inverse.shape[0]
     slab, block = modules * 6, lags.shape[1]
     capacity = 2 * modules // rows
     size = -(-capacity * 6 // 8) * 8
@@ -509,19 +581,11 @@
             jax.ShapeDtypeStruct((rows * size, slab), F32),
             jax.ShapeDtypeStruct((cols, slab, rows * size), F32),
             jax.ShapeDtypeStruct((slab, rows * size), F32),
-            jax.ShapeDtypeStruct((modules * 3 * points, slab), F32),
         ),
-        [SMEM] + [VMEM] * 4,
-        (
-            owned,
-            links.reshape(-1, 1),
-            arms.transpose(0, 2, 1).reshape(-1, 3),
-            lags,
-            solve_inverse.transpose(1, 0, 2),
-        ),
-        12 * (modules * points) ** 2 * 4, 4 * modules * 3 * points * rows * modules * 6,
+        [SMEM, VMEM, VMEM],
+        (owned, lags, solve_inverse.transpose(1, 0, 2)),
+        4 * rows * cols * size * slab * lag_rows, 16 * rows * lines * lanes,
         [
-            pltpu.VMEM((modules * points, 4), F32),
             pltpu.VMEM((cols, rows * size, slab), F32),
             pltpu.VMEM((slab, 6), F32),
             pltpu.VMEM((block, lag_rows), BF16),
@@ -560,20 +624,21 @@
     inverse, stiff = diagonals(solve_inverse, stiffness)
     predicted, load = prepare(x, v, a, excitation[0], stiff)
     pieces, bases = force_pieces(lags, arrived, bases, slab, cols)
-    riders, send, take, own_take, weights = plan(
-        after(owned, pieces[0]), links, arms, lags, solve_inverse, rows, cols, rows * slab, reals
+    riders, send, take, own_take = plan(
+        after(owned, pieces[0]), lags, solve_inverse, rows, cols, rows * slab, reals
     )
     parts = exchange(pieces, "col")
     x, v, a, messages = first_advance(parts, predicted, v, a, load, inverse, riders)
     arrived = exchange(messages, "row")
     predicted, load = prepare(x, v, a, excitation[1], stiff)
+    weights, early, late = gap_map(after(links, v), arms, inverse, stiff, send)
+    drifted = drift(predicted, v, a, excitation[2], early)
     pieces, _ = force_pieces(lags, arrived, bases, slab, cols)
     parts = exchange(pieces, "col")
     listed, pull = listed_parts(arrived, take, own_take, weights, slab, rows * slab)
-    settled, messages = last_advance(
-        parts, predicted, v, a, load, excitation[2], inverse, stiff, send, rows
-    )
+    v, a, rest, messages = last_advance(parts, v, a, load, inverse, drifted, late, rows)
     arrived = exchange(messages, "row")
+    settled = settled_velocity(predicted, v, a, excitation[2], rest, inverse, stiff)
     pieces = last_force(lags, listed, arrived, slab, cols)
     parts = exchange(pieces, "col")
     known = settled_gaps(arrived, own_take, weights)

time: 55.4 us -> 56.4 us (1.018)
  Pallas kernels: 9.61 us -> 12.2 us
  waiting for transfers between devices: 19.5 us -> 17.5 us
    pallas_call x12 -> x15, Pallas kernels: 8.38 us -> 11 us  [call(): pl.pallas_call(body, out_shape=shapes, in_specs=in_specs, out_specs=jax.t...]
    ppermute x18, waiting for transfers between devices: 19.5 us -> 17.5 us  [exchange(): lax.ppermute(pieces[d], axis, [(i, sends_to(i, d, n)) for i in range(n)])]
  transfers between devices with their start and end apart: 18 -> 18, of which waited for: 14 -> 10; matrix products, arithmetic and copies ran while one was open for 0% -> 0% of each run, Pallas kernels for 12% -> 17%
where the time goes in v4:
time: 56.4 us; the launch traced here: 56.2 us
  starting transfers between devices  25.3 us (45%)
  waiting for transfers between devices  17.5 us (31%)
  Pallas kernels  12.2 us (22%)
  between operations  0.91 us (2%)
    ppermute x18, starting transfers between devices, exchange(): lax.ppermute(pieces[d], axis, [(i, sends_to(i, d, n)) for i in range(n)])  25.3 us
    ppermute x18, waiting for transfers between devices, exchange(): lax.ppermute(pieces[d], axis, [(i, sends_to(i, d, n)) for i in range(n)])  17.5 us
    pallas_call x15, Pallas kernels, call(): pl.pallas_call(body, out_shape=shapes, in_specs=in_specs, out_specs=jax.t...  11 us
    pallas_call x1, Pallas kernels, end(): pl.pallas_call(functools.partial(end_kernel, len(parts), pieces), out_sha...  1.22 us
  transfers between devices with their start and end apart: 18, of which 10 were waited for; matrix products, arithmetic and copies ran while one was open for 0% of the time, Pallas kernels for 17%

profile of v4, /device:TPU:0, one launch (start us, length us, event | category | flops | bytes accessed | tf_op | source)
XLA Modules:
  0.0 56.2 jit_solution(15654322008350342262)
XLA Ops:
  0.6 4.0 %collective-permute-start.2 = (f32[48,256]{1,0:T(8,128)}, f32[48,256]{1,0:T(8,128)S(1)}, u32[]{:S(2)}, u32[]{:S(2)}) collective-permute-start(f32[48,256]{1,0:T(8,128)} %refs_5_.1), channel_id=1, source_target_pairs={{0,24},{8,16},{16,8},{24,0},{1,25},{9,17},{17,9},{25,1},{2,26},{10... | collective-permute-start | bytes 147464 | tf_op jit(solution)/shard_map/ppermute | solution.py:32
  5.3 5.1 %shard_map.122 = (bf16[576,192]{1,0:T(8,128)(2,1)S(1)}, f32[192,256]{1,0:T(8,128)S(1)}, f32[192,256]{1,0:T(8,128)S(1)}, f32[192,256]{1,0:T(8,128)S(1)}) custom-call(bf16[3072,192]{1,0:T(8,128)(2,1)} %bitcast.20, bf16[2880,256]{1,0:T(8,128)(2,1)} %bitcast.21), custom_call_target="tpu_custom_call" | custom-call | flops 905969664 | bytes 2654208 | tf_op jit(solution)/shard_map/pallas_call | solution.py:58
  10.8 2.0 %collective-permute-start.3 = (f32[48,256]{1,0:T(8,128)S(1)}, f32[48,256]{1,0:T(8,128)S(1)}, u32[]{:S(2)}, u32[]{:S(2)}) collective-permute-start(f32[48,256]{1,0:T(8,128)S(1)} %get-tuple-element.61), channel_id=1, source_target_pairs={{0,2},{2,0},{4,6},{6,4},{1,3},{3,1},{5,7},{7,5},{8,10},{10,8},{12,... | collective-permute-start | bytes 147464 | tf_op jit(solution)/shard_map/ppermute | solution.py:32
  12.8 2.6 %collective-permute-start.4 = (f32[48,256]{1,0:T(8,128)S(1)}, f32[48,256]{1,0:T(8,128)S(1)}, u32[]{:S(2)}, u32[]{:S(2)}) collective-permute-start(f32[48,256]{1,0:T(8,128)S(1)} %get-tuple-element.62), channel_id=1, source_target_pairs={{0,4},{2,6},{4,0},{6,2},{1,5},{3,7},{5,1},{7,3},{8,12},{10,14},{12... | collective-permute-start | bytes 147464 | tf_op jit(solution)/shard_map/ppermute | solution.py:32
  15.8 1.4 %shard_map.126 = (bf16[96,256]{1,0:T(8,128)(2,1)S(1)}, bf16[96,256]{1,0:T(8,128)(2,1)S(1)}, bf16[96,256]{1,0:T(8,128)(2,1)S(1)}, bf16[96,256]{1,0:T(8,128)(2,1)S...) custom-call(s32[128]{0:T(128)S(1)} %copy-done.5, ...), custom_call_target="tpu_custom_call" | custom-call | flops 14155776 | bytes 1572864 | tf_op jit(solution)/shard_map/pallas_call | solution.py:58
  17.2 1.7 %collective-permute-done.4.refs_2_ = f32[48,256]{1,0:T(8,128)S(1)} collective-permute-done((f32[48,256]{1,0:T(8,128)S(1)}, f32[48,256]{1,0:T(8,128)S(1)}, u32[]{:S(2)}, u32[]{:S(2)}) %collective-permute-start.4) | collective-permute-done | bytes 49184 | tf_op jit(solution)/shard_map/ppermute | solution.py:32
  18.9 2.4 %collective-permute-done.5.refs_3_ = f32[48,256]{1,0:T(8,128)S(1)} collective-permute-done((f32[48,256]{1,0:T(8,128)S(1)}, f32[48,256]{1,0:T(8,128)S(1)}, u32[]{:S(2)}, u32[]{:S(2)}) %collective-permute-start.5) | collective-permute-done | bytes 49184 | tf_op jit(solution)/shard_map/ppermute | solution.py:32
  21.5 1.6 %collective-permute-start.6 = (bf16[144,256]{1,0:T(8,128)(2,1)S(1)}, bf16[144,256]{1,0:T(8,128)(2,1)S(1)}, u32[]{:S(2)}, u32[]{:S(2)}) collective-permute-start(bf16[144,256]{1,0:T(8,128)(2,1)S(1)} %get-tuple-element.74), channel_id=1, source_target_pairs={{0,8},{8,0},{16,24},{24,16},{1,9},{9,1},{17,25},{25,17},{2,10},{10... | collective-permute-start | bytes 221192 | tf_op jit(solution)/shard_map/ppermute | solution.py:32
  23.0 1.5 %collective-permute-start.7 = (bf16[144,256]{1,0:T(8,128)(2,1)S(1)}, bf16[144,256]{1,0:T(8,128)(2,1)S(1)}, u32[]{:S(2)}, u32[]{:S(2)}) collective-permute-start(bf16[144,256]{1,0:T(8,128)(2,1)S(1)} %get-tuple-element.75), channel_id=1, source_target_pairs={{0,16},{8,24},{16,0},{24,8},{1,17},{9,25},{17,1},{25,9},{2,18},{10... | collective-permute-start | bytes 221192 | tf_op jit(solution)/shard_map/ppermute | solution.py:32
  25.0 0.9 %collective-permute-done.6.refs_1_.refs_2_ = bf16[144,256]{1,0:T(8,128)(2,1)S(1)} collective-permute-done((bf16[144,256]{1,0:T(8,128)(2,1)S(1)}, bf16[144,256]{1,0:T(8,128)(2,1)S(1)}, u32[]{:S(2)}, u32[]{:S(2)}) %collective-permute-start.6) | collective-permute-done | bytes 73760 | tf_op jit(solution)/shard_map/ppermute | solution.py:32
  25.9 1.5 %collective-permute-done.7.refs_2_.refs_3_ = bf16[144,256]{1,0:T(8,128)(2,1)S(1)} collective-permute-done((bf16[144,256]{1,0:T(8,128)(2,1)S(1)}, bf16[144,256]{1,0:T(8,128)(2,1)S(1)}, u32[]{:S(2)}, u32[]{:S(2)}) %collective-permute-start.7) | collective-permute-done | bytes 73760 | tf_op jit(solution)/shard_map/ppermute | solution.py:32
  27.4 2.4 %collective-permute-done.8.refs_3_.refs_4_ = bf16[144,256]{1,0:T(8,128)(2,1)S(1)} collective-permute-done((bf16[144,256]{1,0:T(8,128)(2,1)S(1)}, bf16[144,256]{1,0:T(8,128)(2,1)S(1)}, u32[]{:S(2)}, u32[]{:S(2)}) %collective-permute-start.8) | collective-permute-done | bytes 73760 | tf_op jit(solution)/shard_map/ppermute | solution.py:32
  30.2 1.1 %collective-permute-start.10 = (f32[96,256]{1,0:T(8,128)S(1)}, f32[96,256]{1,0:T(8,128)S(1)}, u32[]{:S(2)}, u32[]{:S(2)}) collective-permute-start(f32[96,256]{1,0:T(8,128)S(1)} %get-tuple-element.88), channel_id=1, source_target_pairs={{0,4},{2,6},{4,0},{6,2},{1,5},{3,7},{5,1},{7,3},{8,12},{10,14},{12... | collective-permute-start | bytes 294920 | tf_op jit(solution)/shard_map/ppermute | solution.py:32
  31.3 3.2 %collective-permute-start.11 = (f32[96,256]{1,0:T(8,128)S(1)}, f32[96,256]{1,0:T(8,128)S(1)}, u32[]{:S(2)}, u32[]{:S(2)}) collective-permute-start(f32[96,256]{1,0:T(8,128)S(1)} %get-tuple-element.89), channel_id=1, source_target_pairs={{0,6},{2,4},{4,2},{6,0},{1,7},{3,5},{5,3},{7,1},{8,14},{10,12},{12... | collective-permute-start | bytes 294920 | tf_op jit(solution)/shard_map/ppermute | solution.py:32
  35.8 2.5 %collective-permute-done.11.refs_3_ = f32[96,256]{1,0:T(8,128)S(1)} collective-permute-done((f32[96,256]{1,0:T(8,128)S(1)}, f32[96,256]{1,0:T(8,128)S(1)}, u32[]{:S(2)}, u32[]{:S(2)}) %collective-permute-start.11) | collective-permute-done | bytes 98336 | tf_op jit(solution)/shard_map/ppermute | solution.py:32
  39.7 2.4 %collective-permute-start.14 = (bf16[120,256]{1,0:T(8,128)(2,1)S(1)}, bf16[120,256]{1,0:T(8,128)(2,1)S(1)}, u32[]{:S(2)}, u32[]{:S(2)}) collective-permute-start(bf16[120,256]{1,0:T(8,128)(2,1)S(1)} %get-tuple-element.99), channel_id=1, source_target_pairs={{0,24},{8,16},{16,8},{24,0},{1,25},{9,17},{17,9},{25,1},{2,26},{10... | collective-permute-start | bytes 184328 | tf_op jit(solution)/shard_map/ppermute | solution.py:32
  42.2 0.8 %shard_map.129 = (bf16[192,192]{1,0:T(8,128)(2,1)S(1)}, f32[384,48]{1,0:T(8,128)S(1)}) custom-call(bf16[144,256]{1,0:T(8,128)(2,1)S(1)} %get-tuple-element.73.refs_0_.refs_1_, bf16[144,256]{1,0:T(8,128)(2,1)S(1)} %collective-permute-done.6.refs_1_.refs_2_, bf16[144,256]{1,0:T(8,128)(2,1)S(1)} %collective-permute-done.7.refs_2_.refs_3_, ...), custom_call_target="tpu_custom_call" | custom-call | flops 14155776 | bytes 73728 | tf_op jit(solution)/shard_map/pallas_call | solution.py:58
  43.4 1.4 %collective-permute-done.14.refs_5_.refs_3_ = bf16[120,256]{1,0:T(8,128)(2,1)S(1)} collective-permute-done((bf16[120,256]{1,0:T(8,128)(2,1)S(1)}, bf16[120,256]{1,0:T(8,128)(2,1)S(1)}, u32[]{:S(2)}, u32[]{:S(2)}) %collective-permute-start.14) | collective-permute-done | bytes 61472 | tf_op jit(solution)/shard_map/ppermute | solution.py:32
  45.1 1.3 %collective-permute-start.15 = (f32[96,256]{1,0:T(8,128)S(1)}, f32[96,256]{1,0:T(8,128)S(1)}, u32[]{:S(2)}, u32[]{:S(2)}) collective-permute-start(f32[96,256]{1,0:T(8,128)S(1)} %get-tuple-element.101), channel_id=1, source_target_pairs={{0,2},{2,0},{4,6},{6,4},{1,3},{3,1},{5,7},{7,5},{8,10},{10,8},{12,... | collective-permute-start | bytes 294920 | tf_op jit(solution)/shard_map/ppermute | solution.py:32
  46.4 2.0 %collective-permute-start.16 = (f32[96,256]{1,0:T(8,128)S(1)}, f32[96,256]{1,0:T(8,128)S(1)}, u32[]{:S(2)}, u32[]{:S(2)}) collective-permute-start(f32[96,256]{1,0:T(8,128)S(1)} %get-tuple-element.102), channel_id=1, source_target_pairs={{0,4},{2,6},{4,0},{6,2},{1,5},{3,7},{5,1},{7,3},{8,12},{10,14},{12... | collective-permute-start | bytes 294920 | tf_op jit(solution)/shard_map/ppermute | solution.py:32
  48.4 1.1 %collective-permute-start.17 = (f32[96,256]{1,0:T(8,128)S(1)}, f32[96,256]{1,0:T(8,128)S(1)}, u32[]{:S(2)}, u32[]{:S(2)}) collective-permute-start(f32[96,256]{1,0:T(8,128)S(1)} %get-tuple-element.103), channel_id=1, source_target_pairs={{0,6},{2,4},{4,2},{6,0},{1,7},{3,5},{5,3},{7,1},{8,14},{10,12},{12... | collective-permute-start | bytes 294920 | tf_op jit(solution)/shard_map/ppermute | solution.py:32
  50.7 2.3 %collective-permute-done.16.refs_2_ = f32[96,256]{1,0:T(8,128)S(1)} collective-permute-done((f32[96,256]{1,0:T(8,128)S(1)}, f32[96,256]{1,0:T(8,128)S(1)}, u32[]{:S(2)}, u32[]{:S(2)}) %collective-permute-start.16) | collective-permute-done | bytes 98336 | tf_op jit(solution)/shard_map/ppermute | solution.py:32
  53.0 2.0 %collective-permute-done.17.refs_3_ = f32[96,256]{1,0:T(8,128)S(1)} collective-permute-done((f32[96,256]{1,0:T(8,128)S(1)}, f32[96,256]{1,0:T(8,128)S(1)}, u32[]{:S(2)}, u32[]{:S(2)}) %collective-permute-start.17) | collective-permute-done | bytes 98336 | tf_op jit(solution)/shard_map/ppermute | solution.py:32
  54.9 1.2 %shard_map.137 = (f32[48,256]{1,0:T(8,128)}, f32[384,256]{1,0:T(8,128)}) custom-call(f32[96,256]{1,0:T(8,128)S(1)} %get-tuple-element.100.refs_0_, f32[96,256]{1,0:T(8,128)S(1)} %collective-permute-done.15.refs_1_, f32[96,256]{1,0:T(8,128)S(1)} %collective-permute-done.16.refs_2_, f32[96,256]{1,0:T(8,128)S(1)} %collective-permute-done.17.refs_3_, ...), custom_call_target="tpu_custom_call" | custom-call | flops 56623104 | bytes 786432 | tf_op jit(solution)/shard_map/pallas_call | solution.py:434
  (49 shorter events, 6.9 us)
Async XLA Ops:
  0.6 9.8 %collective-permute-start.2 = (f32[48,256]{1,0:T(8,128)}, f32[48,256]{1,0:T(8,128)S(1)}, u32[]{:S(2)}, u32[]{:S(2)}) collective-permute-start(f32[48,256]{1,0:T(8,128)} %refs_5_.1), channel_id=1, source_target_pairs={{0,24},{8,16},{16,8},{24,0},{1,25},{9,17},{17,9},{25,1},{2,26},{10... | collective-permute-start | bytes 147464 | tf_op jit(solution)/shard_map/ppermute | solution.py:32
  4.6 5.8 %collective-permute-start.1 = (f32[48,256]{1,0:T(8,128)}, f32[48,256]{1,0:T(8,128)S(1)}, u32[]{:S(2)}, u32[]{:S(2)}) collective-permute-start(f32[48,256]{1,0:T(8,128)} %refs_5_.1), channel_id=1, source_target_pairs={{0,16},{8,24},{16,0},{24,8},{1,17},{9,25},{17,1},{25,9},{2,18},{10... | collective-permute-start | bytes 147464 | tf_op jit(solution)/shard_map/ppermute | solution.py:32
  5.1 5.3 %collective-permute-start = (f32[48,256]{1,0:T(8,128)}, f32[48,256]{1,0:T(8,128)S(1)}, u32[]{:S(2)}, u32[]{:S(2)}) collective-permute-start(f32[48,256]{1,0:T(8,128)} %refs_5_.1), channel_id=1, source_target_pairs={{0,8},{8,0},{16,24},{24,16},{1,9},{9,1},{17,25},{25,17},{2,10},{10... | collective-permute-start | bytes 147464 | tf_op jit(solution)/shard_map/ppermute | solution.py:32
  5.3 10.2 %copy-start.2 = (f32[8,6,6]{2,0,1:T(8,128)S(1)}, f32[8,6,6]{2,0,1:T(8,128)}, u32[]{:S(2)}) copy-start(f32[8,6,6]{2,0,1:T(8,128)} %param.17) | copy-start | bytes 3460
  5.3 10.2 %copy-start.4 = (f32[8,6,6]{2,0,1:T(8,128)S(1)}, f32[8,6,6]{2,0,1:T(8,128)}, u32[]{:S(2)}) copy-start(f32[8,6,6]{2,0,1:T(8,128)} %param.18) | copy-start | bytes 3460
  5.3 10.3 %copy-start.1 = (f32[48,256]{1,0:T(8,128)S(1)}, f32[48,256]{1,0:T(8,128)}, u32[]{:S(2)}) copy-start(f32[48,256]{1,0:T(8,128)} %refs_6_.1) | copy-start | bytes 147460
  5.3 10.3 %copy-start.3 = (f32[48,256]{1,0:T(8,128)S(1)}, f32[48,256]{1,0:T(8,128)}, u32[]{:S(2)}) copy-start(f32[48,256]{1,0:T(8,128)} %x.1) | copy-start | bytes 147460
  10.4 24.1 %copy-start.7 = (f32[8,3,16]{2,0,1:T(8,128)S(1)}, f32[8,3,16]{2,0,1:T(8,128)}, u32[]{:S(2)}) copy-start(f32[8,3,16]{2,0,1:T(8,128)} %param.21) | copy-start | bytes 4612
  10.8 23.9 %copy-start.8 = (s32[8,16]{1,0:T(8,128)S(1)}, s32[8,16]{1,0:T(8,128)}, u32[]{:S(2)}) copy-start(s32[8,16]{1,0:T(8,128)} %param.20) | copy-start | bytes 1540
  10.8 6.4 %collective-permute-start.3 = (f32[48,256]{1,0:T(8,128)S(1)}, f32[48,256]{1,0:T(8,128)S(1)}, u32[]{:S(2)}, u32[]{:S(2)}) collective-permute-start(f32[48,256]{1,0:T(8,128)S(1)} %get-tuple-element.61), channel_id=1, source_target_pairs={{0,2},{2,0},{4,6},{6,4},{1,3},{3,1},{5,7},{7,5},{8,10},{10,8},{12,... | collective-permute-start | bytes 147464 | tf_op jit(solution)/shard_map/ppermute | solution.py:32
  12.8 6.0 %collective-permute-start.4 = (f32[48,256]{1,0:T(8,128)S(1)}, f32[48,256]{1,0:T(8,128)S(1)}, u32[]{:S(2)}, u32[]{:S(2)}) collective-permute-start(f32[48,256]{1,0:T(8,128)S(1)} %get-tuple-element.62), channel_id=1, source_target_pairs={{0,4},{2,6},{4,0},{6,2},{1,5},{3,7},{5,1},{7,3},{8,12},{10,14},{12... | collective-permute-start | bytes 147464 | tf_op jit(solution)/shard_map/ppermute | solution.py:32
  15.4 5.9 %collective-permute-start.5 = (f32[48,256]{1,0:T(8,128)S(1)}, f32[48,256]{1,0:T(8,128)S(1)}, u32[]{:S(2)}, u32[]{:S(2)}) collective-permute-start(f32[48,256]{1,0:T(8,128)S(1)} %get-tuple-element.63), channel_id=1, source_target_pairs={{0,6},{2,4},{4,2},{6,0},{1,7},{3,5},{5,3},{7,1},{8,14},{10,12},{12... | collective-permute-start | bytes 147464 | tf_op jit(solution)/shard_map/ppermute | solution.py:32
  21.5 4.4 %collective-permute-start.6 = (bf16[144,256]{1,0:T(8,128)(2,1)S(1)}, bf16[144,256]{1,0:T(8,128)(2,1)S(1)}, u32[]{:S(2)}, u32[]{:S(2)}) collective-permute-start(bf16[144,256]{1,0:T(8,128)(2,1)S(1)} %get-tuple-element.74), channel_id=1, source_target_pairs={{0,8},{8,0},{16,24},{24,16},{1,9},{9,1},{17,25},{25,17},{2,10},{10... | collective-permute-start | bytes 221192 | tf_op jit(solution)/shard_map/ppermute | solution.py:32
  23.0 4.4 %collective-permute-start.7 = (bf16[144,256]{1,0:T(8,128)(2,1)S(1)}, bf16[144,256]{1,0:T(8,128)(2,1)S(1)}, u32[]{:S(2)}, u32[]{:S(2)}) collective-permute-start(bf16[144,256]{1,0:T(8,128)(2,1)S(1)} %get-tuple-element.75), channel_id=1, source_target_pairs={{0,16},{8,24},{16,0},{24,8},{1,17},{9,25},{17,1},{25,9},{2,18},{10... | collective-permute-start | bytes 221192 | tf_op jit(solution)/shard_map/ppermute | solution.py:32
  24.6 5.3 %collective-permute-start.8 = (bf16[144,256]{1,0:T(8,128)(2,1)S(1)}, bf16[144,256]{1,0:T(8,128)(2,1)S(1)}, u32[]{:S(2)}, u32[]{:S(2)}) collective-permute-start(bf16[144,256]{1,0:T(8,128)(2,1)S(1)} %get-tuple-element.76), channel_id=1, source_target_pairs={{0,24},{8,16},{16,8},{24,0},{1,25},{9,17},{17,9},{25,1},{2,26},{10... | collective-permute-start | bytes 221192 | tf_op jit(solution)/shard_map/ppermute | solution.py:32
  30.1 5.7 %collective-permute-start.9 = (f32[96,256]{1,0:T(8,128)S(1)}, f32[96,256]{1,0:T(8,128)S(1)}, u32[]{:S(2)}, u32[]{:S(2)}) collective-permute-start(f32[96,256]{1,0:T(8,128)S(1)} %get-tuple-element.87), channel_id=1, source_target_pairs={{0,2},{2,0},{4,6},{6,4},{1,3},{3,1},{5,7},{7,5},{8,10},{10,8},{12,... | collective-permute-start | bytes 294920 | tf_op jit(solution)/shard_map/ppermute | solution.py:32
  30.2 5.7 %collective-permute-start.10 = (f32[96,256]{1,0:T(8,128)S(1)}, f32[96,256]{1,0:T(8,128)S(1)}, u32[]{:S(2)}, u32[]{:S(2)}) collective-permute-start(f32[96,256]{1,0:T(8,128)S(1)} %get-tuple-element.88), channel_id=1, source_target_pairs={{0,4},{2,6},{4,0},{6,2},{1,5},{3,7},{5,1},{7,3},{8,12},{10,14},{12... | collective-permute-start | bytes 294920 | tf_op jit(solution)/shard_map/ppermute | solution.py:32
  31.3 7.0 %collective-permute-start.11 = (f32[96,256]{1,0:T(8,128)S(1)}, f32[96,256]{1,0:T(8,128)S(1)}, u32[]{:S(2)}, u32[]{:S(2)}) collective-permute-start(f32[96,256]{1,0:T(8,128)S(1)} %get-tuple-element.89), channel_id=1, source_target_pairs={{0,6},{2,4},{4,2},{6,0},{1,7},{3,5},{5,3},{7,1},{8,14},{10,12},{12... | collective-permute-start | bytes 294920 | tf_op jit(solution)/shard_map/ppermute | solution.py:32
  38.6 4.4 %collective-permute-start.12 = (bf16[120,256]{1,0:T(8,128)(2,1)S(1)}, bf16[120,256]{1,0:T(8,128)(2,1)S(1)}, u32[]{:S(2)}, u32[]{:S(2)}) collective-permute-start(bf16[120,256]{1,0:T(8,128)(2,1)S(1)} %get-tuple-element.97), channel_id=1, source_target_pairs={{0,8},{8,0},{16,24},{24,16},{1,9},{9,1},{17,25},{25,17},{2,10},{10... | collective-permute-start | bytes 184328 | tf_op jit(solution)/shard_map/ppermute | solution.py:32
  39.2 4.2 %collective-permute-start.13 = (bf16[120,256]{1,0:T(8,128)(2,1)S(1)}, bf16[120,256]{1,0:T(8,128)(2,1)S(1)}, u32[]{:S(2)}, u32[]{:S(2)}) collective-permute-start(bf16[120,256]{1,0:T(8,128)(2,1)S(1)} %get-tuple-element.98), channel_id=1, source_target_pairs={{0,16},{8,24},{16,0},{24,8},{1,17},{9,25},{17,1},{25,9},{2,18},{10... | collective-permute-start | bytes 184328 | tf_op jit(solution)/shard_map/ppermute | solution.py:32
  39.7 5.1 %collective-permute-start.14 = (bf16[120,256]{1,0:T(8,128)(2,1)S(1)}, bf16[120,256]{1,0:T(8,128)(2,1)S(1)}, u32[]{:S(2)}, u32[]{:S(2)}) collective-permute-start(bf16[120,256]{1,0:T(8,128)(2,1)S(1)} %get-tuple-element.99), channel_id=1, source_target_pairs={{0,24},{8,16},{16,8},{24,0},{1,25},{9,17},{17,9},{25,1},{2,26},{10... | collective-permute-start | bytes 184328 | tf_op jit(solution)/shard_map/ppermute | solution.py:32
  45.1 5.6 %collective-permute-start.15 = (f32[96,256]{1,0:T(8,128)S(1)}, f32[96,256]{1,0:T(8,128)S(1)}, u32[]{:S(2)}, u32[]{:S(2)}) collective-permute-start(f32[96,256]{1,0:T(8,128)S(1)} %get-tuple-element.101), channel_id=1, source_target_pairs={{0,2},{2,0},{4,6},{6,4},{1,3},{3,1},{5,7},{7,5},{8,10},{10,8},{12,... | collective-permute-start | bytes 294920 | tf_op jit(solution)/shard_map/ppermute | solution.py:32
  46.4 6.6 %collective-permute-start.16 = (f32[96,256]{1,0:T(8,128)S(1)}, f32[96,256]{1,0:T(8,128)S(1)}, u32[]{:S(2)}, u32[]{:S(2)}) collective-permute-start(f32[96,256]{1,0:T(8,128)S(1)} %get-tuple-element.102), channel_id=1, source_target_pairs={{0,4},{2,6},{4,0},{6,2},{1,5},{3,7},{5,1},{7,3},{8,12},{10,14},{12... | collective-permute-start | bytes 294920 | tf_op jit(solution)/shard_map/ppermute | solution.py:32
  48.4 6.5 %collective-permute-start.17 = (f32[96,256]{1,0:T(8,128)S(1)}, f32[96,256]{1,0:T(8,128)S(1)}, u32[]{:S(2)}, u32[]{:S(2)}) collective-permute-start(f32[96,256]{1,0:T(8,128)S(1)} %get-tuple-element.103), channel_id=1, source_target_pairs={{0,6},{2,4},{4,2},{6,0},{1,7},{3,5},{5,3},{7,1},{8,14},{10,12},{12... | collective-permute-start | bytes 294920 | tf_op jit(solution)/shard_map/ppermute | solution.py:32
  (3 other events, 20.7 us)

commit v5 on v4

--- a/solution.py
+++ b/solution.py
@@ -68,111 +68,117 @@
     )(*args)
 
 
-def known_kernel(lag_rows, steps, per, k_hbm, h_hbm, lags_ref, *refs):
-    outs, (k_ref, h_ref, k_sem, h_sem) = refs[:steps], refs[steps:]
-    total, known = k_ref.shape[0], h_ref.shape[0]
-    size = per * lag_rows
-    count = -(-total // size)
+def known_kernel(lag_rows, pieces, k_hbm, h_hbm, k_ref, h_ref, out, k_sem, h_sem):
     copies = []
-    for i in range(count):
-        k_rows = pl.ds(i * size, min(size, total - i * size))
-        pair = [pltpu.make_async_copy(k_hbm.at[k_rows], k_ref.at[k_rows], k_sem.at[i])]
-        if i * size < known:
-            h_rows = pl.ds(i * size, min(size, known - i * size))
-            pair.append(pltpu.make_async_copy(h_hbm.at[h_rows], h_ref.at[h_rows], h_sem.at[i]))
-        copies.append(pair)
-    for i in range(min(2, count)):
-        for copy in copies[i]:
-            copy.start()
-    for i in range(count):
-        for copy in copies[i]:
-            copy.wait()
-        if i + 2 < count:
-            for copy in copies[i + 2]:
-                copy.start()
-        last = min((i + 1) * size, total)
-        turned = k_ref[i * size : last, :].T if i * size >= steps * lag_rows else None
-        for s in range(steps):
-            shift = (s + 1) * lag_rows
-            first = max(i * size, shift)
-            if first >= last:
-                outs[s][...] = jnp.zeros_like(outs[s])
-                continue
-            rows = h_ref[first - shift : last - shift, :]
-            if turned is None:
-                term = dot_rows(k_ref[first:last, :], rows)
-            else:
-                term = jnp.dot(turned, rows, preferred_element_type=F32)
-            outs[s][...] = term if i == 0 else outs[s][...] + term
-    lags_ref[...] = k_ref[: steps * lag_rows, :]
-
-
-def known_forces(kernel_flat, history_flat, lag_rows, steps):
-    block = kernel_flat.shape[1]
-    shape = jax.ShapeDtypeStruct((block, history_flat.shape[1]), F32)
-    per = 2
-    count = -(-kernel_flat.shape[0] // (per * lag_rows))
-    out = call(
-        functools.partial(known_kernel, lag_rows, steps, per),
-        (jax.ShapeDtypeStruct((steps * lag_rows, block), BF16),) + (shape,) * steps,
+    for far, near, sems in ((k_hbm, k_ref, k_sem), (h_hbm, h_ref, h_sem)):
+        size = far.shape[0] // pieces
+        for i in range(pieces):
+            at = pl.ds(i * size, size)
+            copies.append(pltpu.make_async_copy(far.at[at], near.at[at], sems.at[i]))
+            copies[-1].start()
+    for copy in copies:
+        copy.wait()
+    total = k_ref.shape[0]
+    out[...] = dot_rows(k_ref[lag_rows:, :], h_ref[: total - lag_rows, :])
+
+
+def known_force(kernel_flat, history_flat, lag_rows):
+    shapes = (
+        jax.ShapeDtypeStruct(kernel_flat.shape, BF16),
+        jax.ShapeDtypeStruct(history_flat.shape, BF16),
+        jax.ShapeDtypeStruct((kernel_flat.shape[1], history_flat.shape[1]), F32),
+    )
+    pieces = 2 if kernel_flat.shape[0] % 32 == 0 and history_flat.shape[0] % 32 == 0 else 1
+    return call(
+        functools.partial(known_kernel, lag_rows, pieces),
+        shapes,
         [pl.BlockSpec(memory_space=pltpu.MemorySpace.HBM)] * 2,
         tuple(
             pltpu.with_memory_space_constraint(t, pltpu.MemorySpace.HBM)
             for t in (kernel_flat, history_flat)
         ),
-        2 * steps * kernel_flat.size * history_flat.shape[1],
+        2 * kernel_flat.size * history_flat.shape[1],
         2 * (kernel_flat.size + history_flat.size),
-        [
-            pltpu.VMEM(kernel_flat.shape, BF16),
-            pltpu.VMEM(history_flat.shape, BF16),
-            pltpu.SemaphoreType.DMA((count,)),
-            pltpu.SemaphoreType.DMA((count,)),
-        ],
-    )
-    return out[0], out[1:]
-
-
-def force_kernel(cols, ahead, keep, *refs):
-    lags = refs[0]
-    arrived, refs = refs[1 : 1 + keep], refs[1 + keep :]
-    bases, outs = refs[:ahead], refs[ahead:-2]
-    chunks, later = outs[:cols], outs[cols:]
-    whole, total = refs[-2:]
-    rows = keep
-    slab, reals = chunks[0].shape[0] // (2 if ahead == 2 else 1), chunks[0].shape[1]
-    row, col = lax.axis_index("row"), lax.axis_index("col")
+        [pltpu.SemaphoreType.DMA((pieces,)), pltpu.SemaphoreType.DMA((pieces,))],
+    )
+
+
+def later_kernel(k_ref, h_ref, newest, *outs):
+    total, lag_rows = k_ref.shape[0], newest.shape[0]
+    for n, out in enumerate(outs):
+        first = (n + 1) * lag_rows
+        out[...] = dot_rows(k_ref[first : first + lag_rows, :], newest[...]) + dot_rows(
+            k_ref[first + lag_rows :, :], h_ref[: total - first - lag_rows, :]
+        )
+
+
+def later_forces(k, h, newest, count):
+    shape = jax.ShapeDtypeStruct((k.shape[1], h.shape[1]), F32)
+    return call(
+        later_kernel, (shape,) * count, [VMEM] * 3, (k, h, newest),
+        2 * count * k.size * h.shape[1], 2 * (k.size + h.size),
+    )
+
+
+def gather_newest(arrived, whole, slab, reals):
+    row, rows = lax.axis_index("row"), len(arrived)
     for d in range(rows):
         start = pl.multiple_of(comes_from(row, d, rows) * slab, 16)
         whole[pl.ds(start, slab), :] = arrived[d][0:slab, 0:reals].astype(BF16)
+
+
+def first_force_kernel(cols, rows, *refs):
+    k_ref, arrived, base = refs[0], refs[1 : 1 + rows], refs[1 + rows]
+    chunks, (whole, total) = refs[2 + rows : -2], refs[-2:]
+    slab, reals = chunks[0].shape
+    gather_newest(arrived, whole, slab, reals)
+    total[...] = base[...] + dot_rows(k_ref[0 : rows * slab, :], whole[...])
+    col = lax.axis_index("col")
+    for d in range(cols):
+        start = pl.multiple_of(sends_to(col, d, cols) * slab, 8)
+        chunks[d][...] = total[pl.ds(start, slab), :]
+
+
+def first_force(k, arrived, base, slab, cols):
+    rows, (block, reals) = len(arrived), base.shape
+    out = call(
+        functools.partial(first_force_kernel, cols, rows),
+        (jax.ShapeDtypeStruct((slab, reals), F32),) * cols
+        + (jax.ShapeDtypeStruct((rows * slab, reals), BF16),),
+        [VMEM] * (2 + rows),
+        (k, *arrived, base),
+        2 * rows * slab * block * reals, 8 * block * reals,
+        [pltpu.VMEM((block, reals), F32)],
+    )
+    return out[:cols], out[cols]
+
+
+def force_kernel(cols, rows, *refs):
+    lags, arrived, bases = refs[0], refs[1 : 1 + rows], refs[1 + rows : 3 + rows]
+    chunks, (whole, total) = refs[3 + rows : -2], refs[-2:]
+    slab, reals = chunks[0].shape[0] // 2, chunks[0].shape[1]
+    gather_newest(arrived, whole, slab, reals)
     lag_rows = rows * slab
-    for n in range(ahead):
-        value = bases[n][...] + dot_rows(lags[n * lag_rows : (n + 1) * lag_rows, :], whole[...])
-        if n == 0 or ahead == 2:
-            total[...] = value
-            for d in range(cols):
-                start = pl.multiple_of(sends_to(col, d, cols) * slab, 8)
-                chunks[d][n * slab : (n + 1) * slab, :] = total[pl.ds(start, slab), :]
-        else:
-            later[n - 1][...] = value
+    col = lax.axis_index("col")
+    for n in range(2):
+        total[n] = bases[n][...] + dot_rows(
+            lags[n * lag_rows : (n + 1) * lag_rows, :], whole[...]
+        )
+        for d in range(cols):
+            start = pl.multiple_of(sends_to(col, d, cols) * slab, 8)
+            chunks[d][n * slab : (n + 1) * slab, :] = total[n, pl.ds(start, slab), :]
 
 
 def force_pieces(lags, arrived, bases, slab, cols):
-    rows, ahead = len(arrived), len(bases)
-    block, reals = bases[0].shape
-    both = ahead == 2
-    shapes = (jax.ShapeDtypeStruct((slab * (2 if both else 1), reals), F32),) * cols
-    if not both:
-        shapes += (jax.ShapeDtypeStruct((block, reals), F32),) * (ahead - 1)
-    out = call(
-        functools.partial(force_kernel, cols, ahead, rows),
-        shapes,
-        [VMEM] * (1 + rows + ahead),
+    rows, (block, reals) = len(arrived), bases[0].shape
+    return call(
+        functools.partial(force_kernel, cols, rows),
+        (jax.ShapeDtypeStruct((2 * slab, reals), F32),) * cols,
+        [VMEM] * (3 + rows),
         (lags, *arrived, *bases),
-        2 * ahead * rows * slab * block * reals,
-        4 * 2 * ahead * block * reals,
-        [pltpu.VMEM((rows * slab, reals), BF16), pltpu.VMEM((block, reals), F32)],
-    )
-    return out[:cols], out[cols:]
+        4 * rows * slab * block * reals, 16 * block * reals,
+        [pltpu.VMEM((rows * slab, reals), BF16), pltpu.VMEM((2, block, reals), F32)],
+    )
 
 
 def prepare_kernel(x, v, a, e, stiff, predicted, load):
@@ -618,12 +624,12 @@
     modules, points = links.shape
     x, v, a = displacement, velocity, acceleration
     arrived = exchange([v] * rows, "row")
-    lags, bases = known_forces(
-        kernel.reshape(-1, kernel.shape[3]), history.reshape(-1, reals), rows * slab, steps
+    lags, past, base = known_force(
+        kernel.reshape(-1, kernel.shape[3]), history.reshape(-1, reals), rows * slab
     )
     inverse, stiff = diagonals(solve_inverse, stiffness)
     predicted, load = prepare(x, v, a, excitation[0], stiff)
-    pieces, bases = force_pieces(lags, arrived, bases, slab, cols)
+    pieces, newest = first_force(lags, arrived, base, slab, cols)
     riders, send, take, own_take = plan(
         after(owned, pieces[0]), lags, solve_inverse, rows, cols, rows * slab, reals
     )
@@ -633,7 +639,8 @@
     predicted, load = prepare(x, v, a, excitation[1], stiff)
     weights, early, late = gap_map(after(links, v), arms, inverse, stiff, send)
     drifted = drift(predicted, v, a, excitation[2], early)
-    pieces, _ = force_pieces(lags, arrived, bases, slab, cols)
+    bases = later_forces(lags, past, after(newest, v), steps - 1)
+    pieces = force_pieces(lags, arrived, bases, slab, cols)
     parts = exchange(pieces, "col")
     listed, pull = listed_parts(arrived, take, own_take, weights, slab, rows * slab)
     v, a, rest, messages = last_advance(parts, v, a, load, inverse, drifted, late, rows)

time: 56.4 us -> 54.8 us (0.972)
  Pallas kernels: 12.2 us -> 10.6 us
    pallas_call x15 -> x16, Pallas kernels: 11 us -> 9.42 us  [call(): pl.pallas_call(body, out_shape=shapes, in_specs=in_specs, out_specs=jax.t...]
  transfers between devices with their start and end apart: 18 -> 18, of which waited for: 10 -> 11; matrix products, arithmetic and copies ran while one was open for 0% -> 0% of each run, Pallas kernels for 17% -> 15%
where the time goes in v5:
time: 54.8 us; the launch traced here: 54.7 us
  starting transfers between devices  25.1 us (46%)
  waiting for transfers between devices  17.8 us (32%)
  Pallas kernels  10.6 us (19%)
  between operations  0.93 us (2%)
    ppermute x18, starting transfers between devices, exchange(): lax.ppermute(pieces[d], axis, [(i, sends_to(i, d, n)) for i in range(n)])  25.1 us
    ppermute x18, waiting for transfers between devices, exchange(): lax.ppermute(pieces[d], axis, [(i, sends_to(i, d, n)) for i in range(n)])  17.8 us
    pallas_call x16, Pallas kernels, call(): pl.pallas_call(body, out_shape=shapes, in_specs=in_specs, out_specs=jax.t...  9.42 us
    pallas_call x1, Pallas kernels, end(): pl.pallas_call(functools.partial(end_kernel, len(parts), pieces), out_sha...  1.22 us
  transfers between devices with their start and end apart: 18, of which 11 were waited for; matrix products, arithmetic and copies ran while one was open for 0% of the time, Pallas kernels for 15%

profile of v5, /device:TPU:0, one launch (start us, length us, event | category | flops | bytes accessed | tf_op | source)
XLA Modules:
  0.0 54.7 jit_solution(11098687150578130881)
XLA Ops:
  0.6 4.0 %collective-permute-start.2 = (f32[48,256]{1,0:T(8,128)}, f32[48,256]{1,0:T(8,128)S(1)}, u32[]{:S(2)}, u32[]{:S(2)}) collective-permute-start(f32[48,256]{1,0:T(8,128)} %refs_5_.1), channel_id=1, source_target_pairs={{0,24},{8,16},{16,8},{24,0},{1,25},{9,17},{17,9},{25,1},{2,26},{10... | collective-permute-start | bytes 147464 | tf_op jit(solution)/shard_map/ppermute | solution.py:32
  5.3 2.5 %shard_map.122 = (bf16[3072,192]{1,0:T(8,128)(2,1)S(1)}, bf16[2880,256]{1,0:T(8,128)(2,1)S(1)}, f32[192,256]{1,0:T(8,128)S(1)}) custom-call(bf16[3072,192]{1,0:T(8,128)(2,1)} %bitcast.19, bf16[2880,256]{1,0:T(8,128)(2,1)} %bitcast.20), custom_call_target="tpu_custom_call" | custom-call | flops 301989888 | bytes 2654208 | tf_op jit(solution)/shard_map/pallas_call | solution.py:58
  7.9 1.1 %collective-permute-done.1.refs_3_ = f32[48,256]{1,0:T(8,128)S(1)} collective-permute-done((f32[48,256]{1,0:T(8,128)}, f32[48,256]{1,0:T(8,128)S(1)}, u32[]{:S(2)}, u32[]{:S(2)}) %collective-permute-start.1) | collective-permute-done | bytes 49184 | tf_op jit(solution)/shard_map/ppermute | solution.py:32
  9.7 1.6 %collective-permute-start.3 = (f32[48,256]{1,0:T(8,128)S(1)}, f32[48,256]{1,0:T(8,128)S(1)}, u32[]{:S(2)}, u32[]{:S(2)}) collective-permute-start(f32[48,256]{1,0:T(8,128)S(1)} %get-tuple-element.60), channel_id=1, source_target_pairs={{0,2},{2,0},{4,6},{6,4},{1,3},{3,1},{5,7},{7,5},{8,10},{10,8},{12,... | collective-permute-start | bytes 147464 | tf_op jit(solution)/shard_map/ppermute | solution.py:32
  11.3 2.6 %collective-permute-start.4 = (f32[48,256]{1,0:T(8,128)S(1)}, f32[48,256]{1,0:T(8,128)S(1)}, u32[]{:S(2)}, u32[]{:S(2)}) collective-permute-start(f32[48,256]{1,0:T(8,128)S(1)} %get-tuple-element.61), channel_id=1, source_target_pairs={{0,4},{2,6},{4,0},{6,2},{1,5},{3,7},{5,1},{7,3},{8,12},{10,14},{12... | collective-permute-start | bytes 147464 | tf_op jit(solution)/shard_map/ppermute | solution.py:32
  14.5 1.4 %shard_map.126 = (bf16[96,256]{1,0:T(8,128)(2,1)S(1)}, bf16[96,256]{1,0:T(8,128)(2,1)S(1)}, bf16[96,256]{1,0:T(8,128)(2,1)S(1)}, bf16[96,256]{1,0:T(8,128)(2,1)S...) custom-call(s32[128]{0:T(128)S(1)} %copy-done.5, ...), custom_call_target="tpu_custom_call" | custom-call | flops 14155776 | bytes 1572864 | tf_op jit(solution)/shard_map/pallas_call | solution.py:58
  15.9 1.4 %collective-permute-done.4.refs_2_ = f32[48,256]{1,0:T(8,128)S(1)} collective-permute-done((f32[48,256]{1,0:T(8,128)S(1)}, f32[48,256]{1,0:T(8,128)S(1)}, u32[]{:S(2)}, u32[]{:S(2)}) %collective-permute-start.4) | collective-permute-done | bytes 49184 | tf_op jit(solution)/shard_map/ppermute | solution.py:32
  17.4 2.4 %collective-permute-done.5.refs_3_ = f32[48,256]{1,0:T(8,128)S(1)} collective-permute-done((f32[48,256]{1,0:T(8,128)S(1)}, f32[48,256]{1,0:T(8,128)S(1)}, u32[]{:S(2)}, u32[]{:S(2)}) %collective-permute-start.5) | collective-permute-done | bytes 49184 | tf_op jit(solution)/shard_map/ppermute | solution.py:32
  20.6 1.5 %collective-permute-start.7 = (bf16[144,256]{1,0:T(8,128)(2,1)S(1)}, bf16[144,256]{1,0:T(8,128)(2,1)S(1)}, u32[]{:S(2)}, u32[]{:S(2)}) collective-permute-start(bf16[144,256]{1,0:T(8,128)(2,1)S(1)} %get-tuple-element.74), channel_id=1, source_target_pairs={{0,16},{8,24},{16,0},{24,8},{1,17},{9,25},{17,1},{25,9},{2,18},{10... | collective-permute-start | bytes 221192 | tf_op jit(solution)/shard_map/ppermute | solution.py:32
  22.1 1.4 %collective-permute-start.8 = (bf16[144,256]{1,0:T(8,128)(2,1)S(1)}, bf16[144,256]{1,0:T(8,128)(2,1)S(1)}, u32[]{:S(2)}, u32[]{:S(2)}) collective-permute-start(bf16[144,256]{1,0:T(8,128)(2,1)S(1)} %get-tuple-element.75), channel_id=1, source_target_pairs={{0,24},{8,16},{16,8},{24,0},{1,25},{9,17},{17,9},{25,1},{2,26},{10... | collective-permute-start | bytes 221192 | tf_op jit(solution)/shard_map/ppermute | solution.py:32
  25.0 2.4 %collective-permute-done.8.refs_3_.refs_4_ = bf16[144,256]{1,0:T(8,128)(2,1)S(1)} collective-permute-done((bf16[144,256]{1,0:T(8,128)(2,1)S(1)}, bf16[144,256]{1,0:T(8,128)(2,1)S(1)}, u32[]{:S(2)}, u32[]{:S(2)}) %collective-permute-start.8) | collective-permute-done | bytes 73760 | tf_op jit(solution)/shard_map/ppermute | solution.py:32
  27.7 1.1 %collective-permute-start.10 = (f32[96,256]{1,0:T(8,128)S(1)}, f32[96,256]{1,0:T(8,128)S(1)}, u32[]{:S(2)}, u32[]{:S(2)}) collective-permute-start(f32[96,256]{1,0:T(8,128)S(1)} %get-tuple-element.90), channel_id=1, source_target_pairs={{0,4},{2,6},{4,0},{6,2},{1,5},{3,7},{5,1},{7,3},{8,12},{10,14},{12... | collective-permute-start | bytes 294920 | tf_op jit(solution)/shard_map/ppermute | solution.py:32
  28.9 3.2 %collective-permute-start.11 = (f32[96,256]{1,0:T(8,128)S(1)}, f32[96,256]{1,0:T(8,128)S(1)}, u32[]{:S(2)}, u32[]{:S(2)}) collective-permute-start(f32[96,256]{1,0:T(8,128)S(1)} %get-tuple-element.91), channel_id=1, source_target_pairs={{0,6},{2,4},{4,2},{6,0},{1,7},{3,5},{5,3},{7,1},{8,14},{10,12},{12... | collective-permute-start | bytes 294920 | tf_op jit(solution)/shard_map/ppermute | solution.py:32
  33.4 2.5 %collective-permute-done.11.refs_3_ = f32[96,256]{1,0:T(8,128)S(1)} collective-permute-done((f32[96,256]{1,0:T(8,128)S(1)}, f32[96,256]{1,0:T(8,128)S(1)}, u32[]{:S(2)}, u32[]{:S(2)}) %collective-permute-start.11) | collective-permute-done | bytes 98336 | tf_op jit(solution)/shard_map/ppermute | solution.py:32
  36.2 1.6 %collective-permute-start.12 = (bf16[120,256]{1,0:T(8,128)(2,1)S(1)}, bf16[120,256]{1,0:T(8,128)(2,1)S(1)}, u32[]{:S(2)}, u32[]{:S(2)}) collective-permute-start(bf16[120,256]{1,0:T(8,128)(2,1)S(1)} %get-tuple-element.99), channel_id=1, source_target_pairs={{0,8},{8,0},{16,24},{24,16},{1,9},{9,1},{17,25},{25,17},{2,10},{10... | collective-permute-start | bytes 184328 | tf_op jit(solution)/shard_map/ppermute | solution.py:32
  38.2 1.5 %collective-permute-start.14 = (bf16[120,256]{1,0:T(8,128)(2,1)S(1)}, bf16[120,256]{1,0:T(8,128)(2,1)S(1)}, u32[]{:S(2)}, u32[]{:S(2)}) collective-permute-start(bf16[120,256]{1,0:T(8,128)(2,1)S(1)} %get-tuple-element.101), channel_id=1, source_target_pairs={{0,24},{8,16},{16,8},{24,0},{1,25},{9,17},{17,9},{25,1},{2,26},{10... | collective-permute-start | bytes 184328 | tf_op jit(solution)/shard_map/ppermute | solution.py:32
  40.5 1.4 %collective-permute-done.13.refs_4_.refs_2_ = bf16[120,256]{1,0:T(8,128)(2,1)S(1)} collective-permute-done((bf16[120,256]{1,0:T(8,128)(2,1)S(1)}, bf16[120,256]{1,0:T(8,128)(2,1)S(1)}, u32[]{:S(2)}, u32[]{:S(2)}) %collective-permute-start.13) | collective-permute-done | bytes 61472 | tf_op jit(solution)/shard_map/ppermute | solution.py:32
  42.0 1.4 %collective-permute-done.14.refs_5_.refs_3_ = bf16[120,256]{1,0:T(8,128)(2,1)S(1)} collective-permute-done((bf16[120,256]{1,0:T(8,128)(2,1)S(1)}, bf16[120,256]{1,0:T(8,128)(2,1)S(1)}, u32[]{:S(2)}, u32[]{:S(2)}) %collective-permute-start.14) | collective-permute-done | bytes 61472 | tf_op jit(solution)/shard_map/ppermute | solution.py:32
  43.6 1.3 %collective-permute-start.15 = (f32[96,256]{1,0:T(8,128)S(1)}, f32[96,256]{1,0:T(8,128)S(1)}, u32[]{:S(2)}, u32[]{:S(2)}) collective-permute-start(f32[96,256]{1,0:T(8,128)S(1)} %get-tuple-element.103), channel_id=1, source_target_pairs={{0,2},{2,0},{4,6},{6,4},{1,3},{3,1},{5,7},{7,5},{8,10},{10,8},{12,... | collective-permute-start | bytes 294920 | tf_op jit(solution)/shard_map/ppermute | solution.py:32
  44.9 2.0 %collective-permute-start.16 = (f32[96,256]{1,0:T(8,128)S(1)}, f32[96,256]{1,0:T(8,128)S(1)}, u32[]{:S(2)}, u32[]{:S(2)}) collective-permute-start(f32[96,256]{1,0:T(8,128)S(1)} %get-tuple-element.104), channel_id=1, source_target_pairs={{0,4},{2,6},{4,0},{6,2},{1,5},{3,7},{5,1},{7,3},{8,12},{10,14},{12... | collective-permute-start | bytes 294920 | tf_op jit(solution)/shard_map/ppermute | solution.py:32
  46.9 1.1 %collective-permute-start.17 = (f32[96,256]{1,0:T(8,128)S(1)}, f32[96,256]{1,0:T(8,128)S(1)}, u32[]{:S(2)}, u32[]{:S(2)}) collective-permute-start(f32[96,256]{1,0:T(8,128)S(1)} %get-tuple-element.105), channel_id=1, source_target_pairs={{0,6},{2,4},{4,2},{6,0},{1,7},{3,5},{5,3},{7,1},{8,14},{10,12},{12... | collective-permute-start | bytes 294920 | tf_op jit(solution)/shard_map/ppermute | solution.py:32
  49.2 2.3 %collective-permute-done.16.refs_2_ = f32[96,256]{1,0:T(8,128)S(1)} collective-permute-done((f32[96,256]{1,0:T(8,128)S(1)}, f32[96,256]{1,0:T(8,128)S(1)}, u32[]{:S(2)}, u32[]{:S(2)}) %collective-permute-start.16) | collective-permute-done | bytes 98336 | tf_op jit(solution)/shard_map/ppermute | solution.py:32
  51.5 2.0 %collective-permute-done.17.refs_3_ = f32[96,256]{1,0:T(8,128)S(1)} collective-permute-done((f32[96,256]{1,0:T(8,128)S(1)}, f32[96,256]{1,0:T(8,128)S(1)}, u32[]{:S(2)}, u32[]{:S(2)}) %collective-permute-start.17) | collective-permute-done | bytes 98336 | tf_op jit(solution)/shard_map/ppermute | solution.py:32
  53.5 1.2 %shard_map.138 = (f32[48,256]{1,0:T(8,128)}, f32[384,256]{1,0:T(8,128)}) custom-call(f32[96,256]{1,0:T(8,128)S(1)} %get-tuple-element.102.refs_0_, f32[96,256]{1,0:T(8,128)S(1)} %collective-permute-done.15.refs_1_, f32[96,256]{1,0:T(8,128)S(1)} %collective-permute-done.16.refs_2_, f32[96,256]{1,0:T(8,128)S(1)} %collective-permute-done.17.refs_3_, ...), custom_call_target="tpu_custom_call" | custom-call | flops 56623104 | bytes 786432 | tf_op jit(solution)/shard_map/pallas_call | solution.py:440
  (50 shorter events, 8.7 us)
Async XLA Ops:
  0.6 8.8 %copy-start = (f32[48,256]{1,0:T(8,128)S(1)}, f32[48,256]{1,0:T(8,128)}, u32[]{:S(2)}) copy-start(f32[48,256]{1,0:T(8,128)} %refs_5_.1) | copy-start | bytes 147460
  0.6 7.2 %collective-permute-start.2 = (f32[48,256]{1,0:T(8,128)}, f32[48,256]{1,0:T(8,128)S(1)}, u32[]{:S(2)}, u32[]{:S(2)}) collective-permute-start(f32[48,256]{1,0:T(8,128)} %refs_5_.1), channel_id=1, source_target_pairs={{0,24},{8,16},{16,8},{24,0},{1,25},{9,17},{17,9},{25,1},{2,26},{10... | collective-permute-start | bytes 147464 | tf_op jit(solution)/shard_map/ppermute | solution.py:32
  4.6 4.3 %collective-permute-start.1 = (f32[48,256]{1,0:T(8,128)}, f32[48,256]{1,0:T(8,128)S(1)}, u32[]{:S(2)}, u32[]{:S(2)}) collective-permute-start(f32[48,256]{1,0:T(8,128)} %refs_5_.1), channel_id=1, source_target_pairs={{0,16},{8,24},{16,0},{24,8},{1,17},{9,25},{17,1},{25,9},{2,18},{10... | collective-permute-start | bytes 147464 | tf_op jit(solution)/shard_map/ppermute | solution.py:32
  5.1 4.3 %collective-permute-start = (f32[48,256]{1,0:T(8,128)}, f32[48,256]{1,0:T(8,128)S(1)}, u32[]{:S(2)}, u32[]{:S(2)}) collective-permute-start(f32[48,256]{1,0:T(8,128)} %refs_5_.1), channel_id=1, source_target_pairs={{0,8},{8,0},{16,24},{24,16},{1,9},{9,1},{17,25},{25,17},{2,10},{10... | collective-permute-start | bytes 147464 | tf_op jit(solution)/shard_map/ppermute | solution.py:32
  7.8 6.5 %copy-start.1 = (f32[48,256]{1,0:T(8,128)S(1)}, f32[48,256]{1,0:T(8,128)}, u32[]{:S(2)}) copy-start(f32[48,256]{1,0:T(8,128)} %refs_6_.1) | copy-start | bytes 147460
  7.8 6.5 %copy-start.3 = (f32[48,256]{1,0:T(8,128)S(1)}, f32[48,256]{1,0:T(8,128)}, u32[]{:S(2)}) copy-start(f32[48,256]{1,0:T(8,128)} %x.1) | copy-start | bytes 147460
  7.9 6.7 %copy-start.5 = (s32[128]{0:T(128)S(1)}, s32[128]{0:T(128)}, u32[]{:S(2)}) copy-start(s32[128]{0:T(128)} %refs_0_) | copy-start | bytes 1540
  9.7 6.2 %collective-permute-start.3 = (f32[48,256]{1,0:T(8,128)S(1)}, f32[48,256]{1,0:T(8,128)S(1)}, u32[]{:S(2)}, u32[]{:S(2)}) collective-permute-start(f32[48,256]{1,0:T(8,128)S(1)} %get-tuple-element.60), channel_id=1, source_target_pairs={{0,2},{2,0},{4,6},{6,4},{1,3},{3,1},{5,7},{7,5},{8,10},{10,8},{12,... | collective-permute-start | bytes 147464 | tf_op jit(solution)/shard_map/ppermute | solution.py:32
  11.3 6.0 %collective-permute-start.4 = (f32[48,256]{1,0:T(8,128)S(1)}, f32[48,256]{1,0:T(8,128)S(1)}, u32[]{:S(2)}, u32[]{:S(2)}) collective-permute-start(f32[48,256]{1,0:T(8,128)S(1)} %get-tuple-element.61), channel_id=1, source_target_pairs={{0,4},{2,6},{4,0},{6,2},{1,5},{3,7},{5,1},{7,3},{8,12},{10,14},{12... | collective-permute-start | bytes 147464 | tf_op jit(solution)/shard_map/ppermute | solution.py:32
  13.9 5.9 %collective-permute-start.5 = (f32[48,256]{1,0:T(8,128)S(1)}, f32[48,256]{1,0:T(8,128)S(1)}, u32[]{:S(2)}, u32[]{:S(2)}) collective-permute-start(f32[48,256]{1,0:T(8,128)S(1)} %get-tuple-element.62), channel_id=1, source_target_pairs={{0,6},{2,4},{4,2},{6,0},{1,7},{3,5},{5,3},{7,1},{8,14},{10,12},{12... | collective-permute-start | bytes 147464 | tf_op jit(solution)/shard_map/ppermute | solution.py:32
  20.0 4.6 %collective-permute-start.6 = (bf16[144,256]{1,0:T(8,128)(2,1)S(1)}, bf16[144,256]{1,0:T(8,128)(2,1)S(1)}, u32[]{:S(2)}, u32[]{:S(2)}) collective-permute-start(bf16[144,256]{1,0:T(8,128)(2,1)S(1)} %get-tuple-element.73), channel_id=1, source_target_pairs={{0,8},{8,0},{16,24},{24,16},{1,9},{9,1},{17,25},{25,17},{2,10},{10... | collective-permute-start | bytes 221192 | tf_op jit(solution)/shard_map/ppermute | solution.py:32
  20.6 4.4 %collective-permute-start.7 = (bf16[144,256]{1,0:T(8,128)(2,1)S(1)}, bf16[144,256]{1,0:T(8,128)(2,1)S(1)}, u32[]{:S(2)}, u32[]{:S(2)}) collective-permute-start(bf16[144,256]{1,0:T(8,128)(2,1)S(1)} %get-tuple-element.74), channel_id=1, source_target_pairs={{0,16},{8,24},{16,0},{24,8},{1,17},{9,25},{17,1},{25,9},{2,18},{10... | collective-permute-start | bytes 221192 | tf_op jit(solution)/shard_map/ppermute | solution.py:32
  22.1 5.3 %collective-permute-start.8 = (bf16[144,256]{1,0:T(8,128)(2,1)S(1)}, bf16[144,256]{1,0:T(8,128)(2,1)S(1)}, u32[]{:S(2)}, u32[]{:S(2)}) collective-permute-start(bf16[144,256]{1,0:T(8,128)(2,1)S(1)} %get-tuple-element.75), channel_id=1, source_target_pairs={{0,24},{8,16},{16,8},{24,0},{1,25},{9,17},{17,9},{25,1},{2,26},{10... | collective-permute-start | bytes 221192 | tf_op jit(solution)/shard_map/ppermute | solution.py:32
  24.6 7.5 %copy-start.7 = (f32[8,3,16]{2,0,1:T(8,128)S(1)}, f32[8,3,16]{2,0,1:T(8,128)}, u32[]{:S(2)}) copy-start(f32[8,3,16]{2,0,1:T(8,128)} %param.21) | copy-start | bytes 4612
  24.6 7.6 %copy-start.8 = (s32[8,16]{1,0:T(8,128)S(1)}, s32[8,16]{1,0:T(8,128)}, u32[]{:S(2)}) copy-start(s32[8,16]{1,0:T(8,128)} %param.20) | copy-start | bytes 1540
  27.7 5.7 %collective-permute-start.9 = (f32[96,256]{1,0:T(8,128)S(1)}, f32[96,256]{1,0:T(8,128)S(1)}, u32[]{:S(2)}, u32[]{:S(2)}) collective-permute-start(f32[96,256]{1,0:T(8,128)S(1)} %get-tuple-element.89), channel_id=1, source_target_pairs={{0,2},{2,0},{4,6},{6,4},{1,3},{3,1},{5,7},{7,5},{8,10},{10,8},{12,... | collective-permute-start | bytes 294920 | tf_op jit(solution)/shard_map/ppermute | solution.py:32
  27.7 5.7 %collective-permute-start.10 = (f32[96,256]{1,0:T(8,128)S(1)}, f32[96,256]{1,0:T(8,128)S(1)}, u32[]{:S(2)}, u32[]{:S(2)}) collective-permute-start(f32[96,256]{1,0:T(8,128)S(1)} %get-tuple-element.90), channel_id=1, source_target_pairs={{0,4},{2,6},{4,0},{6,2},{1,5},{3,7},{5,1},{7,3},{8,12},{10,14},{12... | collective-permute-start | bytes 294920 | tf_op jit(solution)/shard_map/ppermute | solution.py:32
  28.9 7.0 %collective-permute-start.11 = (f32[96,256]{1,0:T(8,128)S(1)}, f32[96,256]{1,0:T(8,128)S(1)}, u32[]{:S(2)}, u32[]{:S(2)}) collective-permute-start(f32[96,256]{1,0:T(8,128)S(1)} %get-tuple-element.91), channel_id=1, source_target_pairs={{0,6},{2,4},{4,2},{6,0},{1,7},{3,5},{5,3},{7,1},{8,14},{10,12},{12... | collective-permute-start | bytes 294920 | tf_op jit(solution)/shard_map/ppermute | solution.py:32
  36.2 4.4 %collective-permute-start.12 = (bf16[120,256]{1,0:T(8,128)(2,1)S(1)}, bf16[120,256]{1,0:T(8,128)(2,1)S(1)}, u32[]{:S(2)}, u32[]{:S(2)}) collective-permute-start(bf16[120,256]{1,0:T(8,128)(2,1)S(1)} %get-tuple-element.99), channel_id=1, source_target_pairs={{0,8},{8,0},{16,24},{24,16},{1,9},{9,1},{17,25},{25,17},{2,10},{10... | collective-permute-start | bytes 184328 | tf_op jit(solution)/shard_map/ppermute | solution.py:32
  37.7 4.2 %collective-permute-start.13 = (bf16[120,256]{1,0:T(8,128)(2,1)S(1)}, bf16[120,256]{1,0:T(8,128)(2,1)S(1)}, u32[]{:S(2)}, u32[]{:S(2)}) collective-permute-start(bf16[120,256]{1,0:T(8,128)(2,1)S(1)} %get-tuple-element.100), channel_id=1, source_target_pairs={{0,16},{8,24},{16,0},{24,8},{1,17},{9,25},{17,1},{25,9},{2,18},{10... | collective-permute-start | bytes 184328 | tf_op jit(solution)/shard_map/ppermute | solution.py:32
  38.2 5.1 %collective-permute-start.14 = (bf16[120,256]{1,0:T(8,128)(2,1)S(1)}, bf16[120,256]{1,0:T(8,128)(2,1)S(1)}, u32[]{:S(2)}, u32[]{:S(2)}) collective-permute-start(bf16[120,256]{1,0:T(8,128)(2,1)S(1)} %get-tuple-element.101), channel_id=1, source_target_pairs={{0,24},{8,16},{16,8},{24,0},{1,25},{9,17},{17,9},{25,1},{2,26},{10... | collective-permute-start | bytes 184328 | tf_op jit(solution)/shard_map/ppermute | solution.py:32
  43.6 5.6 %collective-permute-start.15 = (f32[96,256]{1,0:T(8,128)S(1)}, f32[96,256]{1,0:T(8,128)S(1)}, u32[]{:S(2)}, u32[]{:S(2)}) collective-permute-start(f32[96,256]{1,0:T(8,128)S(1)} %get-tuple-element.103), channel_id=1, source_target_pairs={{0,2},{2,0},{4,6},{6,4},{1,3},{3,1},{5,7},{7,5},{8,10},{10,8},{12,... | collective-permute-start | bytes 294920 | tf_op jit(solution)/shard_map/ppermute | solution.py:32
  44.9 6.6 %collective-permute-start.16 = (f32[96,256]{1,0:T(8,128)S(1)}, f32[96,256]{1,0:T(8,128)S(1)}, u32[]{:S(2)}, u32[]{:S(2)}) collective-permute-start(f32[96,256]{1,0:T(8,128)S(1)} %get-tuple-element.104), channel_id=1, source_target_pairs={{0,4},{2,6},{4,0},{6,2},{1,5},{3,7},{5,1},{7,3},{8,12},{10,14},{12... | collective-permute-start | bytes 294920 | tf_op jit(solution)/shard_map/ppermute | solution.py:32
  46.9 6.5 %collective-permute-start.17 = (f32[96,256]{1,0:T(8,128)S(1)}, f32[96,256]{1,0:T(8,128)S(1)}, u32[]{:S(2)}, u32[]{:S(2)}) collective-permute-start(f32[96,256]{1,0:T(8,128)S(1)} %get-tuple-element.105), channel_id=1, source_target_pairs={{0,6},{2,4},{4,2},{6,0},{1,7},{3,5},{5,3},{7,1},{8,14},{10,12},{12... | collective-permute-start | bytes 294920 | tf_op jit(solution)/shard_map/ppermute | solution.py:32
  (3 other events, 19.0 us)

commit v6 on v5

--- a/solution.py
+++ b/solution.py
@@ -13,6 +13,7 @@
 F32 = jnp.float32
 BF16 = jnp.bfloat16
 HIGHEST = lax.Precision.HIGHEST
+PAIRS = ((0, 0), (0, 1), (0, 2), (1, 0), (1, 1), (2, 0))
 VMEM = pl.BlockSpec(memory_space=pltpu.VMEM)
 SMEM = pl.BlockSpec(memory_space=pltpu.SMEM)
 
@@ -202,9 +203,9 @@
     return total
 
 
-def split(value):
+def split(value, count):
     out = []
-    for _ in range(3):
+    for _ in range(count):
         out.append(value.astype(BF16).astype(F32))
         value = value - out[-1]
     return out
@@ -275,9 +276,9 @@
     a_next = dot_exact(inverse[...], turning)
     v_next = v[...] + 0.5 * DT * (a[...] + a_next)
     v_half = v_next.astype(BF16)
-    cuts = split(moved)
+    cuts = split(moved, 2)
     for d in range(rows):
-        for k in range(3):
+        for k in range(2):
             held[k * size : (k + 1) * size, :] = cuts[k][d * size : (d + 1) * size, :]
         messages[d][0:slab, :] = v_half
         messages[d][slab:, :] = held[...].astype(BF16)
@@ -292,11 +293,11 @@
     shape = jax.ShapeDtypeStruct(v.shape, F32)
     out = call(
         functools.partial(last_advance_kernel, len(parts), rows),
-        (shape,) * 3 + (jax.ShapeDtypeStruct((slab + 3 * size, reals), BF16),) * rows,
+        (shape,) * 3 + (jax.ShapeDtypeStruct((slab + 2 * size, reals), BF16),) * rows,
         [VMEM] * (len(parts) + 6),
         (*parts, v, a, load, inverse, drifted, late),
         48 * v.size * slab, 40 * v.size,
-        [pltpu.VMEM((3 * size, reals), F32), pltpu.VMEM((2 * slab, reals), F32)],
+        [pltpu.VMEM((2 * size, reals), F32), pltpu.VMEM((2 * slab, reals), F32)],
     )
     return out[0], out[1], out[2], out[3:]
 
@@ -365,7 +366,9 @@
     lane = lax.broadcasted_iota(jnp.int32, (slab, slab), 1) // 6
     module = lax.broadcasted_iota(jnp.int32, (slab, slab), 0) // 6
     inverse = jnp.where(lane == module, jnp.concatenate([block] * modules, axis=1), 0.0)
-    pull[...] = QUARTER * dot_exact(weights[...], inverse)
+    cuts = split(QUARTER * dot_exact(weights[...], inverse), 3)
+    for k, (part, _) in enumerate(PAIRS):
+        pull[:, k * slab : (k + 1) * slab] = cuts[part].astype(BF16)
 
 
 def listed_parts(arrived, take, own_take, weights, slab, lag_rows):
@@ -375,7 +378,7 @@
         functools.partial(listed_kernel, rows, cols, slab, lag_rows),
         (
             jax.ShapeDtypeStruct((cols * slab, lag_rows), BF16),
-            jax.ShapeDtypeStruct(weights.shape, F32),
+            jax.ShapeDtypeStruct((weights.shape[0], len(PAIRS) * slab), BF16),
         ),
         [VMEM] * (rows + 3),
         (*arrived, take, own_take, weights),
@@ -394,9 +397,7 @@
     slab = own_take.shape[0]
     for d in range(rows):
         cuts = arrived[d][slab:, :].astype(F32)
-        held[d * size : (d + 1) * size, :] = (
-            cuts[2 * size : 3 * size, :] + cuts[size : 2 * size, :]
-        ) + cuts[0:size, :]
+        held[d * size : (d + 1) * size, :] = cuts[size : 2 * size, :] + cuts[0:size, :]
     out[...] = dot_exact(weights[...], dot_exact(own_take[...], held[...]))
 
 
@@ -414,14 +415,18 @@
 
 def end_kernel(cols, pieces, *refs):
     parts = refs[:cols]
-    settled, inverse, known, pull, v_out, out, v_done, done, sems = refs[cols:]
+    settled, inverse, known, pull, v_out, out, v_done, done, stack, sems = refs[cols:]
     slab = settled.shape[0]
     lines = known.shape[0] // pieces
-    force = summed(parts, slab, slab)
+    cuts = split(summed(parts, slab, slab), 3)
+    for k, (_, part) in enumerate(PAIRS):
+        stack[k * slab : (k + 1) * slab, :] = cuts[part].astype(BF16)
     copies = []
     for i in range(pieces):
         at = pl.ds(i * lines, lines)
-        done[at, :] = known[at, :] - dot_exact(pull[at, :], force)
+        done[at, :] = known[at, :] - jnp.dot(
+            pull[at, :], stack[...], preferred_element_type=F32
+        )
         copies.append(pltpu.make_async_copy(done.at[at], out.at[at], sems.at[i]))
         copies[-1].start()
         if i == 0:
@@ -445,6 +450,7 @@
         scratch_shapes=[
             pltpu.VMEM(settled.shape, F32),
             pltpu.VMEM(known.shape, F32),
+            pltpu.VMEM((len(PAIRS) * settled.shape[0], settled.shape[1]), BF16),
             pltpu.SemaphoreType.DMA((pieces + 1,)),
         ],
         compiler_params=pltpu.CompilerParams(vmem_limit_bytes=16 << 20),
@@ -515,7 +521,7 @@
     own_take[...] = take[col]
     for k in range(6):
         coef[pl.ds(k, modules, stride=6), :] = blocks[k]
-    cuts = jnp.concatenate(split(dot_exact(send[...], coef[...])), axis=1)
+    cuts = jnp.concatenate(split(dot_exact(send[...], coef[...]), 3), axis=1)
     for d in range(rows):
         held[d, 0:size, lag_rows : lag_rows + 18] = cuts[d * size : (d + 1) * size, :]
         riders[d][...] = held[d].astype(BF16)

time: 54.8 us -> 54.5 us (level)
  no operation moved by 1% of the time
where the time goes in v6:
time: 54.5 us; the launch traced here: 54.4 us
  starting transfers between devices  25.1 us (46%)
  waiting for transfers between devices  17.4 us (32%)
  Pallas kernels  10.7 us (20%)
  between operations  0.93 us (2%)
    ppermute x18, starting transfers between devices, exchange(): lax.ppermute(pieces[d], axis, [(i, sends_to(i, d, n)) for i in range(n)])  25.1 us
    ppermute x18, waiting for transfers between devices, exchange(): lax.ppermute(pieces[d], axis, [(i, sends_to(i, d, n)) for i in range(n)])  17.4 us
    pallas_call x16, Pallas kernels, call(): pl.pallas_call(body, out_shape=shapes, in_specs=in_specs, out_specs=jax.t...  9.66 us
  transfers between devices with their start and end apart: 18, of which 11 were waited for; matrix products, arithmetic and copies ran while one was open for 0% of the time, Pallas kernels for 15%

profile of v6, /device:TPU:0, one launch (start us, length us, event | category | flops | bytes accessed | tf_op | source)
XLA Modules:
  0.0 54.4 jit_solution(13977026393469429380)
XLA Ops:
  0.6 4.0 %collective-permute-start.2 = (f32[48,256]{1,0:T(8,128)}, f32[48,256]{1,0:T(8,128)S(1)}, u32[]{:S(2)}, u32[]{:S(2)}) collective-permute-start(f32[48,256]{1,0:T(8,128)} %refs_5_.1), channel_id=1, source_target_pairs={{0,24},{8,16},{16,8},{24,0},{1,25},{9,17},{17,9},{25,1},{2,26},{10... | collective-permute-start | bytes 147464 | tf_op jit(solution)/shard_map/ppermute | solution.py:33
  5.3 2.5 %shard_map.122 = (bf16[3072,192]{1,0:T(8,128)(2,1)S(1)}, bf16[2880,256]{1,0:T(8,128)(2,1)S(1)}, f32[192,256]{1,0:T(8,128)S(1)}) custom-call(bf16[3072,192]{1,0:T(8,128)(2,1)} %bitcast.19, bf16[2880,256]{1,0:T(8,128)(2,1)} %bitcast.20), custom_call_target="tpu_custom_call" | custom-call | flops 301989888 | bytes 2654208 | tf_op jit(solution)/shard_map/pallas_call | solution.py:59
  7.9 1.1 %collective-permute-done.1.refs_3_ = f32[48,256]{1,0:T(8,128)S(1)} collective-permute-done((f32[48,256]{1,0:T(8,128)}, f32[48,256]{1,0:T(8,128)S(1)}, u32[]{:S(2)}, u32[]{:S(2)}) %collective-permute-start.1) | collective-permute-done | bytes 49184 | tf_op jit(solution)/shard_map/ppermute | solution.py:33
  9.7 1.6 %collective-permute-start.3 = (f32[48,256]{1,0:T(8,128)S(1)}, f32[48,256]{1,0:T(8,128)S(1)}, u32[]{:S(2)}, u32[]{:S(2)}) collective-permute-start(f32[48,256]{1,0:T(8,128)S(1)} %get-tuple-element.60), channel_id=1, source_target_pairs={{0,2},{2,0},{4,6},{6,4},{1,3},{3,1},{5,7},{7,5},{8,10},{10,8},{12,... | collective-permute-start | bytes 147464 | tf_op jit(solution)/shard_map/ppermute | solution.py:33
  11.3 2.6 %collective-permute-start.4 = (f32[48,256]{1,0:T(8,128)S(1)}, f32[48,256]{1,0:T(8,128)S(1)}, u32[]{:S(2)}, u32[]{:S(2)}) collective-permute-start(f32[48,256]{1,0:T(8,128)S(1)} %get-tuple-element.61), channel_id=1, source_target_pairs={{0,4},{2,6},{4,0},{6,2},{1,5},{3,7},{5,1},{7,3},{8,12},{10,14},{12... | collective-permute-start | bytes 147464 | tf_op jit(solution)/shard_map/ppermute | solution.py:33
  14.5 1.4 %shard_map.126 = (bf16[96,256]{1,0:T(8,128)(2,1)S(1)}, bf16[96,256]{1,0:T(8,128)(2,1)S(1)}, bf16[96,256]{1,0:T(8,128)(2,1)S(1)}, bf16[96,256]{1,0:T(8,128)(2,1)S...) custom-call(s32[128]{0:T(128)S(1)} %copy-done.5, ...), custom_call_target="tpu_custom_call" | custom-call | flops 14155776 | bytes 1572864 | tf_op jit(solution)/shard_map/pallas_call | solution.py:59
  15.9 1.4 %collective-permute-done.4.refs_2_ = f32[48,256]{1,0:T(8,128)S(1)} collective-permute-done((f32[48,256]{1,0:T(8,128)S(1)}, f32[48,256]{1,0:T(8,128)S(1)}, u32[]{:S(2)}, u32[]{:S(2)}) %collective-permute-start.4) | collective-permute-done | bytes 49184 | tf_op jit(solution)/shard_map/ppermute | solution.py:33
  17.4 2.4 %collective-permute-done.5.refs_3_ = f32[48,256]{1,0:T(8,128)S(1)} collective-permute-done((f32[48,256]{1,0:T(8,128)S(1)}, f32[48,256]{1,0:T(8,128)S(1)}, u32[]{:S(2)}, u32[]{:S(2)}) %collective-permute-start.5) | collective-permute-done | bytes 49184 | tf_op jit(solution)/shard_map/ppermute | solution.py:33
  20.6 1.5 %collective-permute-start.7 = (bf16[144,256]{1,0:T(8,128)(2,1)S(1)}, bf16[144,256]{1,0:T(8,128)(2,1)S(1)}, u32[]{:S(2)}, u32[]{:S(2)}) collective-permute-start(bf16[144,256]{1,0:T(8,128)(2,1)S(1)} %get-tuple-element.74), channel_id=1, source_target_pairs={{0,16},{8,24},{16,0},{24,8},{1,17},{9,25},{17,1},{25,9},{2,18},{10... | collective-permute-start | bytes 221192 | tf_op jit(solution)/shard_map/ppermute | solution.py:33
  22.1 1.4 %collective-permute-start.8 = (bf16[144,256]{1,0:T(8,128)(2,1)S(1)}, bf16[144,256]{1,0:T(8,128)(2,1)S(1)}, u32[]{:S(2)}, u32[]{:S(2)}) collective-permute-start(bf16[144,256]{1,0:T(8,128)(2,1)S(1)} %get-tuple-element.75), channel_id=1, source_target_pairs={{0,24},{8,16},{16,8},{24,0},{1,25},{9,17},{17,9},{25,1},{2,26},{10... | collective-permute-start | bytes 221192 | tf_op jit(solution)/shard_map/ppermute | solution.py:33
  25.0 2.4 %collective-permute-done.8.refs_3_.refs_4_ = bf16[144,256]{1,0:T(8,128)(2,1)S(1)} collective-permute-done((bf16[144,256]{1,0:T(8,128)(2,1)S(1)}, bf16[144,256]{1,0:T(8,128)(2,1)S(1)}, u32[]{:S(2)}, u32[]{:S(2)}) %collective-permute-start.8) | collective-permute-done | bytes 73760 | tf_op jit(solution)/shard_map/ppermute | solution.py:33
  27.7 1.1 %collective-permute-start.10 = (f32[96,256]{1,0:T(8,128)S(1)}, f32[96,256]{1,0:T(8,128)S(1)}, u32[]{:S(2)}, u32[]{:S(2)}) collective-permute-start(f32[96,256]{1,0:T(8,128)S(1)} %get-tuple-element.90), channel_id=1, source_target_pairs={{0,4},{2,6},{4,0},{6,2},{1,5},{3,7},{5,1},{7,3},{8,12},{10,14},{12... | collective-permute-start | bytes 294920 | tf_op jit(solution)/shard_map/ppermute | solution.py:33
  28.9 3.2 %collective-permute-start.11 = (f32[96,256]{1,0:T(8,128)S(1)}, f32[96,256]{1,0:T(8,128)S(1)}, u32[]{:S(2)}, u32[]{:S(2)}) collective-permute-start(f32[96,256]{1,0:T(8,128)S(1)} %get-tuple-element.91), channel_id=1, source_target_pairs={{0,6},{2,4},{4,2},{6,0},{1,7},{3,5},{5,3},{7,1},{8,14},{10,12},{12... | collective-permute-start | bytes 294920 | tf_op jit(solution)/shard_map/ppermute | solution.py:33
  33.4 2.5 %collective-permute-done.11.refs_3_ = f32[96,256]{1,0:T(8,128)S(1)} collective-permute-done((f32[96,256]{1,0:T(8,128)S(1)}, f32[96,256]{1,0:T(8,128)S(1)}, u32[]{:S(2)}, u32[]{:S(2)}) %collective-permute-start.11) | collective-permute-done | bytes 98336 | tf_op jit(solution)/shard_map/ppermute | solution.py:33
  36.2 1.6 %collective-permute-start.12 = (bf16[96,256]{1,0:T(8,128)(2,1)S(1)}, bf16[96,256]{1,0:T(8,128)(2,1)S(1)}, u32[]{:S(2)}, u32[]{:S(2)}) collective-permute-start(bf16[96,256]{1,0:T(8,128)(2,1)S(1)} %get-tuple-element.99), channel_id=1, source_target_pairs={{0,8},{8,0},{16,24},{24,16},{1,9},{9,1},{17,25},{25,17},{2,10},{10... | collective-permute-start | bytes 147464 | tf_op jit(solution)/shard_map/ppermute | solution.py:33
  38.2 1.5 %collective-permute-start.14 = (bf16[96,256]{1,0:T(8,128)(2,1)S(1)}, bf16[96,256]{1,0:T(8,128)(2,1)S(1)}, u32[]{:S(2)}, u32[]{:S(2)}) collective-permute-start(bf16[96,256]{1,0:T(8,128)(2,1)S(1)} %get-tuple-element.101), channel_id=1, source_target_pairs={{0,24},{8,16},{16,8},{24,0},{1,25},{9,17},{17,9},{25,1},{2,26},{10... | collective-permute-start | bytes 147464 | tf_op jit(solution)/shard_map/ppermute | solution.py:33
  39.7 1.1 %shard_map.129 = (bf16[192,192]{1,0:T(8,128)(2,1)S(1)}, bf16[384,288]{1,0:T(8,128)(2,1)S(1)}) custom-call(bf16[144,256]{1,0:T(8,128)(2,1)S(1)} %get-tuple-element.72.refs_0_.refs_1_, bf16[144,256]{1,0:T(8,128)(2,1)S(1)} %collective-permute-done.6.refs_1_.refs_2_, bf16[144,256]{1,0:T(8,128)(2,1)S(1)} %collective-permute-done.7.refs_2_.refs_3_, ...), custom_call_target="tpu_custom_call" | custom-call | flops 14155776 | bytes 73728 | tf_op jit(solution)/shard_map/pallas_call | solution.py:59
  41.8 1.4 %collective-permute-done.14.refs_5_.refs_3_ = bf16[96,256]{1,0:T(8,128)(2,1)S(1)} collective-permute-done((bf16[96,256]{1,0:T(8,128)(2,1)S(1)}, bf16[96,256]{1,0:T(8,128)(2,1)S(1)}, u32[]{:S(2)}, u32[]{:S(2)}) %collective-permute-start.14) | collective-permute-done | bytes 49184 | tf_op jit(solution)/shard_map/ppermute | solution.py:33
  43.5 1.3 %collective-permute-start.15 = (f32[96,256]{1,0:T(8,128)S(1)}, f32[96,256]{1,0:T(8,128)S(1)}, u32[]{:S(2)}, u32[]{:S(2)}) collective-permute-start(f32[96,256]{1,0:T(8,128)S(1)} %get-tuple-element.103), channel_id=1, source_target_pairs={{0,2},{2,0},{4,6},{6,4},{1,3},{3,1},{5,7},{7,5},{8,10},{10,8},{12,... | collective-permute-start | bytes 294920 | tf_op jit(solution)/shard_map/ppermute | solution.py:33
  44.8 2.0 %collective-permute-start.16 = (f32[96,256]{1,0:T(8,128)S(1)}, f32[96,256]{1,0:T(8,128)S(1)}, u32[]{:S(2)}, u32[]{:S(2)}) collective-permute-start(f32[96,256]{1,0:T(8,128)S(1)} %get-tuple-element.104), channel_id=1, source_target_pairs={{0,4},{2,6},{4,0},{6,2},{1,5},{3,7},{5,1},{7,3},{8,12},{10,14},{12... | collective-permute-start | bytes 294920 | tf_op jit(solution)/shard_map/ppermute | solution.py:33
  46.8 1.1 %collective-permute-start.17 = (f32[96,256]{1,0:T(8,128)S(1)}, f32[96,256]{1,0:T(8,128)S(1)}, u32[]{:S(2)}, u32[]{:S(2)}) collective-permute-start(f32[96,256]{1,0:T(8,128)S(1)} %get-tuple-element.105), channel_id=1, source_target_pairs={{0,6},{2,4},{4,2},{6,0},{1,7},{3,5},{5,3},{7,1},{8,14},{10,12},{12... | collective-permute-start | bytes 294920 | tf_op jit(solution)/shard_map/ppermute | solution.py:33
  49.1 2.3 %collective-permute-done.16.refs_2_ = f32[96,256]{1,0:T(8,128)S(1)} collective-permute-done((f32[96,256]{1,0:T(8,128)S(1)}, f32[96,256]{1,0:T(8,128)S(1)}, u32[]{:S(2)}, u32[]{:S(2)}) %collective-permute-start.16) | collective-permute-done | bytes 98336 | tf_op jit(solution)/shard_map/ppermute | solution.py:33
  51.3 2.0 %collective-permute-done.17.refs_3_ = f32[96,256]{1,0:T(8,128)S(1)} collective-permute-done((f32[96,256]{1,0:T(8,128)S(1)}, f32[96,256]{1,0:T(8,128)S(1)}, u32[]{:S(2)}, u32[]{:S(2)}) %collective-permute-start.17) | collective-permute-done | bytes 98336 | tf_op jit(solution)/shard_map/ppermute | solution.py:33
  53.3 1.0 %shard_map.138 = (f32[48,256]{1,0:T(8,128)}, f32[384,256]{1,0:T(8,128)}) custom-call(f32[96,256]{1,0:T(8,128)S(1)} %get-tuple-element.102.refs_0_, f32[96,256]{1,0:T(8,128)S(1)} %collective-permute-done.15.refs_1_, f32[96,256]{1,0:T(8,128)S(1)} %collective-permute-done.16.refs_2_, f32[96,256]{1,0:T(8,128)S(1)} %collective-permute-done.17.refs_3_, ...), custom_call_target="tpu_custom_call" | custom-call | flops 339738624 | bytes 786432 | tf_op jit(solution)/shard_map/pallas_call | solution.py:445
  (50 shorter events, 8.9 us)
Async XLA Ops:
  0.6 8.8 %copy-start = (f32[48,256]{1,0:T(8,128)S(1)}, f32[48,256]{1,0:T(8,128)}, u32[]{:S(2)}) copy-start(f32[48,256]{1,0:T(8,128)} %refs_5_.1) | copy-start | bytes 147460
  0.6 7.2 %collective-permute-start.2 = (f32[48,256]{1,0:T(8,128)}, f32[48,256]{1,0:T(8,128)S(1)}, u32[]{:S(2)}, u32[]{:S(2)}) collective-permute-start(f32[48,256]{1,0:T(8,128)} %refs_5_.1), channel_id=1, source_target_pairs={{0,24},{8,16},{16,8},{24,0},{1,25},{9,17},{17,9},{25,1},{2,26},{10... | collective-permute-start | bytes 147464 | tf_op jit(solution)/shard_map/ppermute | solution.py:33
  4.6 4.3 %collective-permute-start.1 = (f32[48,256]{1,0:T(8,128)}, f32[48,256]{1,0:T(8,128)S(1)}, u32[]{:S(2)}, u32[]{:S(2)}) collective-permute-start(f32[48,256]{1,0:T(8,128)} %refs_5_.1), channel_id=1, source_target_pairs={{0,16},{8,24},{16,0},{24,8},{1,17},{9,25},{17,1},{25,9},{2,18},{10... | collective-permute-start | bytes 147464 | tf_op jit(solution)/shard_map/ppermute | solution.py:33
  5.1 4.3 %collective-permute-start = (f32[48,256]{1,0:T(8,128)}, f32[48,256]{1,0:T(8,128)S(1)}, u32[]{:S(2)}, u32[]{:S(2)}) collective-permute-start(f32[48,256]{1,0:T(8,128)} %refs_5_.1), channel_id=1, source_target_pairs={{0,8},{8,0},{16,24},{24,16},{1,9},{9,1},{17,25},{25,17},{2,10},{10... | collective-permute-start | bytes 147464 | tf_op jit(solution)/shard_map/ppermute | solution.py:33
  7.8 6.5 %copy-start.1 = (f32[48,256]{1,0:T(8,128)S(1)}, f32[48,256]{1,0:T(8,128)}, u32[]{:S(2)}) copy-start(f32[48,256]{1,0:T(8,128)} %refs_6_.1) | copy-start | bytes 147460
  7.8 6.5 %copy-start.3 = (f32[48,256]{1,0:T(8,128)S(1)}, f32[48,256]{1,0:T(8,128)}, u32[]{:S(2)}) copy-start(f32[48,256]{1,0:T(8,128)} %x.1) | copy-start | bytes 147460
  7.9 6.7 %copy-start.5 = (s32[128]{0:T(128)S(1)}, s32[128]{0:T(128)}, u32[]{:S(2)}) copy-start(s32[128]{0:T(128)} %refs_0_) | copy-start | bytes 1540
  9.7 6.2 %collective-permute-start.3 = (f32[48,256]{1,0:T(8,128)S(1)}, f32[48,256]{1,0:T(8,128)S(1)}, u32[]{:S(2)}, u32[]{:S(2)}) collective-permute-start(f32[48,256]{1,0:T(8,128)S(1)} %get-tuple-element.60), channel_id=1, source_target_pairs={{0,2},{2,0},{4,6},{6,4},{1,3},{3,1},{5,7},{7,5},{8,10},{10,8},{12,... | collective-permute-start | bytes 147464 | tf_op jit(solution)/shard_map/ppermute | solution.py:33
  11.3 6.0 %collective-permute-start.4 = (f32[48,256]{1,0:T(8,128)S(1)}, f32[48,256]{1,0:T(8,128)S(1)}, u32[]{:S(2)}, u32[]{:S(2)}) collective-permute-start(f32[48,256]{1,0:T(8,128)S(1)} %get-tuple-element.61), channel_id=1, source_target_pairs={{0,4},{2,6},{4,0},{6,2},{1,5},{3,7},{5,1},{7,3},{8,12},{10,14},{12... | collective-permute-start | bytes 147464 | tf_op jit(solution)/shard_map/ppermute | solution.py:33
  13.9 5.9 %collective-permute-start.5 = (f32[48,256]{1,0:T(8,128)S(1)}, f32[48,256]{1,0:T(8,128)S(1)}, u32[]{:S(2)}, u32[]{:S(2)}) collective-permute-start(f32[48,256]{1,0:T(8,128)S(1)} %get-tuple-element.62), channel_id=1, source_target_pairs={{0,6},{2,4},{4,2},{6,0},{1,7},{3,5},{5,3},{7,1},{8,14},{10,12},{12... | collective-permute-start | bytes 147464 | tf_op jit(solution)/shard_map/ppermute | solution.py:33
  20.0 4.6 %collective-permute-start.6 = (bf16[144,256]{1,0:T(8,128)(2,1)S(1)}, bf16[144,256]{1,0:T(8,128)(2,1)S(1)}, u32[]{:S(2)}, u32[]{:S(2)}) collective-permute-start(bf16[144,256]{1,0:T(8,128)(2,1)S(1)} %get-tuple-element.73), channel_id=1, source_target_pairs={{0,8},{8,0},{16,24},{24,16},{1,9},{9,1},{17,25},{25,17},{2,10},{10... | collective-permute-start | bytes 221192 | tf_op jit(solution)/shard_map/ppermute | solution.py:33
  20.6 4.4 %collective-permute-start.7 = (bf16[144,256]{1,0:T(8,128)(2,1)S(1)}, bf16[144,256]{1,0:T(8,128)(2,1)S(1)}, u32[]{:S(2)}, u32[]{:S(2)}) collective-permute-start(bf16[144,256]{1,0:T(8,128)(2,1)S(1)} %get-tuple-element.74), channel_id=1, source_target_pairs={{0,16},{8,24},{16,0},{24,8},{1,17},{9,25},{17,1},{25,9},{2,18},{10... | collective-permute-start | bytes 221192 | tf_op jit(solution)/shard_map/ppermute | solution.py:33
  22.1 5.3 %collective-permute-start.8 = (bf16[144,256]{1,0:T(8,128)(2,1)S(1)}, bf16[144,256]{1,0:T(8,128)(2,1)S(1)}, u32[]{:S(2)}, u32[]{:S(2)}) collective-permute-start(bf16[144,256]{1,0:T(8,128)(2,1)S(1)} %get-tuple-element.75), channel_id=1, source_target_pairs={{0,24},{8,16},{16,8},{24,0},{1,25},{9,17},{17,9},{25,1},{2,26},{10... | collective-permute-start | bytes 221192 | tf_op jit(solution)/shard_map/ppermute | solution.py:33
  24.6 7.5 %copy-start.7 = (f32[8,3,16]{2,0,1:T(8,128)S(1)}, f32[8,3,16]{2,0,1:T(8,128)}, u32[]{:S(2)}) copy-start(f32[8,3,16]{2,0,1:T(8,128)} %param.21) | copy-start | bytes 4612
  24.6 7.6 %copy-start.8 = (s32[8,16]{1,0:T(8,128)S(1)}, s32[8,16]{1,0:T(8,128)}, u32[]{:S(2)}) copy-start(s32[8,16]{1,0:T(8,128)} %param.20) | copy-start | bytes 1540
  27.7 5.7 %collective-permute-start.9 = (f32[96,256]{1,0:T(8,128)S(1)}, f32[96,256]{1,0:T(8,128)S(1)}, u32[]{:S(2)}, u32[]{:S(2)}) collective-permute-start(f32[96,256]{1,0:T(8,128)S(1)} %get-tuple-element.89), channel_id=1, source_target_pairs={{0,2},{2,0},{4,6},{6,4},{1,3},{3,1},{5,7},{7,5},{8,10},{10,8},{12,... | collective-permute-start | bytes 294920 | tf_op jit(solution)/shard_map/ppermute | solution.py:33
  27.7 5.7 %collective-permute-start.10 = (f32[96,256]{1,0:T(8,128)S(1)}, f32[96,256]{1,0:T(8,128)S(1)}, u32[]{:S(2)}, u32[]{:S(2)}) collective-permute-start(f32[96,256]{1,0:T(8,128)S(1)} %get-tuple-element.90), channel_id=1, source_target_pairs={{0,4},{2,6},{4,0},{6,2},{1,5},{3,7},{5,1},{7,3},{8,12},{10,14},{12... | collective-permute-start | bytes 294920 | tf_op jit(solution)/shard_map/ppermute | solution.py:33
  28.9 7.0 %collective-permute-start.11 = (f32[96,256]{1,0:T(8,128)S(1)}, f32[96,256]{1,0:T(8,128)S(1)}, u32[]{:S(2)}, u32[]{:S(2)}) collective-permute-start(f32[96,256]{1,0:T(8,128)S(1)} %get-tuple-element.91), channel_id=1, source_target_pairs={{0,6},{2,4},{4,2},{6,0},{1,7},{3,5},{5,3},{7,1},{8,14},{10,12},{12... | collective-permute-start | bytes 294920 | tf_op jit(solution)/shard_map/ppermute | solution.py:33
  36.2 4.6 %collective-permute-start.12 = (bf16[96,256]{1,0:T(8,128)(2,1)S(1)}, bf16[96,256]{1,0:T(8,128)(2,1)S(1)}, u32[]{:S(2)}, u32[]{:S(2)}) collective-permute-start(bf16[96,256]{1,0:T(8,128)(2,1)S(1)} %get-tuple-element.99), channel_id=1, source_target_pairs={{0,8},{8,0},{16,24},{24,16},{1,9},{9,1},{17,25},{25,17},{2,10},{10... | collective-permute-start | bytes 147464 | tf_op jit(solution)/shard_map/ppermute | solution.py:33
  37.7 4.1 %collective-permute-start.13 = (bf16[96,256]{1,0:T(8,128)(2,1)S(1)}, bf16[96,256]{1,0:T(8,128)(2,1)S(1)}, u32[]{:S(2)}, u32[]{:S(2)}) collective-permute-start(bf16[96,256]{1,0:T(8,128)(2,1)S(1)} %get-tuple-element.100), channel_id=1, source_target_pairs={{0,16},{8,24},{16,0},{24,8},{1,17},{9,25},{17,1},{25,9},{2,18},{10... | collective-permute-start | bytes 147464 | tf_op jit(solution)/shard_map/ppermute | solution.py:33
  38.2 5.0 %collective-permute-start.14 = (bf16[96,256]{1,0:T(8,128)(2,1)S(1)}, bf16[96,256]{1,0:T(8,128)(2,1)S(1)}, u32[]{:S(2)}, u32[]{:S(2)}) collective-permute-start(bf16[96,256]{1,0:T(8,128)(2,1)S(1)} %get-tuple-element.101), channel_id=1, source_target_pairs={{0,24},{8,16},{16,8},{24,0},{1,25},{9,17},{17,9},{25,1},{2,26},{10... | collective-permute-start | bytes 147464 | tf_op jit(solution)/shard_map/ppermute | solution.py:33
  43.5 5.6 %collective-permute-start.15 = (f32[96,256]{1,0:T(8,128)S(1)}, f32[96,256]{1,0:T(8,128)S(1)}, u32[]{:S(2)}, u32[]{:S(2)}) collective-permute-start(f32[96,256]{1,0:T(8,128)S(1)} %get-tuple-element.103), channel_id=1, source_target_pairs={{0,2},{2,0},{4,6},{6,4},{1,3},{3,1},{5,7},{7,5},{8,10},{10,8},{12,... | collective-permute-start | bytes 294920 | tf_op jit(solution)/shard_map/ppermute | solution.py:33
  44.8 6.6 %collective-permute-start.16 = (f32[96,256]{1,0:T(8,128)S(1)}, f32[96,256]{1,0:T(8,128)S(1)}, u32[]{:S(2)}, u32[]{:S(2)}) collective-permute-start(f32[96,256]{1,0:T(8,128)S(1)} %get-tuple-element.104), channel_id=1, source_target_pairs={{0,4},{2,6},{4,0},{6,2},{1,5},{3,7},{5,1},{7,3},{8,12},{10,14},{12... | collective-permute-start | bytes 294920 | tf_op jit(solution)/shard_map/ppermute | solution.py:33
  46.8 6.5 %collective-permute-start.17 = (f32[96,256]{1,0:T(8,128)S(1)}, f32[96,256]{1,0:T(8,128)S(1)}, u32[]{:S(2)}, u32[]{:S(2)}) collective-permute-start(f32[96,256]{1,0:T(8,128)S(1)} %get-tuple-element.105), channel_id=1, source_target_pairs={{0,6},{2,4},{4,2},{6,0},{1,7},{3,5},{5,3},{7,1},{8,14},{10,12},{12... | collective-permute-start | bytes 294920 | tf_op jit(solution)/shard_map/ppermute | solution.py:33
  (3 other events, 19.0 us)
